TPU v7x, 256 devices: a whole 4x4x8 slice. The times are simulated.
256 devices in a mesh: site: 4 (over x), fsdp: 64 (over z, y, core).
Axes of the slice: x: 4, y: 4, z: 8, core: 2. Of those that a mesh axis runs over, the one named last changes fastest.
Arguments:
- held_input: bfloat16 [4, 32768, 1536], P('site', 'fsdp'), may hold values from -16 to 16
- held_cotangent: bfloat16 [4, 32768, 1536], P('site', 'fsdp'), may hold values from -6 to 6
- proj_weight: bfloat16 [1536, 1536], P('fsdp'), may hold values from -0.15625 to 0.15625
- stem_weight: bfloat16 [3, 512, 1536], P(None, 'fsdp'), may hold values from -0.15625 to 0.15625
- seg_counts: int32 [4, 64], P('site'), may hold values from 1 to 128, 4096 in all within a row
Outputs:
- stem_grad: bfloat16 [4, 131072, 512], P('site', 'fsdp')
- weight_grad: float32 [1536, 1536], P('fsdp')
Inputs may be any that keep to these rules, and one draw needn't show every extreme that they name: `seg_counts`: in every group the 64 counts sum to 4096, so that every holder slot is used; one owner has exactly 128, and a holder keeps at most 2 segments of one owner, a bound reached in every draw.
All inputs are finite; a program needn't handle non-finite values.
Results may differ from a plain program's by a relative error of at most 0.0049.
Values may be sent and summed in bfloat16 or wider, within the bound.
A program may use at most 128 MiB of HBM per device.

v0:
```python
import math

import jax
import jax.numpy as jnp
from jax import lax
from jax.sharding import PartitionSpec as P

D = 1536
SEG = 8
HOLD = 64
OWN_SEG = 128


EPSILON = 1e-05


def stem_taps(frames, stem_weight):
    return jnp.einsum(
        "rd,kcd->krc",
        frames,
        lax.all_gather(stem_weight, "fsdp", axis=1, tiled=True),
        preferred_element_type=jnp.float32,
    )


def body(held_input, held_cotangent, proj_weight, stem_weight, seg_counts):
    group_size = lax.axis_size("fsdp")
    capacity = 2 * ((OWN_SEG + 2 * group_size - 1) // (2 * group_size))
    my_index = lax.axis_index("fsdp")
    inputs = held_input[0].astype(jnp.float32)
    cotangent = held_cotangent[0]
    row_mean = jnp.mean(inputs, axis=-1, keepdims=True)
    centered = inputs - row_mean
    variance = jnp.mean(centered * centered, axis=-1, keepdims=True)
    inverse = lax.rsqrt(variance + EPSILON)
    normed = centered * inverse
    normed_bf = normed.astype(jnp.bfloat16)
    proj_back = lax.dot_general(
        cotangent,
        lax.all_gather(proj_weight, "fsdp", axis=0, tiled=True),
        (((1,), (1,)), ((), ())),
        preferred_element_type=jnp.float32,
    )
    input_grad = cotangent.astype(jnp.float32) + inverse * (
        proj_back
        - jnp.mean(proj_back, axis=-1, keepdims=True)
        - normed * jnp.mean(proj_back * normed, axis=-1, keepdims=True)
    )
    input_grad = input_grad.astype(jnp.bfloat16)
    counts = seg_counts[0]
    endings = jnp.cumsum(counts)
    starts = endings - counts
    slot_ids = jnp.arange(HOLD, dtype=jnp.int32)
    item_index = 2 * (slot_ids // 2 * group_size + my_index) + slot_ids % 2
    owner_ids = jnp.sum((item_index[:, None] >= endings[None, :]).astype(jnp.int32), axis=1)
    earlier = (slot_ids[None, :] < slot_ids[:, None]) & (owner_ids[None, :] == owner_ids[:, None])
    rank_ids = jnp.sum(earlier.astype(jnp.int32), axis=1)
    target = owner_ids * capacity + rank_ids
    positions = jnp.arange(group_size * capacity, dtype=jnp.int32)
    matched = target[None, :] == positions[:, None]
    filled = jnp.any(matched, axis=1)
    source = jnp.sum(jnp.where(matched, slot_ids[None, :], 0), axis=1)
    owner_hit = jnp.arange(group_size, dtype=jnp.int32) == my_index
    my_count = jnp.sum(jnp.where(owner_hit, counts, 0))
    my_start = jnp.sum(jnp.where(owner_hit, starts, 0))
    segment = jnp.arange(OWN_SEG, dtype=jnp.int32)
    is_live = segment < my_count
    holder = (my_start + segment) // 2 % group_size
    before = (
        (segment[None, :] < segment[:, None])
        & (holder[None, :] == holder[:, None])
        & is_live[None, :]
    )
    holder_rank = jnp.sum(before.astype(jnp.int32), axis=1)
    row_index = jnp.where(is_live, holder * capacity + holder_rank, 0)
    held_segments = input_grad.reshape(HOLD, SEG, D)
    zero_bf = jnp.zeros((), jnp.bfloat16)
    send_rows = jnp.where(filled[:, None, None], jnp.take(held_segments, source, axis=0), zero_bf)
    received = lax.all_to_all(
        send_rows.reshape(group_size, capacity, SEG, D),
        "fsdp",
        split_axis=0,
        concat_axis=0,
        tiled=True,
    )
    picked = jnp.take(received.reshape(group_size * capacity, SEG, D), row_index, axis=0)
    frames = jnp.where(is_live[:, None, None], picked, zero_bf).reshape(OWN_SEG * SEG, D)
    tap_terms = stem_taps(frames, stem_weight)
    shifted = jnp.concatenate(
        [tap_terms[0][1:], jnp.zeros((1, tap_terms.shape[2]), jnp.float32)], 0
    )
    odd_rows = tap_terms[2] + shifted
    stem_rows = (
        jnp.stack([tap_terms[1], odd_rows], 1)
        .reshape(2 * OWN_SEG * SEG, tap_terms.shape[2])
        .astype(jnp.bfloat16)
    )
    shard_sum = lax.psum_scatter(
        lax.dot_general(
            normed_bf, cotangent, (((0,), (0,)), ((), ())), preferred_element_type=jnp.float32
        ),
        "fsdp",
        scatter_dimension=0,
        tiled=True,
    )
    shard_sum = lax.psum(shard_sum, "site")
    weight_grad = shard_sum / math.sqrt(lax.axis_size("site") * group_size * HOLD * SEG)
    return (stem_rows[None], weight_grad)


def solution(mesh):
    placed = (
        P("site", "fsdp", None),
        P("site", "fsdp", None),
        P("fsdp", None),
        P(None, "fsdp", None),
        P("site", None),
    )
    return jax.shard_map(
        body,
        mesh=mesh,
        in_specs=placed,
        out_specs=(P("site", "fsdp", None), P("fsdp", None)),
        check_vma=False,
    )
```

profile of v0, /device:TPU:24, one launch (start us, length us, event | category | flops | bytes accessed | tf_op | source)
XLA Modules:
  0.0 405.4 jit_solution(15506953780961973677)
XLA Ops:
  7.2 0.0 copy-start
  7.2 0.0 copy-start.1
  7.2 0.0 reduce-scatter.4.cloned.1.call-start
  7.2 1.8 convert_reduce_fusion
  9.1 2.0 fusion.10
  11.0 0.0 copy-done
  11.1 0.0 copy-done.1
  11.1 5.3 %fusion.25 = f32[1536,1536]{1,0:T(8,128)} fusion(bf16[1,512,1536]{2,1,0:T(8,128)(2,1)S(1)} %copy-done, bf16[1,512,1536]{2,1,0:T(8,128)(2,1)S(1)} %copy-done.1, f32[512]{0:T(512)S(1)} %add_rsqrt_fusion, f32[512]{0:T(512)S(1)} %broadcast_multiply_fusion.3), kind=kOutput, calls=%fused_computation.33 | convolution fusion | flops 2419064832 | bytes 12587008 | tf_op jit(solution)/shard_map/dot_general | solution.py:99
  16.4 0.0 copy-start.3
  16.4 0.0 reduce-scatter.4.cloned.1.call-update
  16.4 0.0 all-gather.3.cloned.1.call-start
  16.5 0.7 all-gather.3.cloned.1.call-update
  17.2 0.0 all-reduce.4.cloned.1.call-start
  17.2 155.4 %reduce-scatter.4.cloned.1.call-done = f32[24,1536]{1,0:T(8,128)} async-done(((f32[1536,1536]{1,0:T(8,128)}), f32[24,1536]{1,0:T(8,128)}) %reduce-scatter.4.cloned.1.call-update) | async-done | bytes 147472
  172.6 0.0 all-reduce.4.cloned.1.call-update
  172.6 0.0 all-gather.5.cloned.1.call-start
  172.7 0.5 all-gather.5.cloned.1.call-update
  173.2 0.0 copy-done.3
  173.2 0.1 copy.12
  173.3 0.1 reduce-window.8
  173.4 0.1 reduce.1
  173.5 0.6 fusion.45
  174.2 0.2 convert_reduce_fusion.3
  174.4 0.2 convert_reduce_fusion.2
  174.6 0.1 fusion.39
  174.7 0.2 broadcast_in_dim.98
  174.8 0.1 select_reduce_fusion
  174.9 0.1 reduce_sum.102
  175.1 77.5 %all-gather.3.cloned.1.call-done = bf16[1536,1536]{1,0:T(8,128)(2,1)} async-done(((bf16[24,1536]{1,0:T(8,128)(2,1)}), bf16[1536,1536]{1,0:T(8,128)(2,1)}) %all-gather.3.cloned.1.call-update) | async-done | bytes 4718608 | tf_op jit(solution)/shard_map/all_gather | solution.py:40
  252.6 0.0 copy-start.2
  252.6 4.9 %fusion.55 = (f32[512]{0:T(512)S(1)}, f32[512]{0:T(512)S(1)}, f32[512,1536]{1,0:T(8,128)S(1)}) fusion(f32[512]{0:T(512)S(1)} %add_rsqrt_fusion, f32[512]{0:T(512)S(1)} %broadcast_multiply_fusion.3, bf16[1,512,1536]{2,1,0:T(8,128)(2,1)S(1)} %copy-done, bf16[1536,1536]{1,0:T(8,128)(2,1)} %all-gather.3.cloned.1.call-done, bf16[1,512,1536]{2,1,0:T(8,128)(2,1)S(1)} %copy-done.1), kind=kOutput, calls=%fused_computation.107 | convolution fusion | flops 2420636672 | bytes 11018240 | tf_op jit(solution)/shard_map/dot_general | solution.py:38
  257.5 0.0 copy-done.2
  257.5 1.2 fusion.27
  258.7 2.5 gather_fusion
  261.1 3.3 select_select_fusion
  264.5 7.8 %all-to-all-start = ((bf16[64,2,8,1536]{3,2,1,0:T(8,128)(2,1)}), bf16[64,2,8,1536]{3,2,1,0:T(8,128)(2,1)S(1)}, u32[]{:S(2)}, u32[]{:S(2)}) async-start(bf16[64,2,8,1536]{3,2,1,0:T(8,128)(2,1)} %select_select_fusion), calls=%async_computation | async-start | bytes 6291456 | tf_op jit(solution)/shard_map/all_to_all | solution.py:79
  272.3 0.7 iota_compare_fusion.3
  273.0 0.7 and_select_fusion.4
  273.7 0.2 convert_reduce_fusion.1
  273.8 1.3 compare_and_fusion.1
  275.2 0.1 broadcast_in_dim.95
  275.2 0.1 broadcast_in_dim.96
  275.4 0.1 broadcast_in_dim.92
  275.4 0.1 broadcast_in_dim.93
  275.5 1.3 fusion.52
  276.9 22.9 %all-reduce.4.cloned.1.call-done = f32[24,1536]{1,0:T(8,128)} async-done(((f32[24,1536]{1,0:T(8,128)}), f32[24,1536]{1,0:T(8,128)}) %all-reduce.4.cloned.1.call-update) | async-done | bytes 147472 | tf_op jit(solution)/shard_map/psum | solution.py:106
  299.8 1.6 broadcast_multiply_fusion
  301.4 47.4 %all-to-all-done = bf16[64,2,8,1536]{3,2,1,0:T(8,128)(2,1)S(1)} async-done(((bf16[64,2,8,1536]{3,2,1,0:T(8,128)(2,1)}), bf16[64,2,8,1536]{3,2,1,0:T(8,128)(2,1)S(1)}, u32[]{:S(2)}, u32[]{:S(2)}) %all-to-all-start) | async-done | bytes 3145760 | tf_op jit(solution)/shard_map/all_to_all | solution.py:79
  348.8 2.4 gather_fusion.1
  351.3 33.7 %all-gather.5.cloned.1.call-done = bf16[3,512,1536]{2,1,0:T(8,128)(2,1)} async-done(((bf16[3,8,1536]{2,1,0:T(8,128)(2,1)}), bf16[3,512,1536]{2,1,0:T(8,128)(2,1)}) %all-gather.5.cloned.1.call-update) | async-done | bytes 4718608 | tf_op jit(solution)/shard_map/all_gather | solution.py:21
  384.9 8.4 %fusion.19 = f32[3,1024,512]{2,1,0:T(8,128)S(1)} fusion(bf16[3,512,1536]{2,1,0:T(8,128)(2,1)} %all-gather.5.cloned.1.call-done, bf16[128,8,1536]{2,1,0:T(8,128)(2,1)} %gather_fusion.1, pred[1024]{0:T(1024)(128)(4,1)S(1)} %broadcast_in_dim.96, pred[1024]{0:T(1024)(128)(4,1)S(1)} %broadcast_in_dim.93), kind=kOutput, calls=%fused_computation.25 | convolution fusion | flops 4834983936 | bytes 14157824 | tf_op jit(solution)/shard_map/rd,kcd->krc/dot_general | solution.py:18
  393.3 0.1 fusion.35
  393.4 0.2 slice_bitcast_fusion
  393.7 0.6 fusion.36
  394.3 0.2 pad_maximum_fusion
  394.5 2.2 copy.13
  396.6 2.2 convert_element_type.46
  (8 shorter events, 0.1 us)
Async XLA Ops:
  7.2 3.9 copy-start
  7.2 3.9 copy-start.1
  7.2 165.4 %reduce-scatter.4.cloned.1.call-start = ((), (), s32[]{:S(2)}) async-start(), calls=%async_computation.5 | async-start | bytes 9584640
  16.4 156.8 %copy-start.3 = (s32[1,64]{1,0:T(1,128)S(1)}, s32[1,64]{1,0:T(1,128)}, u32[]{:S(2)}) copy-start(s32[1,64]{1,0:T(1,128)} %param.9) | copy-start | bytes 772
  16.4 236.2 %all-gather.3.cloned.1.call-start = ((), (), s32[]{:S(2)}) async-start(), calls=%async_computation.2 | async-start | bytes 4792320 | tf_op jit(solution)/shard_map/all_gather | solution.py:40
  17.2 282.7 %all-reduce.4.cloned.1.call-start = ((), (), s32[]{:S(2)}) async-start(), calls=%async_computation.4 | async-start | bytes 294912 | tf_op jit(solution)/shard_map/psum | solution.py:106
  172.6 212.3 %all-gather.5.cloned.1.call-start = ((), (), s32[]{:S(2)}) async-start(), calls=%async_computation.3 | async-start | bytes 4792320 | tf_op jit(solution)/shard_map/all_gather | solution.py:21
  252.6 4.9 %copy-start.2 = (bf16[1,512,1536]{2,1,0:T(8,128)(2,1)S(1)}, bf16[1,512,1536]{2,1,0:T(8,128)(2,1)}, u32[]{:S(2)}) copy-start(bf16[1,512,1536]{2,1,0:T(8,128)(2,1)} %param.6) | copy-start | bytes 4718596
  264.5 84.4 %all-to-all-start = ((bf16[64,2,8,1536]{3,2,1,0:T(8,128)(2,1)}), bf16[64,2,8,1536]{3,2,1,0:T(8,128)(2,1)S(1)}, u32[]{:S(2)}, u32[]{:S(2)}) async-start(bf16[64,2,8,1536]{3,2,1,0:T(8,128)(2,1)} %select_select_fusion), calls=%async_computation | async-start | bytes 6291456 | tf_op jit(solution)/shard_map/all_to_all | solution.py:79
Sparse Core Ops, SparseCore 0:
  16.5 156.0 reduce-scatter.3
  175.4 77.1 all-gather.2
  254.9 44.8 all-reduce.3
  302.7 82.1 all-gather.4
where the time goes:
time: 409 us; the launch traced here: 405 us
  waiting for transfers between devices  338 us (83%)
  matrix products  18.6 us (5%)
  other arithmetic  16.2 us (4%)
  between operations  14 us (3%)
  local copies, waits for them, and re-layouts  10.4 us (3%)
  starting transfers between devices  8 us (2%)
    unnamed x5, waiting for transfers between devices  157 us
    all_gather x1, waiting for transfers between devices, body(): lax.all_gather(proj_weight, 'fsdp', axis=0, tiled=True)  77.5 us
    all_to_all x1, waiting for transfers between devices, body(): lax.all_to_all(send_rows.reshape(group_size, capacity, SEG, D), 'fsdp', s...  47.4 us
    all_gather x1, waiting for transfers between devices, stem_taps(): lax.all_gather(stem_weight, 'fsdp', axis=1, tiled=True)  33.7 us
    psum x1, waiting for transfers between devices, body(): shard_sum = lax.psum(shard_sum, 'site')  22.9 us
    dot_general x1, matrix products, stem_taps(): jnp.einsum('rd,kcd->krc', frames, lax.all_gather(stem_weight, 'fsdp', axi...  8.38 us
  transfers between devices with their start and end apart: 5, of which 5 were waited for; matrix products, arithmetic and copies ran while one was open for 5% of the time, Pallas kernels for 0%

commit v1 on v0

--- a/solution.py
+++ b/solution.py
@@ -14,13 +14,11 @@
 EPSILON = 1e-05
 
 
-def stem_taps(frames, stem_weight):
-    return jnp.einsum(
-        "rd,kcd->krc",
-        frames,
-        lax.all_gather(stem_weight, "fsdp", axis=1, tiled=True),
-        preferred_element_type=jnp.float32,
+def stem_taps(frames, stem_gathered):
+    taps = jnp.einsum(
+        "rd,fkcd->krfc", frames, stem_gathered, preferred_element_type=jnp.float32
     )
+    return taps.reshape(taps.shape[0], taps.shape[1], -1)
 
 
 def body(held_input, held_cotangent, proj_weight, stem_weight, seg_counts):
@@ -35,9 +33,15 @@
     inverse = lax.rsqrt(variance + EPSILON)
     normed = centered * inverse
     normed_bf = normed.astype(jnp.bfloat16)
+    rows_w = proj_weight.shape[0]
+    taps_n, chans = stem_weight.shape[0], stem_weight.shape[1]
+    joined = jnp.concatenate([proj_weight, stem_weight.reshape(taps_n * chans, D)], 0)
+    gathered = lax.all_gather(joined, "fsdp", axis=0, tiled=False)
+    full_weight = gathered[:, :rows_w].reshape(group_size * rows_w, D)
+    stem_gathered = gathered[:, rows_w:].reshape(group_size, taps_n, chans, D)
     proj_back = lax.dot_general(
         cotangent,
-        lax.all_gather(proj_weight, "fsdp", axis=0, tiled=True),
+        full_weight,
         (((1,), (1,)), ((), ())),
         preferred_element_type=jnp.float32,
     )
@@ -85,7 +89,7 @@
     )
     picked = jnp.take(received.reshape(group_size * capacity, SEG, D), row_index, axis=0)
     frames = jnp.where(is_live[:, None, None], picked, zero_bf).reshape(OWN_SEG * SEG, D)
-    tap_terms = stem_taps(frames, stem_weight)
+    tap_terms = stem_taps(frames, stem_gathered)
     shifted = jnp.concatenate(
         [tap_terms[0][1:], jnp.zeros((1, tap_terms.shape[2]), jnp.float32)], 0
     )
@@ -95,10 +99,12 @@
         .reshape(2 * OWN_SEG * SEG, tap_terms.shape[2])
         .astype(jnp.bfloat16)
     )
+    partial = lax.dot_general(
+        normed_bf, cotangent, (((0,), (0,)), ((), ())), preferred_element_type=jnp.float32
+    )
+    partial, gathered = lax.optimization_barrier((partial, gathered))
     shard_sum = lax.psum_scatter(
-        lax.dot_general(
-            normed_bf, cotangent, (((0,), (0,)), ((), ())), preferred_element_type=jnp.float32
-        ),
+        partial,
         "fsdp",
         scatter_dimension=0,
         tiled=True,

time: 409 us -> 318 us (0.78)
  waiting for transfers between devices: 338 us -> 235 us
  local copies, waits for them, and re-layouts: 10.4 us -> 18.5 us
  other arithmetic: 16.2 us -> 23.4 us
    unnamed x5 -> x4, waiting for transfers between devices: 157 us -> 42.5 us
    all_gather x2 -> x1, waiting for transfers between devices: 111 us -> 79 us  [body(): gathered = lax.all_gather(joined, 'fsdp', axis=0, tiled=False)]
    all_to_all x1, waiting for transfers between devices: 47.4 us -> 75.3 us  [body(): lax.all_to_all(send_rows.reshape(group_size, capacity, SEG, D), 'fsdp', s...]
    psum x1, waiting for transfers between devices: 22.9 us -> 38.1 us  [body(): shard_sum = lax.psum(shard_sum, 'site')]
  transfers between devices with their start and end apart: 5 -> 4, of which waited for: 5 -> 4; matrix products, arithmetic and copies ran while one was open for 5% -> 18% of each run, Pallas kernels for 0% -> 0%
where the time goes in v1:
time: 318 us
  waiting for transfers between devices  235 us (74%)
  other arithmetic  23.4 us (7%)
  local copies, waits for them, and re-layouts  18.5 us (6%)
  matrix products  18.5 us (6%)
  between operations  13.9 us (4%)
  starting transfers between devices  8.41 us (3%)
    all_gather x1, waiting for transfers between devices, body(): gathered = lax.all_gather(joined, 'fsdp', axis=0, tiled=False)  79 us
    all_to_all x1, waiting for transfers between devices, body(): lax.all_to_all(send_rows.reshape(group_size, capacity, SEG, D), 'fsdp', s...  75.3 us
    unnamed x4, waiting for transfers between devices  42.5 us
    psum x1, waiting for transfers between devices, body(): shard_sum = lax.psum(shard_sum, 'site')  38.1 us
    dot_general x1, matrix products, stem_taps(): jnp.einsum('rd,fkcd->krfc', frames, stem_gathered, preferred_element_type...  8.76 us
    all_to_all x1, starting transfers between devices, body(): lax.all_to_all(send_rows.reshape(group_size, capacity, SEG, D), 'fsdp', s...  8.11 us
  transfers between devices with their start and end apart: 4, of which 4 were waited for; matrix products, arithmetic and copies ran while one was open for 18% of the time, Pallas kernels for 0%

profile of v1, /device:TPU:24, one launch (start us, length us, event | category | flops | bytes accessed | tf_op | source)
XLA Modules:
  0.0 317.7 jit_solution(13144479513820641416)
XLA Ops:
  7.2 0.0 copy-start
  7.2 0.0 copy-start.1
  7.2 0.0 all-gather.3.cloned.1.call-start
  7.2 1.7 pad_maximum_fusion.1
  9.0 0.0 all-gather.3.cloned.1.call-update
  9.0 0.0 reduce-scatter.4.cloned.1.call-start
  9.1 1.7 convert_reduce_fusion
  10.8 2.0 fusion.11
  12.7 0.0 copy-done
  12.7 0.0 copy-done.1
  12.7 5.3 %fusion.25 = f32[1536,1536]{1,0:T(8,128)} fusion(bf16[1,512,1536]{2,1,0:T(8,128)(2,1)S(1)} %copy-done, bf16[1,512,1536]{2,1,0:T(8,128)(2,1)S(1)} %copy-done.1, f32[512]{0:T(512)S(1)} %add_rsqrt_fusion, f32[512]{0:T(512)S(1)} %broadcast_multiply_fusion.3), kind=kOutput, calls=%fused_computation.35 | convolution fusion | flops 2419064832 | bytes 12587008 | tf_op jit(solution)/shard_map/dot_general | solution.py:102
  18.1 79.0 %all-gather.3.cloned.1.call-done = bf16[3072,1536]{1,0:T(8,128)(2,1)} async-done(((bf16[48,1536]{1,0:T(8,128)(2,1)}), bf16[3072,1536]{1,0:T(8,128)(2,1)}) %all-gather.3.cloned.1.call-update) | async-done | bytes 9437200 | tf_op jit(solution)/shard_map/all_gather | solution.py:39
  97.1 0.0 copy-start.2
  97.1 0.0 reduce-scatter.4.cloned.1.call-update
  97.1 0.6 copy-done.2
  97.7 0.1 copy.13
  97.8 0.1 reduce-window.8
  97.9 0.1 reduce.2
  98.0 0.6 fusion.45
  98.7 0.2 convert_reduce_fusion.3
  98.9 0.2 convert_reduce_fusion.2
  99.1 0.1 fusion.39
  99.2 0.2 broadcast_in_dim.86
  99.3 0.1 select_reduce_fusion
  99.4 0.1 reduce_sum.102
  99.6 2.7 slice.35
  102.3 4.4 %fusion.6 = (f32[512]{0:T(512)S(1)}, f32[1536,512]{0,1:T(8,128)}) fusion(bf16[1,512,1536]{2,1,0:T(8,128)(2,1)S(1)} %copy-done, f32[512]{0:T(512)S(1)} %add_rsqrt_fusion, f32[512]{0:T(512)S(1)} %broadcast_multiply_fusion.3, bf16[1536,1536]{1,0:T(8,128)(2,1)S(1)} %bitcast.101, bf16[1,512,1536]{2,1,0:T(8,128)(2,1)S(1)} %copy-done.1), kind=kOutput, calls=%fused_computation.12 | convolution fusion | flops 2419850752 | bytes 11016192 | tf_op jit(solution)/shard_map/dot_general | solution.py:42
  106.7 2.1 reduce_sum.105
  108.8 3.5 %fusion.27 = bf16[64,8,1536]{2,1,0:T(8,128)(2,1)S(1)} fusion(bf16[1,512,1536]{2,1,0:T(8,128)(2,1)S(1)} %copy-done, f32[1536,512]{0,1:T(8,128)} %get-tuple-element.7, bf16[1,512,1536]{2,1,0:T(8,128)(2,1)} %param.6, f32[512]{0:T(512)S(1)} %get-tuple-element.8, f32[512]{0:T(512)S(1)} %get-tuple-element.9, f32[512]{0:T(512)S(1)} %add_rsqrt_fusion, ...), kind=kLoop, calls=%fused_computation.36 | loop fusion | flops 7864320 | bytes 7872512 | tf_op jit(solution)/shard_map/reshape | solution.py:80
  112.2 2.4 gather_fusion
  114.7 3.4 %select_select_fusion = bf16[64,2,8,1536]{3,2,1,0:T(8,128)(2,1)} fusion(bf16[64,2,8,1536]{3,2,1,0:T(8,128)(2,1)} %bitcast.100, pred[64,2]{1,0:T(8,128)(4,1)S(1)} %compare_and_fusion, pred[64,2]{1,0:T(8,128)(4,1)S(1)} %broadcast_in_dim.86), kind=kLoop, calls=%fused_computation.24 | loop fusion | flops 3145728 | bytes 6291712 | tf_op jit(solution)/shard_map/jit(_where)/select_n | solution.py:82
  118.1 8.1 %all-to-all-start = ((bf16[64,2,8,1536]{3,2,1,0:T(8,128)(2,1)}), bf16[64,2,8,1536]{3,2,1,0:T(8,128)(2,1)S(1)}, u32[]{:S(2)}, u32[]{:S(2)}) async-start(bf16[64,2,8,1536]{3,2,1,0:T(8,128)(2,1)} %select_select_fusion), calls=%async_computation | async-start | bytes 6291456 | tf_op jit(solution)/shard_map/all_to_all | solution.py:83
  126.2 0.2 all-reduce.4.cloned.1.call-start
  126.4 0.7 iota_compare_fusion.3
  127.1 0.7 and_select_fusion.4
  127.7 0.2 convert_reduce_fusion.1
  127.9 1.3 fusion.52
  129.3 1.3 compare_and_fusion.1
  130.6 75.3 %all-to-all-done = bf16[64,2,8,1536]{3,2,1,0:T(8,128)(2,1)S(1)} async-done(((bf16[64,2,8,1536]{3,2,1,0:T(8,128)(2,1)}), bf16[64,2,8,1536]{3,2,1,0:T(8,128)(2,1)S(1)}, u32[]{:S(2)}, u32[]{:S(2)}) %all-to-all-start) | async-done | bytes 3145760 | tf_op jit(solution)/shard_map/all_to_all | solution.py:83
  205.9 2.4 gather_fusion.1
  208.3 8.8 %fusion.19 = f32[3,1024,64,8]{1,3,0,2:T(8,128)S(1)} fusion(bf16[128,8,1536]{2,1,0:T(8,128)(2,1)} %gather_fusion.1, pred[128]{0:T(512)(128)(4,1)S(1)} %compare_and_fusion.1, pred[128]{0:T(512)(128)(4,1)S(1)} %iota_compare_fusion.3, bf16[64,48,1536]{2,1,0:T(8,128)(2,1)} %bitcast.103), kind=kOutput, calls=%fused_computation.27 | convolution fusion | flops 4834983936 | bytes 14156032 | tf_op jit(solution)/shard_map/rd,fkcd->krfc/dot_general | solution.py:18
  217.1 1.1 fusion.35
  218.2 0.6 slice_bitcast_fusion.4
  218.8 0.5 fusion.36
  219.3 42.4 %reduce-scatter.4.cloned.1.call-done = f32[24,1536]{1,0:T(8,128)} async-done(((f32[1536,1536]{1,0:T(8,128)}), f32[24,1536]{1,0:T(8,128)}) %reduce-scatter.4.cloned.1.call-update) | async-done | bytes 147472
  261.8 0.0 all-reduce.4.cloned.1.call-update
  261.8 1.4 pad_maximum_fusion
  263.2 4.1 %copy.14 = bf16[1024,2,512]{2,1,0:T(2,128)(2,1)} copy(bf16[1024,2,512]{0,2,1:T(8,128)(2,1)S(1)} %pad_maximum_fusion) | data formatting | bytes 4194304 | tf_op jit(solution)/shard_map/stack | solution.py:98
  267.3 4.1 %convert_element_type.46 = bf16[1,2048,512]{2,1,0:T(8,128)(2,1)} reshape(bf16[1024,2,512]{2,1,0:T(2,128)(2,1)} %copy.14) | data formatting | bytes 4194304 | tf_op jit(solution)/shard_map/convert_element_type | solution.py:100
  271.4 38.1 %all-reduce.4.cloned.1.call-done = f32[24,1536]{1,0:T(8,128)} async-done(((f32[24,1536]{1,0:T(8,128)}), f32[24,1536]{1,0:T(8,128)}) %all-reduce.4.cloned.1.call-update) | async-done | bytes 147472 | tf_op jit(solution)/shard_map/psum | solution.py:112
  309.5 1.6 broadcast_multiply_fusion
  (8 shorter events, 0.1 us)
Async XLA Ops:
  7.2 5.6 %copy-start = (bf16[1,512,1536]{2,1,0:T(8,128)(2,1)S(1)}, bf16[1,512,1536]{2,1,0:T(8,128)(2,1)}, u32[]{:S(2)}) copy-start(bf16[1,512,1536]{2,1,0:T(8,128)(2,1)} %param.5) | copy-start | bytes 4718596
  7.2 5.6 %copy-start.1 = (bf16[1,512,1536]{2,1,0:T(8,128)(2,1)S(1)}, bf16[1,512,1536]{2,1,0:T(8,128)(2,1)}, u32[]{:S(2)}) copy-start(bf16[1,512,1536]{2,1,0:T(8,128)(2,1)} %param.6) | copy-start | bytes 4718596
  7.2 89.9 %all-gather.3.cloned.1.call-start = ((), (), s32[]{:S(2)}) async-start(), calls=%async_computation.3 | async-start | bytes 9584640 | tf_op jit(solution)/shard_map/all_gather | solution.py:39
  9.0 252.8 %reduce-scatter.4.cloned.1.call-start = ((), (), s32[]{:S(2)}) async-start(), calls=%async_computation.4 | async-start | bytes 9584640
  97.1 0.7 copy-start.2
  118.1 87.8 %all-to-all-start = ((bf16[64,2,8,1536]{3,2,1,0:T(8,128)(2,1)}), bf16[64,2,8,1536]{3,2,1,0:T(8,128)(2,1)S(1)}, u32[]{:S(2)}, u32[]{:S(2)}) async-start(bf16[64,2,8,1536]{3,2,1,0:T(8,128)(2,1)} %select_select_fusion), calls=%async_computation | async-start | bytes 6291456 | tf_op jit(solution)/shard_map/all_to_all | solution.py:83
  126.2 183.4 %all-reduce.4.cloned.1.call-start = ((), (), s32[]{:S(2)}) async-start(), calls=%async_computation.2 | async-start | bytes 294912 | tf_op jit(solution)/shard_map/psum | solution.py:112
Sparse Core Ops, SparseCore 0:
  11.3 85.7 all-gather.2
  101.4 160.3 reduce-scatter.3
  264.1 45.3 all-reduce.3

commit v2 on v1

--- a/solution.py
+++ b/solution.py
@@ -1,8 +1,11 @@
+import functools
 import math
 
 import jax
 import jax.numpy as jnp
 from jax import lax
+from jax.experimental import pallas as pl
+from jax.experimental.pallas import tpu as pltpu
 from jax.sharding import PartitionSpec as P
 
 D = 1536
@@ -19,6 +22,63 @@
         "rd,fkcd->krfc", frames, stem_gathered, preferred_element_type=jnp.float32
     )
     return taps.reshape(taps.shape[0], taps.shape[1], -1)
+
+
+def site_sum_kernel(n_site, part_ref, out_ref, slots, send_sems, recv_sems):
+    me = lax.axis_index("site")
+    col = lax.axis_index("fsdp")
+    mesh_kind = pl.DeviceIdType.MESH
+    barrier = pltpu.get_barrier_semaphore()
+    for step in range(1, n_site):
+        peer = lax.rem(me + step, n_site)
+        pl.semaphore_signal(barrier, inc=1, device_id=(peer, col), device_id_type=mesh_kind)
+    pl.semaphore_wait(barrier, n_site - 1)
+    copies = []
+    for step in range(1, n_site):
+        peer = lax.rem(me + step, n_site)
+        copy = pltpu.make_async_remote_copy(
+            src_ref=part_ref,
+            dst_ref=slots.at[me],
+            send_sem=send_sems.at[step],
+            recv_sem=recv_sems.at[me],
+            device_id=(peer, col),
+            device_id_type=mesh_kind,
+        )
+        copy.start()
+        copies.append(copy)
+    slots[me] = part_ref[...]
+    for copy in copies:
+        copy.wait_send()
+    for step in range(1, n_site):
+        src = lax.rem(me + step, n_site)
+        pltpu.make_async_remote_copy(
+            src_ref=part_ref,
+            dst_ref=slots.at[src],
+            send_sem=send_sems.at[0],
+            recv_sem=recv_sems.at[src],
+            device_id=(src, col),
+            device_id_type=mesh_kind,
+        ).wait_recv()
+    total = slots[0]
+    for index in range(1, n_site):
+        total = total + slots[index]
+    out_ref[...] = total
+
+
+def site_sum(part):
+    n_site = lax.axis_size("site")
+    return pl.pallas_call(
+        functools.partial(site_sum_kernel, n_site),
+        out_shape=jax.ShapeDtypeStruct(part.shape, part.dtype),
+        in_specs=[pl.BlockSpec(memory_space=pltpu.VMEM)],
+        out_specs=pl.BlockSpec(memory_space=pltpu.VMEM),
+        scratch_shapes=[
+            pltpu.VMEM((n_site,) + part.shape, part.dtype),
+            pltpu.SemaphoreType.DMA((n_site,)),
+            pltpu.SemaphoreType.DMA((n_site,)),
+        ],
+        compiler_params=pltpu.CompilerParams(collective_id=0, has_side_effects=True),
+    )(part)
 
 
 def body(held_input, held_cotangent, proj_weight, stem_weight, seg_counts):
@@ -109,7 +169,7 @@
         scatter_dimension=0,
         tiled=True,
     )
-    shard_sum = lax.psum(shard_sum, "site")
+    shard_sum = site_sum(shard_sum)
     weight_grad = shard_sum / math.sqrt(lax.axis_size("site") * group_size * HOLD * SEG)
     return (stem_rows[None], weight_grad)
 

time: 318 us -> 282 us (0.89)
  waiting for transfers between devices: 235 us -> 190 us
  Pallas kernels: 0 us -> 10.5 us
    psum x1 -> x0, waiting for transfers between devices: 38.1 us -> none  [body(): shard_sum = lax.psum(shard_sum, 'site')]
    pallas_call x0 -> x1, Pallas kernels: none -> 10.5 us  [site_sum(): pl.pallas_call(functools.partial(site_sum_kernel, n_site), out_shape=jax....]
    unnamed x4 -> x3, waiting for transfers between devices: 42.5 us -> 35.1 us
  transfers between devices with their start and end apart: 4 -> 3, of which waited for: 4 -> 3; matrix products, arithmetic and copies ran while one was open for 18% -> 19% of each run, Pallas kernels for 0% -> 0%
where the time goes in v2:
time: 282 us; the launch traced here: 281 us
  waiting for transfers between devices  190 us (67%)
  other arithmetic  22.2 us (8%)
  matrix products  18.5 us (7%)
  local copies, waits for them, and re-layouts  17.5 us (6%)
  between operations  14.2 us (5%)
  Pallas kernels  10.5 us (4%)
  starting transfers between devices  8.19 us (3%)
    all_gather x1, waiting for transfers between devices, body(): gathered = lax.all_gather(joined, 'fsdp', axis=0, tiled=False)  79 us
    all_to_all x1, waiting for transfers between devices, body(): lax.all_to_all(send_rows.reshape(group_size, capacity, SEG, D), 'fsdp', s...  75.5 us
    unnamed x3, waiting for transfers between devices  35.1 us
    pallas_call x1, Pallas kernels, site_sum(): pl.pallas_call(functools.partial(site_sum_kernel, n_site), out_shape=jax....  10.5 us
    dot_general x1, matrix products, stem_taps(): jnp.einsum('rd,fkcd->krfc', frames, stem_gathered, preferred_element_type...  8.75 us
    all_to_all x1, starting transfers between devices, body(): lax.all_to_all(send_rows.reshape(group_size, capacity, SEG, D), 'fsdp', s...  8.11 us
  transfers between devices with their start and end apart: 3, of which 3 were waited for; matrix products, arithmetic and copies ran while one was open for 19% of the time, Pallas kernels for 0%

profile of v2, /device:TPU:24, one launch (start us, length us, event | category | flops | bytes accessed | tf_op | source)
XLA Modules:
  0.0 280.7 jit_solution(11271936387257923441)
XLA Ops:
  7.2 0.0 copy-start
  7.2 0.0 copy-start.1
  7.2 0.0 all-gather.3.cloned.1.call-start
  7.2 1.7 pad_maximum_fusion.1
  9.0 0.0 all-gather.3.cloned.1.call-update
  9.0 0.0 reduce-scatter.4.cloned.1.call-start
  9.1 1.7 convert_reduce_fusion
  10.8 2.0 fusion.11
  12.7 0.0 copy-done
  12.7 0.0 copy-done.1
  12.7 5.3 %fusion.25 = f32[1536,1536]{1,0:T(8,128)} fusion(bf16[1,512,1536]{2,1,0:T(8,128)(2,1)S(1)} %copy-done, bf16[1,512,1536]{2,1,0:T(8,128)(2,1)S(1)} %copy-done.1, f32[512]{0:T(512)S(1)} %add_rsqrt_fusion, f32[512]{0:T(512)S(1)} %broadcast_multiply_fusion.3), kind=kOutput, calls=%fused_computation.35 | convolution fusion | flops 2419064832 | bytes 12587008 | tf_op jit(solution)/shard_map/dot_general | solution.py:162
  18.1 79.0 %all-gather.3.cloned.1.call-done = bf16[3072,1536]{1,0:T(8,128)(2,1)} async-done(((bf16[48,1536]{1,0:T(8,128)(2,1)}), bf16[3072,1536]{1,0:T(8,128)(2,1)}) %all-gather.3.cloned.1.call-update) | async-done | bytes 9437200 | tf_op jit(solution)/shard_map/all_gather | solution.py:99
  97.1 0.0 copy-start.2
  97.1 0.0 reduce-scatter.4.cloned.1.call-update
  97.1 0.6 copy-done.2
  97.7 0.1 copy.13
  97.8 0.1 reduce-window.8
  97.9 0.1 reduce.2
  98.0 0.6 fusion.45
  98.7 0.2 convert_reduce_fusion.3
  98.9 0.2 convert_reduce_fusion.2
  99.1 0.1 fusion.39
  99.2 0.2 broadcast_in_dim.86
  99.3 0.1 select_reduce_fusion
  99.4 0.1 reduce_sum.102
  99.6 2.7 slice.35
  102.3 4.4 %fusion.6 = (f32[512]{0:T(512)S(1)}, f32[1536,512]{0,1:T(8,128)}) fusion(bf16[1,512,1536]{2,1,0:T(8,128)(2,1)S(1)} %copy-done, f32[512]{0:T(512)S(1)} %add_rsqrt_fusion, f32[512]{0:T(512)S(1)} %broadcast_multiply_fusion.3, bf16[1536,1536]{1,0:T(8,128)(2,1)S(1)} %bitcast.101, bf16[1,512,1536]{2,1,0:T(8,128)(2,1)S(1)} %copy-done.1), kind=kOutput, calls=%fused_computation.12 | convolution fusion | flops 2419850752 | bytes 11016192 | tf_op jit(solution)/shard_map/dot_general | solution.py:102
  106.7 2.1 reduce_sum.105
  108.8 3.5 %fusion.27 = bf16[64,8,1536]{2,1,0:T(8,128)(2,1)S(1)} fusion(bf16[1,512,1536]{2,1,0:T(8,128)(2,1)S(1)} %copy-done, f32[1536,512]{0,1:T(8,128)} %get-tuple-element.7, bf16[1,512,1536]{2,1,0:T(8,128)(2,1)} %param.6, f32[512]{0:T(512)S(1)} %get-tuple-element.8, f32[512]{0:T(512)S(1)} %get-tuple-element.9, f32[512]{0:T(512)S(1)} %add_rsqrt_fusion, ...), kind=kLoop, calls=%fused_computation.36 | loop fusion | flops 7864320 | bytes 7872512 | tf_op jit(solution)/shard_map/reshape | solution.py:140
  112.2 2.4 gather_fusion
  114.7 3.4 %select_select_fusion = bf16[64,2,8,1536]{3,2,1,0:T(8,128)(2,1)} fusion(bf16[64,2,8,1536]{3,2,1,0:T(8,128)(2,1)} %bitcast.100, pred[64,2]{1,0:T(8,128)(4,1)S(1)} %compare_and_fusion, pred[64,2]{1,0:T(8,128)(4,1)S(1)} %broadcast_in_dim.86), kind=kLoop, calls=%fused_computation.24 | loop fusion | flops 3145728 | bytes 6291712 | tf_op jit(solution)/shard_map/jit(_where)/select_n | solution.py:142
  118.1 8.1 %all-to-all-start = ((bf16[64,2,8,1536]{3,2,1,0:T(8,128)(2,1)}), bf16[64,2,8,1536]{3,2,1,0:T(8,128)(2,1)S(1)}, u32[]{:S(2)}, u32[]{:S(2)}) async-start(bf16[64,2,8,1536]{3,2,1,0:T(8,128)(2,1)} %select_select_fusion), calls=%async_computation | async-start | bytes 6291456 | tf_op jit(solution)/shard_map/all_to_all | solution.py:143
  126.2 0.7 iota_compare_fusion.3
  126.8 0.7 and_select_fusion.4
  127.5 0.2 convert_reduce_fusion.1
  127.7 1.3 fusion.52
  129.0 1.3 compare_and_fusion.1
  130.4 75.5 %all-to-all-done = bf16[64,2,8,1536]{3,2,1,0:T(8,128)(2,1)S(1)} async-done(((bf16[64,2,8,1536]{3,2,1,0:T(8,128)(2,1)}), bf16[64,2,8,1536]{3,2,1,0:T(8,128)(2,1)S(1)}, u32[]{:S(2)}, u32[]{:S(2)}) %all-to-all-start) | async-done | bytes 3145760 | tf_op jit(solution)/shard_map/all_to_all | solution.py:143
  205.9 2.4 gather_fusion.1
  208.3 8.8 %fusion.19 = f32[3,1024,64,8]{1,3,0,2:T(8,128)S(1)} fusion(bf16[128,8,1536]{2,1,0:T(8,128)(2,1)} %gather_fusion.1, pred[128]{0:T(512)(128)(4,1)S(1)} %compare_and_fusion.1, pred[128]{0:T(512)(128)(4,1)S(1)} %iota_compare_fusion.3, bf16[64,48,1536]{2,1,0:T(8,128)(2,1)} %bitcast.103), kind=kOutput, calls=%fused_computation.27 | convolution fusion | flops 4834983936 | bytes 14156032 | tf_op jit(solution)/shard_map/rd,fkcd->krfc/dot_general | solution.py:21
  217.1 0.2 fusion.35
  217.3 0.6 slice_bitcast_fusion.4
  217.9 0.5 fusion.36
  218.4 0.2 pad_maximum_fusion
  218.6 4.1 %copy.14 = bf16[1024,2,512]{2,1,0:T(2,128)(2,1)} copy(bf16[1024,2,512]{0,2,1:T(8,128)(2,1)S(1)} %pad_maximum_fusion) | data formatting | bytes 4194304 | tf_op jit(solution)/shard_map/stack | solution.py:158
  222.7 4.1 %convert_element_type.46 = bf16[1,2048,512]{2,1,0:T(8,128)(2,1)} reshape(bf16[1024,2,512]{2,1,0:T(2,128)(2,1)} %copy.14) | data formatting | bytes 4194304 | tf_op jit(solution)/shard_map/convert_element_type | solution.py:160
  226.8 35.0 %reduce-scatter.4.cloned.1.call-done.part_ref = f32[24,1536]{1,0:T(8,128)} async-done(((f32[1536,1536]{1,0:T(8,128)}), f32[24,1536]{1,0:T(8,128)}) %reduce-scatter.4.cloned.1.call-update) | async-done | bytes 147472
  261.8 10.5 %shard_map.68 = f32[24,1536]{1,0:T(8,128)} custom-call(f32[24,1536]{1,0:T(8,128)} %reduce-scatter.4.cloned.1.call-done.part_ref), custom_call_target="tpu_custom_call" | custom-call | tf_op jit(solution)/shard_map/pallas_call | solution.py:70
  272.3 1.6 broadcast_multiply_fusion
  (8 shorter events, 0.1 us)
Async XLA Ops:
  7.2 5.6 %copy-start = (bf16[1,512,1536]{2,1,0:T(8,128)(2,1)S(1)}, bf16[1,512,1536]{2,1,0:T(8,128)(2,1)}, u32[]{:S(2)}) copy-start(bf16[1,512,1536]{2,1,0:T(8,128)(2,1)} %param.5) | copy-start | bytes 4718596
  7.2 5.6 %copy-start.1 = (bf16[1,512,1536]{2,1,0:T(8,128)(2,1)S(1)}, bf16[1,512,1536]{2,1,0:T(8,128)(2,1)}, u32[]{:S(2)}) copy-start(bf16[1,512,1536]{2,1,0:T(8,128)(2,1)} %param.6) | copy-start | bytes 4718596
  7.2 89.9 %all-gather.3.cloned.1.call-start = ((), (), s32[]{:S(2)}) async-start(), calls=%async_computation.2 | async-start | bytes 9584640 | tf_op jit(solution)/shard_map/all_gather | solution.py:99
  9.0 252.8 %reduce-scatter.4.cloned.1.call-start = ((), (), s32[]{:S(2)}) async-start(), calls=%async_computation.3 | async-start | bytes 9584640
  97.1 0.7 copy-start.2
  118.1 87.8 %all-to-all-start = ((bf16[64,2,8,1536]{3,2,1,0:T(8,128)(2,1)}), bf16[64,2,8,1536]{3,2,1,0:T(8,128)(2,1)S(1)}, u32[]{:S(2)}, u32[]{:S(2)}) async-start(bf16[64,2,8,1536]{3,2,1,0:T(8,128)(2,1)} %select_select_fusion), calls=%async_computation | async-start | bytes 6291456 | tf_op jit(solution)/shard_map/all_to_all | solution.py:143
Sparse Core Ops, SparseCore 0:
  11.3 85.7 all-gather.2
  101.4 160.3 reduce-scatter.3

commit v3 on v2

--- a/solution.py
+++ b/solution.py
@@ -63,6 +63,99 @@
     for index in range(1, n_site):
         total = total + slots[index]
     out_ref[...] = total
+
+
+def fsdp_sum_kernel(n_chip, part_ref, out_ref, xbuf, rbuf, sems0, send_sems, recv_sems):
+    me = lax.axis_index("fsdp")
+    site = lax.axis_index("site")
+    core = lax.rem(me, 2)
+    chip = me // 2
+    sibling = me + 1 - 2 * core
+    mesh_kind = pl.DeviceIdType.MESH
+    barrier = pltpu.get_barrier_semaphore()
+    pl.semaphore_signal(barrier, inc=1, device_id=(site, sibling), device_id_type=mesh_kind)
+
+    def greet(step, carry):
+        peer = 2 * lax.rem(chip + step, n_chip) + core
+        pl.semaphore_signal(barrier, inc=1, device_id=(site, peer), device_id_type=mesh_kind)
+        return carry
+
+    lax.fori_loop(1, n_chip, greet, 0)
+    pl.semaphore_wait(barrier, n_chip)
+    swap = pltpu.make_async_remote_copy(
+        src_ref=part_ref.at[1 - core],
+        dst_ref=xbuf,
+        send_sem=sems0.at[0],
+        recv_sem=sems0.at[1],
+        device_id=(site, sibling),
+        device_id_type=mesh_kind,
+    )
+    swap.start()
+    swap.wait()
+
+    def push(step, carry):
+        target = lax.rem(chip + step, n_chip)
+        xbuf[target] = xbuf[target] + part_ref[core, target]
+        pltpu.make_async_remote_copy(
+            src_ref=xbuf.at[target],
+            dst_ref=rbuf.at[chip],
+            send_sem=send_sems.at[target],
+            recv_sem=recv_sems.at[chip],
+            device_id=(site, 2 * target + core),
+            device_id_type=mesh_kind,
+        ).start()
+        return carry
+
+    lax.fori_loop(1, n_chip, push, 0)
+    rbuf[chip] = xbuf[chip] + part_ref[core, chip]
+
+    def drain(step, carry):
+        target = lax.rem(chip + step, n_chip)
+        pltpu.make_async_remote_copy(
+            src_ref=xbuf.at[target],
+            dst_ref=rbuf.at[chip],
+            send_sem=send_sems.at[target],
+            recv_sem=recv_sems.at[chip],
+            device_id=(site, 2 * target + core),
+            device_id_type=mesh_kind,
+        ).wait_send()
+        pltpu.make_async_remote_copy(
+            src_ref=xbuf.at[target],
+            dst_ref=rbuf.at[target],
+            send_sem=send_sems.at[target],
+            recv_sem=recv_sems.at[target],
+            device_id=(site, 2 * target + core),
+            device_id_type=mesh_kind,
+        ).wait_recv()
+        return carry
+
+    lax.fori_loop(1, n_chip, drain, 0)
+    out_ref[...] = rbuf[0]
+
+    def gather_sum(index, carry):
+        out_ref[...] = out_ref[...] + rbuf[index]
+        return carry
+
+    lax.fori_loop(1, n_chip, gather_sum, 0)
+
+
+def fsdp_sum(part):
+    n_chip = part.shape[1]
+    block = part.shape[2:]
+    return pl.pallas_call(
+        functools.partial(fsdp_sum_kernel, n_chip),
+        out_shape=jax.ShapeDtypeStruct(block, part.dtype),
+        in_specs=[pl.BlockSpec(memory_space=pltpu.VMEM)],
+        out_specs=pl.BlockSpec(memory_space=pltpu.VMEM),
+        scratch_shapes=[
+            pltpu.VMEM((n_chip,) + block, part.dtype),
+            pltpu.VMEM((n_chip,) + block, part.dtype),
+            pltpu.SemaphoreType.DMA((2,)),
+            pltpu.SemaphoreType.DMA((n_chip,)),
+            pltpu.SemaphoreType.DMA((n_chip,)),
+        ],
+        compiler_params=pltpu.CompilerParams(collective_id=1, has_side_effects=True),
+    )(part)
 
 
 def site_sum(part):
@@ -159,16 +252,14 @@
         .reshape(2 * OWN_SEG * SEG, tap_terms.shape[2])
         .astype(jnp.bfloat16)
     )
-    partial = lax.dot_general(
-        normed_bf, cotangent, (((0,), (0,)), ((), ())), preferred_element_type=jnp.float32
-    )
-    partial, gathered = lax.optimization_barrier((partial, gathered))
-    shard_sum = lax.psum_scatter(
-        partial,
-        "fsdp",
-        scatter_dimension=0,
-        tiled=True,
-    )
+    rows_out = D // group_size
+    partial = jnp.einsum(
+        "rckj,rd->kcjd",
+        normed_bf.reshape(normed_bf.shape[0], group_size // 2, 2, rows_out),
+        cotangent,
+        preferred_element_type=jnp.float32,
+    )
+    shard_sum = fsdp_sum(partial)
     shard_sum = site_sum(shard_sum)
     weight_grad = shard_sum / math.sqrt(lax.axis_size("site") * group_size * HOLD * SEG)
     return (stem_rows[None], weight_grad)

time: 282 us -> 364 us (1.29)
  Pallas kernels: 10.5 us -> 193 us
  waiting for transfers between devices: 190 us -> 82.6 us
  local copies, waits for them, and re-layouts: 17.5 us -> 22.2 us
    pallas_call x0 -> x1, Pallas kernels: none -> 181 us  [fsdp_sum(): pl.pallas_call(functools.partial(fsdp_sum_kernel, n_chip), out_shape=jax....]
    all_to_all x1, waiting for transfers between devices: 75.5 us -> 0.01 us  [body(): lax.all_to_all(send_rows.reshape(group_size, capacity, SEG, D), 'fsdp', s...]
    unnamed x3 -> x1, waiting for transfers between devices: 35.1 us -> 0.02 us
  transfers between devices with their start and end apart: 3 -> 2, of which waited for: 3 -> 1; matrix products, arithmetic and copies ran while one was open for 19% -> 5% of each run, Pallas kernels for 0% -> 53%
where the time goes in v3:
time: 364 us; the launch traced here: 363 us
  Pallas kernels  193 us (53%)
  waiting for transfers between devices  82.6 us (23%)
  other arithmetic  23.2 us (6%)
  local copies, waits for them, and re-layouts  22.2 us (6%)
  matrix products  19.5 us (5%)
  between operations  14.2 us (4%)
  starting transfers between devices  8.33 us (2%)
    pallas_call x1, Pallas kernels, fsdp_sum(): pl.pallas_call(functools.partial(fsdp_sum_kernel, n_chip), out_shape=jax....  181 us
    all_gather x1, waiting for transfers between devices, body(): gathered = lax.all_gather(joined, 'fsdp', axis=0, tiled=False)  82.6 us
    pallas_call x1, Pallas kernels, site_sum(): pl.pallas_call(functools.partial(site_sum_kernel, n_site), out_shape=jax....  12.5 us
    dot_general x1, matrix products, stem_taps(): jnp.einsum('rd,fkcd->krfc', frames, stem_gathered, preferred_element_type...  8.7 us
    all_to_all x1, starting transfers between devices, body(): lax.all_to_all(send_rows.reshape(group_size, capacity, SEG, D), 'fsdp', s...  8.29 us
  transfers between devices with their start and end apart: 2, of which 1 were waited for; matrix products, arithmetic and copies ran while one was open for 5% of the time, Pallas kernels for 53%

profile of v3, /device:TPU:24, one launch (start us, length us, event | category | flops | bytes accessed | tf_op | source)
XLA Modules:
  0.0 363.3 jit_solution(6020575101004305251)
XLA Ops:
  7.2 0.0 copy-start
  7.2 0.0 all-gather.3.cloned.1.call-start
  7.2 1.7 pad_maximum_fusion.1
  8.9 0.0 all-gather.3.cloned.1.call-update
  9.0 0.7 copy.15
  9.7 0.1 reduce-window.8
  9.8 0.1 reduce.2
  9.9 1.4 fusion.41
  11.3 0.2 convert_reduce_fusion.3
  11.4 0.2 convert_reduce_fusion.2
  11.6 0.1 select_reduce_fusion
  11.7 0.1 reduce_sum.102
  11.9 0.1 fusion.35
  12.0 0.2 broadcast_in_dim.86
  12.2 1.7 convert_reduce_fusion
  13.9 0.0 copy-done
  13.9 0.5 fusion.11
  14.5 82.6 %all-gather.3.cloned.1.call-done = bf16[3072,1536]{1,0:T(8,128)(2,1)} async-done(((bf16[48,1536]{1,0:T(8,128)(2,1)}), bf16[3072,1536]{1,0:T(8,128)(2,1)}) %all-gather.3.cloned.1.call-update) | async-done | bytes 9437200 | tf_op jit(solution)/shard_map/all_gather | solution.py:192
  97.1 0.0 copy-start.1
  97.1 2.8 slice.35
  99.9 0.1 copy-done.1
  99.9 4.4 %fusion.6 = (f32[512]{0:T(512)S(1)}, f32[1536,512]{0,1:T(8,128)}) fusion(bf16[1,512,1536]{2,1,0:T(8,128)(2,1)S(1)} %copy-done, f32[512]{0:T(512)S(1)} %add_rsqrt_fusion, f32[512]{0:T(512)S(1)} %broadcast_multiply_fusion.3, bf16[1536,1536]{1,0:T(8,128)(2,1)S(1)} %bitcast.101, bf16[1,512,1536]{2,1,0:T(8,128)(2,1)S(1)} %copy-done.1), kind=kOutput, calls=%fused_computation.13 | convolution fusion | flops 2419850752 | bytes 11016192 | tf_op jit(solution)/shard_map/dot_general | solution.py:195
  104.3 2.1 reduce_sum.105
  106.4 3.4 fusion.24
  109.8 2.4 gather_fusion
  112.2 3.3 select_select_fusion
  115.6 8.3 %all-to-all-start = ((bf16[64,2,8,1536]{3,2,1,0:T(8,128)(2,1)}), bf16[64,2,8,1536]{3,2,1,0:T(8,128)(2,1)}, u32[]{:S(2)}, u32[]{:S(2)}) async-start(bf16[64,2,8,1536]{3,2,1,0:T(8,128)(2,1)} %select_select_fusion), calls=%async_computation | async-start | bytes 6291456 | tf_op jit(solution)/shard_map/all_to_all | solution.py:236
  123.9 0.4 fusion.13
  124.3 0.7 copy.17
  125.0 6.5 %convolution_bitcast_fusion.part_ref = f32[2,32,24,1536]{3,2,1,0:T(8,128)} fusion(bf16[1,512,1536]{2,1,0:T(8,128)(2,1)} %param.6, bf16[512,32,2,24]{0,3,2,1:T(8,128)(2,1)S(1)} %bitcast.104), kind=kOutput, calls=%fused_computation.2 | convolution fusion | flops 2415919104 | bytes 12582912 | tf_op jit(solution)/shard_map/rckj,rd->kcjd/dot_general | solution.py:256
  131.5 180.6 %shard_map.68.part_ref = f32[24,1536]{1,0:T(8,128)} custom-call(f32[2,32,24,1536]{3,2,1,0:T(8,128)} %convolution_bitcast_fusion.part_ref), custom_call_target="tpu_custom_call" | custom-call | tf_op jit(solution)/shard_map/pallas_call | solution.py:145
  312.1 12.5 %shard_map.69 = f32[24,1536]{1,0:T(8,128)} custom-call(f32[24,1536]{1,0:T(8,128)} %shard_map.68.part_ref), custom_call_target="tpu_custom_call" | custom-call | tf_op jit(solution)/shard_map/pallas_call | solution.py:163
  324.6 0.7 iota_compare_fusion.3
  325.3 0.7 and_select_fusion.4
  326.0 0.2 convert_reduce_fusion.1
  326.2 1.4 fusion.48
  327.5 1.3 compare_and_fusion.1
  328.9 1.6 broadcast_multiply_fusion
  330.5 0.0 all-to-all-done
  330.5 4.3 %gather_fusion.1 = bf16[128,8,1536]{2,1,0:T(8,128)(2,1)} fusion(bf16[128,8,1536]{2,1,0:T(8,128)(2,1)} %bitcast.13, s32[1024]{0:T(1024)S(1)} %pad_clamp_fusion), kind=kCustom, calls=%fused_computation.1 | custom fusion | bytes 6291968 | tf_op jit(solution)/shard_map/jit(_take)/gather | solution.py:243
  334.7 8.7 %fusion.19 = f32[3,1024,64,8]{1,3,0,2:T(8,128)S(1)} fusion(bf16[128,8,1536]{2,1,0:T(8,128)(2,1)} %gather_fusion.1, pred[128]{0:T(512)(128)(4,1)S(1)} %compare_and_fusion.1, pred[128]{0:T(512)(128)(4,1)S(1)} %iota_compare_fusion.3, bf16[64,48,1536]{2,1,0:T(8,128)(2,1)} %bitcast.103), kind=kOutput, calls=%fused_computation.28 | convolution fusion | flops 4834983936 | bytes 14156032 | tf_op jit(solution)/shard_map/rd,fkcd->krfc/dot_general | solution.py:21
  343.4 0.6 slice_bitcast_fusion.4
  344.1 0.2 fusion.31
  344.2 0.5 fusion.32
  344.7 1.5 pad_maximum_fusion
  346.2 6.1 %copy.16 = bf16[1024,2,512]{2,1,0:T(2,128)(2,1)} copy(bf16[1024,2,512]{0,2,1:T(8,128)(2,1)} %pad_maximum_fusion) | data formatting | bytes 4194304 | tf_op jit(solution)/shard_map/stack | solution.py:251
  352.4 4.1 %convert_element_type.48 = bf16[1,2048,512]{2,1,0:T(8,128)(2,1)} reshape(bf16[1024,2,512]{2,1,0:T(2,128)(2,1)} %copy.16) | data formatting | bytes 4194304 | tf_op jit(solution)/shard_map/convert_element_type | solution.py:253
  (8 shorter events, 0.1 us)
Async XLA Ops:
  7.2 6.7 %copy-start = (bf16[1,512,1536]{2,1,0:T(8,128)(2,1)S(1)}, bf16[1,512,1536]{2,1,0:T(8,128)(2,1)}, u32[]{:S(2)}) copy-start(bf16[1,512,1536]{2,1,0:T(8,128)(2,1)} %param.5) | copy-start | bytes 4718596
  7.2 89.9 %all-gather.3.cloned.1.call-start = ((), (), s32[]{:S(2)}) async-start(), calls=%async_computation.1 | async-start | bytes 9584640 | tf_op jit(solution)/shard_map/all_gather | solution.py:192
  97.1 2.8 copy-start.1
  115.6 214.9 %all-to-all-start = ((bf16[64,2,8,1536]{3,2,1,0:T(8,128)(2,1)}), bf16[64,2,8,1536]{3,2,1,0:T(8,128)(2,1)}, u32[]{:S(2)}, u32[]{:S(2)}) async-start(bf16[64,2,8,1536]{3,2,1,0:T(8,128)(2,1)} %select_select_fusion), calls=%async_computation | async-start | bytes 6291456 | tf_op jit(solution)/shard_map/all_to_all | solution.py:236
Sparse Core Ops, SparseCore 0:
  11.3 85.7 all-gather.2

commit v4 on v3

--- a/solution.py
+++ b/solution.py
@@ -190,6 +190,21 @@
     taps_n, chans = stem_weight.shape[0], stem_weight.shape[1]
     joined = jnp.concatenate([proj_weight, stem_weight.reshape(taps_n * chans, D)], 0)
     gathered = lax.all_gather(joined, "fsdp", axis=0, tiled=False)
+    rows_out = D // group_size
+    half = D // 2
+    partial = jnp.einsum(
+        "rckj,rd->kcjd",
+        normed_bf.reshape(normed_bf.shape[0], group_size // 2, 2, rows_out),
+        cotangent[:, :half],
+        preferred_element_type=jnp.float32,
+    )
+    kernel_sum = fsdp_sum(partial)
+    partial_sc = lax.dot_general(
+        normed_bf, cotangent[:, half:], (((0,), (0,)), ((), ())), preferred_element_type=jnp.float32
+    )
+    partial_sc, kernel_sum, gathered = lax.optimization_barrier((partial_sc, kernel_sum, gathered))
+    queue_sum = lax.psum_scatter(partial_sc, "fsdp", scatter_dimension=0, tiled=True)
+    shard_sum = jnp.concatenate([kernel_sum, queue_sum], 1)
     full_weight = gathered[:, :rows_w].reshape(group_size * rows_w, D)
     stem_gathered = gathered[:, rows_w:].reshape(group_size, taps_n, chans, D)
     proj_back = lax.dot_general(
@@ -252,14 +267,6 @@
         .reshape(2 * OWN_SEG * SEG, tap_terms.shape[2])
         .astype(jnp.bfloat16)
     )
-    rows_out = D // group_size
-    partial = jnp.einsum(
-        "rckj,rd->kcjd",
-        normed_bf.reshape(normed_bf.shape[0], group_size // 2, 2, rows_out),
-        cotangent,
-        preferred_element_type=jnp.float32,
-    )
-    shard_sum = fsdp_sum(partial)
     shard_sum = site_sum(shard_sum)
     weight_grad = shard_sum / math.sqrt(lax.axis_size("site") * group_size * HOLD * SEG)
     return (stem_rows[None], weight_grad)

time: 364 us -> 324 us (0.89)
  Pallas kernels: 193 us -> 87.5 us
  waiting for transfers between devices: 82.6 us -> 149 us
    pallas_call x1, Pallas kernels: 181 us -> 77 us  [fsdp_sum(): pl.pallas_call(functools.partial(fsdp_sum_kernel, n_chip), out_shape=jax....]
    all_to_all x1, waiting for transfers between devices: 0.01 us -> 68.9 us  [body(): lax.all_to_all(send_rows.reshape(group_size, capacity, SEG, D), 'fsdp', s...]
    all_gather x1, waiting for transfers between devices: 82.6 us -> 24.3 us  [body(): gathered = lax.all_gather(joined, 'fsdp', axis=0, tiled=False)]
    unnamed x1 -> x3, waiting for transfers between devices: 0.02 us -> 56.2 us
    dot_general x0 -> x1, matrix products: none -> 3.82 us  [body(): lax.dot_general(normed_bf, cotangent[:, half:], (((0,), (0,)), ((), ())),...]
  transfers between devices with their start and end apart: 2 -> 3, of which waited for: 1 -> 3; matrix products, arithmetic and copies ran while one was open for 5% -> 12% of each run, Pallas kernels for 53% -> 24%
where the time goes in v4:
time: 324 us; the launch traced here: 323 us
  waiting for transfers between devices  149 us (46%)
  Pallas kernels  87.5 us (27%)
  local copies, waits for them, and re-layouts  21.6 us (7%)
  other arithmetic  21.4 us (7%)
  matrix products  20.6 us (6%)
  between operations  14.2 us (4%)
  starting transfers between devices  8.26 us (3%)
    pallas_call x1, Pallas kernels, fsdp_sum(): pl.pallas_call(functools.partial(fsdp_sum_kernel, n_chip), out_shape=jax....  77 us
    all_to_all x1, waiting for transfers between devices, body(): lax.all_to_all(send_rows.reshape(group_size, capacity, SEG, D), 'fsdp', s...  68.9 us
    unnamed x3, waiting for transfers between devices  56.2 us
    all_gather x1, waiting for transfers between devices, body(): gathered = lax.all_gather(joined, 'fsdp', axis=0, tiled=False)  24.3 us
    pallas_call x1, Pallas kernels, site_sum(): pl.pallas_call(functools.partial(site_sum_kernel, n_site), out_shape=jax....  10.5 us
    dot_general x1, matrix products, stem_taps(): jnp.einsum('rd,fkcd->krfc', frames, stem_gathered, preferred_element_type...  8.7 us
    all_to_all x1, starting transfers between devices, body(): lax.all_to_all(send_rows.reshape(group_size, capacity, SEG, D), 'fsdp', s...  8 us
  transfers between devices with their start and end apart: 3, of which 3 were waited for; matrix products, arithmetic and copies ran while one was open for 12% of the time, Pallas kernels for 24%

profile of v4, /device:TPU:24, one launch (start us, length us, event | category | flops | bytes accessed | tf_op | source)
XLA Modules:
  0.0 323.1 jit_solution(17524168066903947171)
XLA Ops:
  7.2 0.0 copy-start
  7.2 0.0 all-gather.3.cloned.1.call-start
  7.2 1.7 pad_maximum_fusion.1
  8.9 0.0 all-gather.3.cloned.1.call-update
  9.0 0.7 copy.21
  9.7 0.1 reduce-window.8
  9.8 0.1 reduce.2
  9.9 1.4 fusion.41
  11.3 0.2 convert_reduce_fusion.3
  11.4 0.2 convert_reduce_fusion.2
  11.6 0.1 fusion.35
  11.7 0.2 broadcast_in_dim.86
  11.9 0.1 select_reduce_fusion
  12.0 0.1 reduce_sum.104
  12.1 0.0 copy-start.2
  12.2 3.2 copy.19
  15.3 0.0 copy-done
  15.3 0.0 copy-start.1
  15.3 0.3 convert_reduce_fusion
  15.6 0.5 multiply_reduce_fusion
  16.2 0.0 copy-done.2
  16.2 1.0 copy-done.1
  17.2 3.7 %convolution_bitcast_fusion.part_ref = f32[2,32,24,768]{3,2,1,0:T(8,128)} fusion(bf16[512,1536]{1,0:T(8,128)(2,1)S(1)} %bitcast.101, f32[512,32,2,24]{0,3,2,1:T(8,128)S(1)} %bitcast.97, f32[512]{0:T(512)S(1)} %add_rsqrt_fusion, f32[512]{0:T(512)S(1)} %broadcast_multiply_fusion.3), kind=kOutput, calls=%fused_computation.25 | convolution fusion | flops 1210318848 | bytes 8654848 | tf_op jit(solution)/shard_map/rckj,rd->kcjd/dot_general | solution.py:195
  20.9 77.0 %shard_map.68 = f32[24,768]{1,0:T(8,128)} custom-call(f32[2,32,24,768]{3,2,1,0:T(8,128)} %convolution_bitcast_fusion.part_ref), custom_call_target="tpu_custom_call" | custom-call | tf_op jit(solution)/shard_map/pallas_call | solution.py:145
  98.0 3.8 %fusion.22 = f32[1536,768]{1,0:T(8,128)} fusion(bf16[1,512,1536]{2,1,0:T(8,128)(2,1)S(1)} %copy-done, f32[512]{0:T(512)S(1)} %add_rsqrt_fusion, f32[512]{0:T(512)S(1)} %broadcast_multiply_fusion.3, bf16[512,1536]{1,0:T(8,128)(2,1)S(1)} %bitcast.102), kind=kOutput, calls=%fused_computation.32 | convolution fusion | flops 1211105280 | bytes 7081984 | tf_op jit(solution)/shard_map/dot_general | solution.py:202
  101.8 24.3 %all-gather.3.cloned.1.call-done = bf16[3072,1536]{1,0:T(8,128)(2,1)} async-done(((bf16[48,1536]{1,0:T(8,128)(2,1)}), bf16[3072,1536]{1,0:T(8,128)(2,1)}) %all-gather.3.cloned.1.call-update) | async-done | bytes 9437200 | tf_op jit(solution)/shard_map/all_gather | solution.py:192
  126.1 2.6 slice.33
  128.8 4.3 %fusion.8 = (f32[512]{0:T(512)S(1)}, f32[1536,512]{0,1:T(8,128)}) fusion(bf16[1,512,1536]{2,1,0:T(8,128)(2,1)S(1)} %copy-done, f32[512]{0:T(512)S(1)} %add_rsqrt_fusion, f32[512]{0:T(512)S(1)} %broadcast_multiply_fusion.3, bf16[1536,1536]{1,0:T(8,128)(2,1)S(1)} %bitcast.100, bf16[1,512,1536]{2,1,0:T(8,128)(2,1)S(1)} %copy-done.2), kind=kOutput, calls=%fused_computation.12 | convolution fusion | flops 2419850752 | bytes 11016192 | tf_op jit(solution)/shard_map/dot_general | solution.py:210
  133.1 2.1 reduce_sum.105
  135.2 3.4 %fusion.24 = bf16[64,8,1536]{2,1,0:T(8,128)(2,1)S(1)} fusion(bf16[1,512,1536]{2,1,0:T(8,128)(2,1)S(1)} %copy-done, f32[1536,512]{0,1:T(8,128)} %get-tuple-element.11, f32[512]{0:T(512)S(1)} %get-tuple-element.12, f32[512]{0:T(512)S(1)} %get-tuple-element.13, f32[512]{0:T(512)S(1)} %add_rsqrt_fusion, f32[512]{0:T(512)S(1)} %broadcast_multiply_fusion.3, ...), kind=kLoop, calls=%fused_computation.33 | loop fusion | flops 7864320 | bytes 7872512 | tf_op jit(solution)/shard_map/reshape | solution.py:248
  138.7 2.4 gather_fusion
  141.1 3.3 %select_select_fusion = bf16[64,2,8,1536]{3,2,1,0:T(8,128)(2,1)} fusion(bf16[64,2,8,1536]{3,2,1,0:T(8,128)(2,1)} %bitcast.99, pred[64,2]{1,0:T(8,128)(4,1)S(1)} %compare_and_fusion, pred[64,2]{1,0:T(8,128)(4,1)S(1)} %broadcast_in_dim.86), kind=kLoop, calls=%fused_computation.16 | loop fusion | flops 3145728 | bytes 6291712 | tf_op jit(solution)/shard_map/jit(_where)/select_n | solution.py:250
  144.4 8.0 %all-to-all-start = ((bf16[64,2,8,1536]{3,2,1,0:T(8,128)(2,1)}), bf16[64,2,8,1536]{3,2,1,0:T(8,128)(2,1)S(1)}, u32[]{:S(2)}, u32[]{:S(2)}) async-start(bf16[64,2,8,1536]{3,2,1,0:T(8,128)(2,1)} %select_select_fusion), calls=%async_computation | async-start | bytes 6291456 | tf_op jit(solution)/shard_map/all_to_all | solution.py:251
  152.4 0.2 reduce-scatter.4.cloned.1.call-start
  152.6 0.5 reduce-scatter.4.cloned.1.call-update
  153.1 0.7 iota_compare_fusion.3
  153.8 0.6 and_select_fusion.4
  154.4 0.2 convert_reduce_fusion.1
  154.6 1.3 fusion.48
  155.9 1.3 compare_and_fusion.1
  157.2 68.9 %all-to-all-done = bf16[64,2,8,1536]{3,2,1,0:T(8,128)(2,1)S(1)} async-done(((bf16[64,2,8,1536]{3,2,1,0:T(8,128)(2,1)}), bf16[64,2,8,1536]{3,2,1,0:T(8,128)(2,1)S(1)}, u32[]{:S(2)}, u32[]{:S(2)}) %all-to-all-start) | async-done | bytes 3145760 | tf_op jit(solution)/shard_map/all_to_all | solution.py:251
  226.2 2.4 gather_fusion.1
  228.5 8.7 %fusion.14 = f32[3,1024,64,8]{1,3,0,2:T(8,128)S(1)} fusion(bf16[128,8,1536]{2,1,0:T(8,128)(2,1)} %gather_fusion.1, pred[128]{0:T(512)(128)(4,1)S(1)} %compare_and_fusion.1, pred[128]{0:T(512)(128)(4,1)S(1)} %iota_compare_fusion.3, bf16[64,48,1536]{2,1,0:T(8,128)(2,1)} %bitcast.104), kind=kOutput, calls=%fused_computation.22 | convolution fusion | flops 4834983936 | bytes 14156032 | tf_op jit(solution)/shard_map/rd,fkcd->krfc/dot_general | solution.py:21
  237.2 0.2 fusion.30
  237.4 0.6 slice_bitcast_fusion
  238.0 0.5 fusion.31
  238.5 0.2 pad_maximum_fusion
  238.7 4.1 %copy.22 = bf16[1024,2,512]{2,1,0:T(2,128)(2,1)} copy(bf16[1024,2,512]{0,2,1:T(8,128)(2,1)S(1)} %pad_maximum_fusion) | data formatting | bytes 4194304 | tf_op jit(solution)/shard_map/stack | solution.py:266
  242.8 0.0 copy-start.3
  242.8 4.1 %convert_element_type.55 = bf16[1,2048,512]{2,1,0:T(8,128)(2,1)} reshape(bf16[1024,2,512]{2,1,0:T(2,128)(2,1)} %copy.22) | data formatting | bytes 4194304 | tf_op jit(solution)/shard_map/convert_element_type | solution.py:268
  246.9 55.6 %reduce-scatter.4.cloned.1.call-done = f32[24,768]{1,0:T(8,128)} async-done(((f32[1536,768]{1,0:T(8,128)}), f32[24,768]{1,0:T(8,128)}) %reduce-scatter.4.cloned.1.call-update) | async-done | bytes 73744
  302.6 0.0 copy-done.3
  302.6 1.6 pad_maximum_fusion.2.part_ref
  304.1 10.5 %shard_map.69 = f32[24,1536]{1,0:T(8,128)} custom-call(f32[24,1536]{1,0:T(8,128)} %pad_maximum_fusion.2.part_ref), custom_call_target="tpu_custom_call" | custom-call | tf_op jit(solution)/shard_map/pallas_call | solution.py:163
  314.7 1.6 broadcast_multiply_fusion
  (8 shorter events, 0.1 us)
Async XLA Ops:
  7.2 8.2 %copy-start = (bf16[1,512,1536]{2,1,0:T(8,128)(2,1)S(1)}, bf16[1,512,1536]{2,1,0:T(8,128)(2,1)}, u32[]{:S(2)}) copy-start(bf16[1,512,1536]{2,1,0:T(8,128)(2,1)} %param.5) | copy-start | bytes 4718596
  7.2 118.9 %all-gather.3.cloned.1.call-start = ((), (), s32[]{:S(2)}) async-start(), calls=%async_computation.2 | async-start | bytes 9584640 | tf_op jit(solution)/shard_map/all_gather | solution.py:192
  12.1 4.0 %copy-start.2 = (bf16[1,512,1536]{2,1,0:T(8,128)(2,1)S(1)}, bf16[1,512,1536]{2,1,0:T(8,128)(2,1)}, u32[]{:S(2)}) copy-start(bf16[1,512,1536]{2,1,0:T(8,128)(2,1)} %param.6) | copy-start | bytes 4718596
  15.3 1.9 copy-start.1
  144.4 81.8 %all-to-all-start = ((bf16[64,2,8,1536]{3,2,1,0:T(8,128)(2,1)}), bf16[64,2,8,1536]{3,2,1,0:T(8,128)(2,1)S(1)}, u32[]{:S(2)}, u32[]{:S(2)}) async-start(bf16[64,2,8,1536]{3,2,1,0:T(8,128)(2,1)} %select_select_fusion), calls=%async_computation | async-start | bytes 6291456 | tf_op jit(solution)/shard_map/all_to_all | solution.py:251
  152.4 150.2 %reduce-scatter.4.cloned.1.call-start = ((), (), s32[]{:S(2)}) async-start(), calls=%async_computation.3 | async-start | bytes 4792320
  242.8 59.8 %copy-start.3 = (f32[24,768]{1,0:T(8,128)S(1)}, f32[24,768]{1,0:T(8,128)}, u32[]{:S(2)}) copy-start(f32[24,768]{1,0:T(8,128)} %shard_map.68) | copy-start | bytes 221188
Sparse Core Ops, SparseCore 0:
  11.3 114.7 all-gather.2
  157.4 145.1 reduce-scatter.3

commit v5 on v2

--- a/solution.py
+++ b/solution.py
@@ -12,6 +12,7 @@
 SEG = 8
 HOLD = 64
 OWN_SEG = 128
+N_Z = 8
 
 
 EPSILON = 1e-05
@@ -65,6 +66,112 @@
     out_ref[...] = total
 
 
+def ring_pass(n, left, right, chunk_of, land, recv_buf, send_buf, recv_sems, send_sems, free_sem):
+    mesh_kind = pl.DeviceIdType.MESH
+    for step in range(n):
+        slot, prev = step % 2, (step + 1) % 2
+        if step == 0:
+            source = chunk_of(step)
+        else:
+            pltpu.make_async_remote_copy(
+                src_ref=send_buf.at[prev],
+                dst_ref=recv_buf.at[prev],
+                send_sem=send_sems.at[prev],
+                recv_sem=recv_sems.at[prev],
+                device_id=left,
+                device_id_type=mesh_kind,
+            ).wait_recv()
+            target = land if step == n - 1 else send_buf.at[slot]
+            target[...] = recv_buf[prev] + chunk_of(step)[...]
+            if step <= n - 3:
+                pl.semaphore_signal(free_sem, inc=1, device_id=left, device_id_type=mesh_kind)
+            source = send_buf.at[slot]
+        if step < n - 1:
+            if step >= 2:
+                pl.semaphore_wait(free_sem, 1)
+            copy = pltpu.make_async_remote_copy(
+                src_ref=source,
+                dst_ref=recv_buf.at[slot],
+                send_sem=send_sems.at[slot],
+                recv_sem=recv_sems.at[slot],
+                device_id=right,
+                device_id_type=mesh_kind,
+            )
+            copy.start()
+            copy.wait_send()
+
+
+def fsdp_sum_kernel(n_z, n_y, part_ref, out_ref, xbuf, zrecv, zsend, ztot, yrecv, ysend, sems0, dsems, free_sems):
+    me = lax.axis_index("fsdp")
+    site = lax.axis_index("site")
+    core = lax.rem(me, 2)
+    chip = me // 2
+    zc, yc = chip // n_y, lax.rem(chip, n_y)
+    sibling = me + 1 - 2 * core
+
+    def device(z, y):
+        return (site, 2 * (lax.rem(z + n_z, n_z) * n_y + lax.rem(y + n_y, n_y)) + core)
+
+    mesh_kind = pl.DeviceIdType.MESH
+    z_left, z_right = device(zc - 1, yc), device(zc + 1, yc)
+    y_left, y_right = device(zc, yc - 1), device(zc, yc + 1)
+    barrier = pltpu.get_barrier_semaphore()
+    for peer in ((site, sibling), z_left, z_right, y_left, y_right):
+        pl.semaphore_signal(barrier, inc=1, device_id=peer, device_id_type=mesh_kind)
+    pl.semaphore_wait(barrier, 5)
+    swap = pltpu.make_async_remote_copy(
+        src_ref=part_ref.at[1 - core],
+        dst_ref=xbuf,
+        send_sem=sems0.at[0],
+        recv_sem=sems0.at[1],
+        device_id=(site, sibling),
+        device_id_type=mesh_kind,
+    )
+    swap.start()
+    swap.wait()
+
+    def add_own(index, carry):
+        xbuf[index] = xbuf[index] + part_ref[core, index]
+        return carry
+
+    lax.fori_loop(0, n_z * n_y, add_own, 0)
+
+    def z_chunk(step):
+        column = lax.rem(zc - 1 - step + 2 * n_z, n_z)
+        return xbuf.at[pl.ds(column * n_y, n_y)]
+
+    ring_pass(n_z, z_left, z_right, z_chunk, ztot, zrecv, zsend, dsems.at[0], dsems.at[1], free_sems.at[0])
+
+    def y_chunk(step):
+        return ztot.at[lax.rem(yc - 1 - step + 2 * n_y, n_y)]
+
+    ring_pass(n_y, y_left, y_right, y_chunk, out_ref, yrecv, ysend, dsems.at[2], dsems.at[3], free_sems.at[1])
+
+
+def fsdp_sum(part, n_z):
+    n_chip = part.shape[1]
+    n_y = n_chip // n_z
+    block = part.shape[2:]
+    return pl.pallas_call(
+        functools.partial(fsdp_sum_kernel, n_z, n_y),
+        out_shape=jax.ShapeDtypeStruct(block, part.dtype),
+        in_specs=[pl.BlockSpec(memory_space=pltpu.VMEM)],
+        out_specs=pl.BlockSpec(memory_space=pltpu.VMEM),
+        scratch_shapes=[
+            pltpu.VMEM((n_chip,) + block, part.dtype),
+            pltpu.VMEM((2, n_y) + block, part.dtype),
+            pltpu.VMEM((2, n_y) + block, part.dtype),
+            pltpu.VMEM((n_y,) + block, part.dtype),
+            pltpu.VMEM((2,) + block, part.dtype),
+            pltpu.VMEM((2,) + block, part.dtype),
+            pltpu.SemaphoreType.DMA((2,)),
+            pltpu.SemaphoreType.DMA((4, 2)),
+            pltpu.SemaphoreType.REGULAR((2,)),
+        ],
+        compiler_params=pltpu.CompilerParams(collective_id=1, has_side_effects=True),
+    )(part)
+
+
 def site_sum(part):
     n_site = lax.axis_size("site")
     return pl.pallas_call(
@@ -97,6 +204,15 @@
     taps_n, chans = stem_weight.shape[0], stem_weight.shape[1]
     joined = jnp.concatenate([proj_weight, stem_weight.reshape(taps_n * chans, D)], 0)
     gathered = lax.all_gather(joined, "fsdp", axis=0, tiled=False)
+    rows_out = D // group_size
+    partial = jnp.einsum(
+        "rckj,rd->kcjd",
+        normed_bf.reshape(normed_bf.shape[0], group_size // 2, 2, rows_out),
+        cotangent,
+        preferred_element_type=jnp.float32,
+    )
+    shard_sum = fsdp_sum(partial, N_Z)
+    shard_sum, gathered = lax.optimization_barrier((shard_sum, gathered))
     full_weight = gathered[:, :rows_w].reshape(group_size * rows_w, D)
     stem_gathered = gathered[:, rows_w:].reshape(group_size, taps_n, chans, D)
     proj_back = lax.dot_general(
@@ -159,16 +275,6 @@
         .reshape(2 * OWN_SEG * SEG, tap_terms.shape[2])
         .astype(jnp.bfloat16)
     )
-    partial = lax.dot_general(
-        normed_bf, cotangent, (((0,), (0,)), ((), ())), preferred_element_type=jnp.float32
-    )
-    partial, gathered = lax.optimization_barrier((partial, gathered))
-    shard_sum = lax.psum_scatter(
-        partial,
-        "fsdp",
-        scatter_dimension=0,
-        tiled=True,
-    )
     shard_sum = site_sum(shard_sum)
     weight_grad = shard_sum / math.sqrt(lax.axis_size("site") * group_size * HOLD * SEG)
     return (stem_rows[None], weight_grad)

time: 282 us -> 307 us (1.089)
  Pallas kernels: 10.5 us -> 163 us
  waiting for transfers between devices: 190 us -> 55.2 us
  starting transfers between devices: 8.19 us -> 11.4 us
    pallas_call x0 -> x1, Pallas kernels: none -> 150 us  [fsdp_sum(): pl.pallas_call(functools.partial(fsdp_sum_kernel, n_z, n_y), out_shape=ja...]
    all_gather x1, waiting for transfers between devices: 79 us -> 0.02 us  [body(): gathered = lax.all_gather(joined, 'fsdp', axis=0, tiled=False)]
    unnamed x3 -> x1, waiting for transfers between devices: 35.1 us -> 0.02 us
    all_to_all x1, waiting for transfers between devices: 75.5 us -> 55.2 us  [body(): lax.all_to_all(send_rows.reshape(group_size, capacity, SEG, D), 'fsdp', s...]
    all_to_all x1, starting transfers between devices: 8.11 us -> 11.4 us  [body(): lax.all_to_all(send_rows.reshape(group_size, capacity, SEG, D), 'fsdp', s...]
  transfers between devices with their start and end apart: 3 -> 2, of which waited for: 3 -> 1; matrix products, arithmetic and copies ran while one was open for 19% -> 7% of each run, Pallas kernels for 0% -> 53%
where the time goes in v5:
time: 307 us; the launch traced here: 306 us
  Pallas kernels  163 us (53%)
  waiting for transfers between devices  55.2 us (18%)
  other arithmetic  22.5 us (7%)
  matrix products  21.2 us (7%)
  local copies, waits for them, and re-layouts  18.5 us (6%)
  between operations  14.2 us (5%)
  starting transfers between devices  11.4 us (4%)
    pallas_call x1, Pallas kernels, fsdp_sum(): pl.pallas_call(functools.partial(fsdp_sum_kernel, n_z, n_y), out_shape=ja...  150 us
    all_to_all x1, waiting for transfers between devices, body(): lax.all_to_all(send_rows.reshape(group_size, capacity, SEG, D), 'fsdp', s...  55.2 us
    pallas_call x1, Pallas kernels, site_sum(): pl.pallas_call(functools.partial(site_sum_kernel, n_site), out_shape=jax....  12.9 us
    all_to_all x1, starting transfers between devices, body(): lax.all_to_all(send_rows.reshape(group_size, capacity, SEG, D), 'fsdp', s...  11.4 us
    dot_general x1, matrix products, stem_taps(): jnp.einsum('rd,fkcd->krfc', frames, stem_gathered, preferred_element_type...  8.7 us
    dot_general x1, matrix products, body(): jnp.einsum('rckj,rd->kcjd', normed_bf.reshape(normed_bf.shape[0], group_s...  8.16 us
  transfers between devices with their start and end apart: 2, of which 1 were waited for; matrix products, arithmetic and copies ran while one was open for 7% of the time, Pallas kernels for 53%

profile of v5, /device:TPU:24, one launch (start us, length us, event | category | flops | bytes accessed | tf_op | source)
XLA Modules:
  0.0 306.2 jit_solution(9689508397397654513)
XLA Ops:
  7.2 0.0 copy-start
  7.2 0.0 all-gather.3.cloned.1.call-start
  7.2 1.7 pad_maximum_fusion.1
  8.9 0.0 all-gather.3.cloned.1.call-update
  9.0 1.7 convert_reduce_fusion
  10.7 2.0 fusion.15
  12.6 0.0 copy-done
  12.6 0.4 fusion.4
  13.1 1.6 copy.15
  14.6 8.2 %convolution_bitcast_fusion.part_ref = f32[2,32,24,1536]{3,2,1,0:T(8,128)} fusion(bf16[1,512,1536]{2,1,0:T(8,128)(2,1)} %param.6, bf16[512,32,2,24]{0,3,2,1:T(8,128)(2,1)} %bitcast.105), kind=kOutput, calls=%fused_computation.2 | convolution fusion | flops 2415919104 | bytes 12582912 | tf_op jit(solution)/shard_map/rckj,rd->kcjd/dot_general | solution.py:208
  22.8 0.0 copy-start.2
  22.8 150.2 %shard_map.68.part_ref = f32[24,1536]{1,0:T(8,128)} custom-call(f32[2,32,24,1536]{3,2,1,0:T(8,128)} %convolution_bitcast_fusion.part_ref), custom_call_target="tpu_custom_call" | custom-call | tf_op jit(solution)/shard_map/pallas_call | solution.py:155
  173.1 0.0 copy-done.2
  173.1 0.1 copy.17
  173.2 0.1 reduce-window.8
  173.3 0.1 reduce.2
  173.4 0.7 fusion.45
  174.0 0.2 convert_reduce_fusion.3
  174.2 0.2 convert_reduce_fusion.2
  174.4 0.1 select_reduce_fusion
  174.5 0.1 reduce_sum.104
  174.7 0.1 fusion.39
  174.8 0.2 broadcast_in_dim.86
  175.0 0.0 all-gather.3.cloned.1.call-done
  175.0 0.0 copy-start.1
  175.0 2.8 slice.25
  177.8 0.0 copy-done.1
  177.8 4.4 %fusion.10 = (f32[512]{0:T(512)S(1)}, f32[1536,512]{0,1:T(8,128)}) fusion(bf16[1,512,1536]{2,1,0:T(8,128)(2,1)S(1)} %copy-done, f32[512]{0:T(512)S(1)} %add_rsqrt_fusion, f32[512]{0:T(512)S(1)} %broadcast_multiply_fusion.3, bf16[1536,1536]{1,0:T(8,128)(2,1)S(1)} %bitcast.102, bf16[1,512,1536]{2,1,0:T(8,128)(2,1)S(1)} %copy-done.1), kind=kOutput, calls=%fused_computation.16 | convolution fusion | flops 2419850752 | bytes 11016192 | tf_op jit(solution)/shard_map/dot_general | solution.py:218
  182.2 2.1 reduce_sum.105
  184.3 3.4 %fusion.28 = bf16[64,8,1536]{2,1,0:T(8,128)(2,1)S(1)} fusion(bf16[1,512,1536]{2,1,0:T(8,128)(2,1)S(1)} %copy-done, f32[1536,512]{0,1:T(8,128)} %get-tuple-element.9, bf16[1,512,1536]{2,1,0:T(8,128)(2,1)} %param.6, f32[512]{0:T(512)S(1)} %get-tuple-element.10, f32[512]{0:T(512)S(1)} %get-tuple-element.11, f32[512]{0:T(512)S(1)} %add_rsqrt_fusion, ...), kind=kLoop, calls=%fused_computation.36 | loop fusion | flops 7864320 | bytes 7872512 | tf_op jit(solution)/shard_map/reshape | solution.py:256
  187.8 2.4 gather_fusion
  190.2 3.3 %select_select_fusion = bf16[64,2,8,1536]{3,2,1,0:T(8,128)(2,1)} fusion(bf16[64,2,8,1536]{3,2,1,0:T(8,128)(2,1)} %bitcast.101, pred[64,2]{1,0:T(8,128)(4,1)S(1)} %compare_and_fusion, pred[64,2]{1,0:T(8,128)(4,1)S(1)} %broadcast_in_dim.86), kind=kLoop, calls=%fused_computation.26 | loop fusion | flops 3145728 | bytes 6291712 | tf_op jit(solution)/shard_map/jit(_where)/select_n | solution.py:258
  193.5 11.4 %all-to-all-start = ((bf16[64,2,8,1536]{3,2,1,0:T(8,128)(2,1)}), bf16[64,2,8,1536]{3,2,1,0:T(8,128)(2,1)S(1)}, u32[]{:S(2)}, u32[]{:S(2)}) async-start(bf16[64,2,8,1536]{3,2,1,0:T(8,128)(2,1)} %select_select_fusion), calls=%async_computation | async-start | bytes 6291456 | tf_op jit(solution)/shard_map/all_to_all | solution.py:259
  204.8 0.7 iota_compare_fusion.3
  205.5 0.7 and_select_fusion.4
  206.1 0.2 convert_reduce_fusion.1
  206.3 1.3 fusion.52
  207.6 1.3 compare_and_fusion.1
  209.0 12.9 %shard_map.69 = f32[24,1536]{1,0:T(8,128)} custom-call(f32[24,1536]{1,0:T(8,128)} %shard_map.68.part_ref), custom_call_target="tpu_custom_call" | custom-call | tf_op jit(solution)/shard_map/pallas_call | solution.py:177
  221.8 1.6 broadcast_multiply_fusion
  223.4 55.2 %all-to-all-done = bf16[64,2,8,1536]{3,2,1,0:T(8,128)(2,1)S(1)} async-done(((bf16[64,2,8,1536]{3,2,1,0:T(8,128)(2,1)}), bf16[64,2,8,1536]{3,2,1,0:T(8,128)(2,1)S(1)}, u32[]{:S(2)}, u32[]{:S(2)}) %all-to-all-start) | async-done | bytes 3145760 | tf_op jit(solution)/shard_map/all_to_all | solution.py:259
  278.6 2.4 gather_fusion.1
  281.0 8.7 %fusion.21 = f32[3,1024,64,8]{1,3,0,2:T(8,128)S(1)} fusion(bf16[128,8,1536]{2,1,0:T(8,128)(2,1)} %gather_fusion.1, pred[128]{0:T(512)(128)(4,1)S(1)} %compare_and_fusion.1, pred[128]{0:T(512)(128)(4,1)S(1)} %iota_compare_fusion.3, bf16[64,48,1536]{2,1,0:T(8,128)(2,1)} %bitcast.104), kind=kOutput, calls=%fused_computation.29 | convolution fusion | flops 4834983936 | bytes 14156032 | tf_op jit(solution)/shard_map/rd,fkcd->krfc/dot_general | solution.py:22
  289.7 0.6 slice_bitcast_fusion
  290.3 0.2 fusion.35
  290.4 0.5 fusion.36
  290.9 0.2 pad_maximum_fusion
  291.1 4.1 %copy.18 = bf16[1024,2,512]{2,1,0:T(2,128)(2,1)} copy(bf16[1024,2,512]{0,2,1:T(8,128)(2,1)S(1)} %pad_maximum_fusion) | data formatting | bytes 4194304 | tf_op jit(solution)/shard_map/stack | solution.py:274
  295.2 4.1 %convert_element_type.50 = bf16[1,2048,512]{2,1,0:T(8,128)(2,1)} reshape(bf16[1024,2,512]{2,1,0:T(2,128)(2,1)} %copy.18) | data formatting | bytes 4194304 | tf_op jit(solution)/shard_map/convert_element_type | solution.py:276
  (8 shorter events, 0.1 us)
Async XLA Ops:
  7.2 5.5 %copy-start = (bf16[1,512,1536]{2,1,0:T(8,128)(2,1)S(1)}, bf16[1,512,1536]{2,1,0:T(8,128)(2,1)}, u32[]{:S(2)}) copy-start(bf16[1,512,1536]{2,1,0:T(8,128)(2,1)} %param.5) | copy-start | bytes 4718596
  7.2 167.8 %all-gather.3.cloned.1.call-start = ((), (), s32[]{:S(2)}) async-start(), calls=%async_computation.1 | async-start | bytes 9584640 | tf_op jit(solution)/shard_map/all_gather | solution.py:206
  22.8 150.3 %copy-start.2 = (s32[1,64]{1,0:T(1,128)S(1)}, s32[1,64]{1,0:T(1,128)}, u32[]{:S(2)}) copy-start(s32[1,64]{1,0:T(1,128)} %param.9) | copy-start | bytes 772
  175.0 2.8 copy-start.1
  193.5 85.1 %all-to-all-start = ((bf16[64,2,8,1536]{3,2,1,0:T(8,128)(2,1)}), bf16[64,2,8,1536]{3,2,1,0:T(8,128)(2,1)S(1)}, u32[]{:S(2)}, u32[]{:S(2)}) async-start(bf16[64,2,8,1536]{3,2,1,0:T(8,128)(2,1)} %select_select_fusion), calls=%async_computation | async-start | bytes 6291456 | tf_op jit(solution)/shard_map/all_to_all | solution.py:259
Sparse Core Ops, SparseCore 0:
  11.3 99.1 all-gather.2

commit v6 on v5

--- a/solution.py
+++ b/solution.py
@@ -66,13 +66,15 @@
     out_ref[...] = total
 
 
-def ring_pass(n, left, right, chunk_of, land, recv_buf, send_buf, recv_sems, send_sems, free_sem):
+def ring_pass(n, lanes):
     mesh_kind = pl.DeviceIdType.MESH
     for step in range(n):
         slot, prev = step % 2, (step + 1) % 2
-        if step == 0:
-            source = chunk_of(step)
-        else:
+        sources = []
+        for left, right, chunk_of, land, recv_buf, send_buf, recv_sems, send_sems, free_sem in lanes:
+            if step == 0:
+                sources.append(chunk_of(step))
+                continue
             pltpu.make_async_remote_copy(
                 src_ref=send_buf.at[prev],
                 dst_ref=recv_buf.at[prev],
@@ -85,8 +87,12 @@
             target[...] = recv_buf[prev] + chunk_of(step)[...]
             if step <= n - 3:
                 pl.semaphore_signal(free_sem, inc=1, device_id=left, device_id_type=mesh_kind)
-            source = send_buf.at[slot]
-        if step < n - 1:
+            sources.append(send_buf.at[slot])
+        if step == n - 1:
+            break
+        copies = []
+        for lane, source in zip(lanes, sources):
+            left, right, chunk_of, land, recv_buf, send_buf, recv_sems, send_sems, free_sem = lane
             if step >= 2:
                 pl.semaphore_wait(free_sem, 1)
             copy = pltpu.make_async_remote_copy(
@@ -98,6 +104,8 @@
                 device_id_type=mesh_kind,
             )
             copy.start()
+            copies.append(copy)
+        for copy in copies:
             copy.wait_send()
 
 
@@ -113,12 +121,11 @@
         return (site, 2 * (lax.rem(z + n_z, n_z) * n_y + lax.rem(y + n_y, n_y)) + core)
 
     mesh_kind = pl.DeviceIdType.MESH
-    z_left, z_right = device(zc - 1, yc), device(zc + 1, yc)
-    y_left, y_right = device(zc, yc - 1), device(zc, yc + 1)
     barrier = pltpu.get_barrier_semaphore()
-    for peer in ((site, sibling), z_left, z_right, y_left, y_right):
+    peers = ((site, sibling), device(zc - 1, yc), device(zc + 1, yc), device(zc, yc - 1), device(zc, yc + 1))
+    for peer in peers:
         pl.semaphore_signal(barrier, inc=1, device_id=peer, device_id_type=mesh_kind)
-    pl.semaphore_wait(barrier, 5)
+    pl.semaphore_wait(barrier, len(peers))
     swap = pltpu.make_async_remote_copy(
         src_ref=part_ref.at[1 - core],
         dst_ref=xbuf,
@@ -136,22 +143,33 @@
 
     lax.fori_loop(0, n_z * n_y, add_own, 0)
 
-    def z_chunk(step):
-        column = lax.rem(zc - 1 - step + 2 * n_z, n_z)
-        return xbuf.at[pl.ds(column * n_y, n_y)]
-
-    ring_pass(n_z, z_left, z_right, z_chunk, ztot, zrecv, zsend, dsems.at[0], dsems.at[1], free_sems.at[0])
-
-    def y_chunk(step):
-        return ztot.at[lax.rem(yc - 1 - step + 2 * n_y, n_y)]
-
-    ring_pass(n_y, y_left, y_right, y_chunk, out_ref, yrecv, ysend, dsems.at[2], dsems.at[3], free_sems.at[1])
+    z_lanes, y_lanes = [], []
+    for lane, way in enumerate((1, -1)):
+
+        def z_chunk(step, lane=lane, way=way):
+            column = lax.rem(zc - way * (1 + step) + 2 * n_z, n_z)
+            return xbuf.at[pl.ds(column * n_y, n_y), lane]
+
+        def y_chunk(step, lane=lane, way=way):
+            return ztot.at[lax.rem(yc - way * (1 + step) + 2 * n_y, n_y), lane]
+
+        z_lanes.append((
+            device(zc - way, yc), device(zc + way, yc), z_chunk, ztot.at[:, lane],
+            zrecv.at[lane], zsend.at[lane], dsems.at[0, lane, 0], dsems.at[0, lane, 1], free_sems.at[0, lane],
+        ))
+        y_lanes.append((
+            device(zc, yc - way), device(zc, yc + way), y_chunk, out_ref.at[lane],
+            yrecv.at[lane], ysend.at[lane], dsems.at[1, lane, 0], dsems.at[1, lane, 1], free_sems.at[1, lane],
+        ))
+    ring_pass(n_z, z_lanes)
+    ring_pass(n_y, y_lanes)
 
 
 def fsdp_sum(part, n_z):
     n_chip = part.shape[1]
     n_y = n_chip // n_z
     block = part.shape[2:]
+    lane_block = part.shape[3:]
     return pl.pallas_call(
         functools.partial(fsdp_sum_kernel, n_z, n_y),
         out_shape=jax.ShapeDtypeStruct(block, part.dtype),
@@ -159,14 +177,14 @@
         out_specs=pl.BlockSpec(memory_space=pltpu.VMEM),
         scratch_shapes=[
             pltpu.VMEM((n_chip,) + block, part.dtype),
-            pltpu.VMEM((2, n_y) + block, part.dtype),
-            pltpu.VMEM((2, n_y) + block, part.dtype),
+            pltpu.VMEM((2, 2, n_y) + lane_block, part.dtype),
+            pltpu.VMEM((2, 2, n_y) + lane_block, part.dtype),
             pltpu.VMEM((n_y,) + block, part.dtype),
-            pltpu.VMEM((2,) + block, part.dtype),
-            pltpu.VMEM((2,) + block, part.dtype),
+            pltpu.VMEM((2, 2) + lane_block, part.dtype),
+            pltpu.VMEM((2, 2) + lane_block, part.dtype),
             pltpu.SemaphoreType.DMA((2,)),
-            pltpu.SemaphoreType.DMA((4, 2)),
-            pltpu.SemaphoreType.REGULAR((2,)),
+            pltpu.SemaphoreType.DMA((2, 2, 2, 2)),
+            pltpu.SemaphoreType.REGULAR((2, 2)),
         ],
         compiler_params=pltpu.CompilerParams(collective_id=1, has_side_effects=True),
     )(part)
@@ -206,12 +224,12 @@
     gathered = lax.all_gather(joined, "fsdp", axis=0, tiled=False)
     rows_out = D // group_size
     partial = jnp.einsum(
-        "rckj,rd->kcjd",
+        "rckj,rhd->kchjd",
         normed_bf.reshape(normed_bf.shape[0], group_size // 2, 2, rows_out),
-        cotangent,
+        cotangent.reshape(cotangent.shape[0], 2, D // 2),
         preferred_element_type=jnp.float32,
     )
-    shard_sum = fsdp_sum(partial, N_Z)
+    shard_sum = fsdp_sum(partial, N_Z).transpose(1, 0, 2).reshape(rows_out, D)
     shard_sum, gathered = lax.optimization_barrier((shard_sum, gathered))
     full_weight = gathered[:, :rows_w].reshape(group_size * rows_w, D)
     stem_gathered = gathered[:, rows_w:].reshape(group_size, taps_n, chans, D)

time: 307 us -> 265 us (0.86)
  Pallas kernels: 163 us -> 120 us
  local copies, waits for them, and re-layouts: 18.5 us -> 24.8 us
  starting transfers between devices: 11.4 us -> 7.53 us
    pallas_call x1, Pallas kernels: 150 us -> 106 us  [fsdp_sum(): pl.pallas_call(functools.partial(fsdp_sum_kernel, n_z, n_y), out_shape=ja...]
    another operation x1 -> x2, local copies, waits for them, and re-layouts: 0.1 us -> 4.81 us  [the longest x1 4.71 us: body(): cotangent.reshape(cotangent.shape[0], 2, D // 2)]
    all_to_all x1, starting transfers between devices: 11.4 us -> 7.5 us  [body(): lax.all_to_all(send_rows.reshape(group_size, capacity, SEG, D), 'fsdp', s...]
  transfers between devices with their start and end apart: 2 -> 2, of which waited for: 1 -> 1; matrix products, arithmetic and copies ran while one was open for 7% -> 10% of each run, Pallas kernels for 53% -> 46%
where the time goes in v6:
time: 265 us; the launch traced here: 263 us
  Pallas kernels  120 us (45%)
  waiting for transfers between devices  53.9 us (20%)
  local copies, waits for them, and re-layouts  24.8 us (9%)
  other arithmetic  22.5 us (8%)
  matrix products  19.6 us (7%)
  between operations  14.2 us (5%)
  starting transfers between devices  7.53 us (3%)
    pallas_call x1, Pallas kernels, fsdp_sum(): pl.pallas_call(functools.partial(fsdp_sum_kernel, n_z, n_y), out_shape=ja...  106 us
    all_to_all x1, waiting for transfers between devices, body(): lax.all_to_all(send_rows.reshape(group_size, capacity, SEG, D), 'fsdp', s...  53.8 us
    pallas_call x1, Pallas kernels, site_sum(): pl.pallas_call(functools.partial(site_sum_kernel, n_site), out_shape=jax....  14.2 us
    dot_general x1, matrix products, stem_taps(): jnp.einsum('rd,fkcd->krfc', frames, stem_gathered, preferred_element_type...  8.7 us
    all_to_all x1, starting transfers between devices, body(): lax.all_to_all(send_rows.reshape(group_size, capacity, SEG, D), 'fsdp', s...  7.5 us
    dot_general x1, matrix products, body(): jnp.einsum('rckj,rhd->kchjd', normed_bf.reshape(normed_bf.shape[0], group...  6.51 us
  transfers between devices with their start and end apart: 2, of which 1 were waited for; matrix products, arithmetic and copies ran while one was open for 10% of the time, Pallas kernels for 46%

profile of v6, /device:TPU:24, one launch (start us, length us, event | category | flops | bytes accessed | tf_op | source)
XLA Modules:
  0.0 262.8 jit_solution(11833486348008102995)
XLA Ops:
  7.2 0.0 copy-start
  7.2 0.0 all-gather.3.cloned.1.call-start
  7.2 1.7 pad_maximum_fusion.1
  8.9 0.0 all-gather.3.cloned.1.call-update
  9.0 1.7 convert_reduce_fusion
  10.7 2.0 fusion.15
  12.6 0.0 copy-done
  12.6 0.4 fusion.4
  13.1 1.6 copy.19
  14.6 0.0 copy-start.2
  14.6 4.7 %reshape_squeeze.3 = bf16[512,2,768]{2,1,0:T(2,128)(2,1)} reshape(bf16[1,512,1536]{2,1,0:T(8,128)(2,1)} %param.6) | data formatting | bytes 3145728 | tf_op jit(solution)/shard_map/reshape;squeeze | solution.py:229
  19.4 0.0 copy-done.2
  19.4 6.5 %convolution_bitcast_fusion.part_ref = f32[2,32,2,24,768]{4,3,2,1,0:T(8,128)} fusion(bf16[512,32,2,24,1]{0,3,2,1,4:T(8,128)(2,1)S(1)} %bitcast.109, bf16[512,2,768]{2,1,0:T(2,128)(2,1)} %reshape_squeeze.3), kind=kOutput, calls=%fused_computation.8 | convolution fusion | flops 2415919104 | bytes 12582912 | tf_op jit(solution)/shard_map/rckj,rhd->kchjd/dot_general | solution.py:226
  25.9 0.0 copy-start.3
  25.9 106.0 %shard_map.68 = f32[2,24,768]{2,1,0:T(8,128)} custom-call(f32[2,32,2,24,768]{4,3,2,1,0:T(8,128)} %convolution_bitcast_fusion.part_ref), custom_call_target="tpu_custom_call" | custom-call | tf_op jit(solution)/shard_map/pallas_call | solution.py:173
  131.9 1.6 copy.29
  133.5 0.0 copy-done.3
  133.5 0.1 copy.23
  133.6 0.1 reduce-window.8
  133.7 0.1 reduce.2
  133.8 0.7 fusion.46
  134.5 0.2 convert_reduce_fusion.3
  134.7 0.2 convert_reduce_fusion.2
  134.9 0.1 select_reduce_fusion
  135.0 0.1 reduce_sum.104
  135.1 0.1 fusion.40
  135.2 0.2 broadcast_in_dim.86
  135.4 0.0 all-gather.3.cloned.1.call-done
  135.4 0.0 copy-start.1
  135.5 2.8 %slice.25 = bf16[64,24,1536]{2,1,0:T(8,128)(2,1)S(1)} slice(bf16[64,48,1536]{2,1,0:T(8,128)(2,1)} %bitcast.107), slice={[0:64], [0:24], [0:1536]} | slice | bytes 9437184 | tf_op jit(solution)/shard_map/slice | solution.py:234
  138.2 0.0 copy-done.1
  138.3 4.4 %fusion.10 = (f32[512]{0:T(512)S(1)}, f32[1536,512]{0,1:T(8,128)}) fusion(bf16[1,512,1536]{2,1,0:T(8,128)(2,1)S(1)} %copy-done, f32[512]{0:T(512)S(1)} %add_rsqrt_fusion, f32[512]{0:T(512)S(1)} %broadcast_multiply_fusion.3, bf16[1536,1536]{1,0:T(8,128)(2,1)S(1)} %bitcast.106, bf16[1,512,1536]{2,1,0:T(8,128)(2,1)S(1)} %copy-done.1), kind=kOutput, calls=%fused_computation.16 | convolution fusion | flops 2419850752 | bytes 11016192 | tf_op jit(solution)/shard_map/dot_general | solution.py:236
  142.6 2.1 reduce_sum.105
  144.8 3.4 %fusion.28 = bf16[64,8,1536]{2,1,0:T(8,128)(2,1)S(1)} fusion(bf16[1,512,1536]{2,1,0:T(8,128)(2,1)S(1)} %copy-done, f32[1536,512]{0,1:T(8,128)} %get-tuple-element.9, bf16[1,512,1536]{2,1,0:T(8,128)(2,1)} %param.6, f32[512]{0:T(512)S(1)} %get-tuple-element.10, f32[512]{0:T(512)S(1)} %get-tuple-element.11, f32[512]{0:T(512)S(1)} %add_rsqrt_fusion, ...), kind=kLoop, calls=%fused_computation.36 | loop fusion | flops 7864320 | bytes 7872512 | tf_op jit(solution)/shard_map/reshape | solution.py:274
  148.2 2.4 gather_fusion
  150.6 3.3 %select_select_fusion = bf16[64,2,8,1536]{3,2,1,0:T(8,128)(2,1)} fusion(bf16[64,2,8,1536]{3,2,1,0:T(8,128)(2,1)} %bitcast.105, pred[64,2]{1,0:T(8,128)(4,1)S(1)} %compare_and_fusion, pred[64,2]{1,0:T(8,128)(4,1)S(1)} %broadcast_in_dim.86), kind=kLoop, calls=%fused_computation.26 | loop fusion | flops 3145728 | bytes 6291712 | tf_op jit(solution)/shard_map/jit(_where)/select_n | solution.py:276
  153.9 7.5 %all-to-all-start = ((bf16[64,2,8,1536]{3,2,1,0:T(8,128)(2,1)}), bf16[64,2,8,1536]{3,2,1,0:T(8,128)(2,1)S(1)}, u32[]{:S(2)}, u32[]{:S(2)}) async-start(bf16[64,2,8,1536]{3,2,1,0:T(8,128)(2,1)} %select_select_fusion), calls=%async_computation | async-start | bytes 6291456 | tf_op jit(solution)/shard_map/all_to_all | solution.py:277
  161.4 0.6 iota_compare_fusion.3
  162.1 0.7 and_select_fusion.4
  162.7 0.2 convert_reduce_fusion.1
  162.9 1.3 fusion.53
  164.2 1.3 compare_and_fusion.1
  165.5 14.2 %shard_map.69 = f32[24,1536]{1,0:T(8,128)} custom-call(f32[24,1536]{1,0:T(8,128)} %bitcast.110), custom_call_target="tpu_custom_call" | custom-call | tf_op jit(solution)/shard_map/pallas_call | solution.py:195
  179.8 1.6 broadcast_multiply_fusion
  181.3 53.8 %all-to-all-done = bf16[64,2,8,1536]{3,2,1,0:T(8,128)(2,1)S(1)} async-done(((bf16[64,2,8,1536]{3,2,1,0:T(8,128)(2,1)}), bf16[64,2,8,1536]{3,2,1,0:T(8,128)(2,1)S(1)}, u32[]{:S(2)}, u32[]{:S(2)}) %all-to-all-start) | async-done | bytes 3145760 | tf_op jit(solution)/shard_map/all_to_all | solution.py:277
  235.2 2.4 gather_fusion.1
  237.6 8.7 %fusion.21 = f32[3,1024,64,8]{1,3,0,2:T(8,128)S(1)} fusion(bf16[128,8,1536]{2,1,0:T(8,128)(2,1)} %gather_fusion.1, pred[128]{0:T(512)(128)(4,1)S(1)} %compare_and_fusion.1, pred[128]{0:T(512)(128)(4,1)S(1)} %iota_compare_fusion.3, bf16[64,48,1536]{2,1,0:T(8,128)(2,1)} %bitcast.108), kind=kOutput, calls=%fused_computation.29 | convolution fusion | flops 4834983936 | bytes 14156032 | tf_op jit(solution)/shard_map/rd,fkcd->krfc/dot_general | solution.py:22
  246.3 0.6 slice_bitcast_fusion
  246.9 0.2 fusion.36
  247.0 0.5 fusion.37
  247.5 0.2 pad_maximum_fusion
  247.7 4.1 %copy.24 = bf16[1024,2,512]{2,1,0:T(2,128)(2,1)} copy(bf16[1024,2,512]{0,2,1:T(8,128)(2,1)S(1)} %pad_maximum_fusion) | data formatting | bytes 4194304 | tf_op jit(solution)/shard_map/stack | solution.py:292
  251.8 4.1 %convert_element_type.50 = bf16[1,2048,512]{2,1,0:T(8,128)(2,1)} reshape(bf16[1024,2,512]{2,1,0:T(2,128)(2,1)} %copy.24) | data formatting | bytes 4194304 | tf_op jit(solution)/shard_map/convert_element_type | solution.py:294
  (8 shorter events, 0.1 us)
Async XLA Ops:
  7.2 5.5 %copy-start = (bf16[1,512,1536]{2,1,0:T(8,128)(2,1)S(1)}, bf16[1,512,1536]{2,1,0:T(8,128)(2,1)}, u32[]{:S(2)}) copy-start(bf16[1,512,1536]{2,1,0:T(8,128)(2,1)} %param.5) | copy-start | bytes 4718596
  7.2 128.3 %all-gather.3.cloned.1.call-start = ((), (), s32[]{:S(2)}) async-start(), calls=%async_computation.1 | async-start | bytes 9584640 | tf_op jit(solution)/shard_map/all_gather | solution.py:224
  14.6 4.7 %copy-start.2 = (bf16[1,512,1536]{1,2,0:T(8,128)(2,1)S(1)}, bf16[1,512,1536]{1,2,0:T(8,128)(2,1)}, u32[]{:S(2)}) copy-start(bf16[1,512,1536]{1,2,0:T(8,128)(2,1)} %copy.19) | copy-start | bytes 4718596
  25.9 107.6 %copy-start.3 = (s32[1,64]{1,0:T(1,128)S(1)}, s32[1,64]{1,0:T(1,128)}, u32[]{:S(2)}) copy-start(s32[1,64]{1,0:T(1,128)} %param.9) | copy-start | bytes 772
  135.4 2.8 %copy-start.1 = (bf16[1,512,1536]{2,1,0:T(8,128)(2,1)S(1)}, bf16[1,512,1536]{2,1,0:T(8,128)(2,1)}, u32[]{:S(2)}) copy-start(bf16[1,512,1536]{2,1,0:T(8,128)(2,1)} %param.6) | copy-start | bytes 4718596
  153.9 81.3 %all-to-all-start = ((bf16[64,2,8,1536]{3,2,1,0:T(8,128)(2,1)}), bf16[64,2,8,1536]{3,2,1,0:T(8,128)(2,1)S(1)}, u32[]{:S(2)}, u32[]{:S(2)}) async-start(bf16[64,2,8,1536]{3,2,1,0:T(8,128)(2,1)} %select_select_fusion), calls=%async_computation | async-start | bytes 6291456 | tf_op jit(solution)/shard_map/all_to_all | solution.py:277
Sparse Core Ops, SparseCore 0:
  11.3 98.9 all-gather.2

commit v7 on v6

--- a/solution.py
+++ b/solution.py
@@ -23,47 +23,6 @@
         "rd,fkcd->krfc", frames, stem_gathered, preferred_element_type=jnp.float32
     )
     return taps.reshape(taps.shape[0], taps.shape[1], -1)
-
-
-def site_sum_kernel(n_site, part_ref, out_ref, slots, send_sems, recv_sems):
-    me = lax.axis_index("site")
-    col = lax.axis_index("fsdp")
-    mesh_kind = pl.DeviceIdType.MESH
-    barrier = pltpu.get_barrier_semaphore()
-    for step in range(1, n_site):
-        peer = lax.rem(me + step, n_site)
-        pl.semaphore_signal(barrier, inc=1, device_id=(peer, col), device_id_type=mesh_kind)
-    pl.semaphore_wait(barrier, n_site - 1)
-    copies = []
-    for step in range(1, n_site):
-        peer = lax.rem(me + step, n_site)
-        copy = pltpu.make_async_remote_copy(
-            src_ref=part_ref,
-            dst_ref=slots.at[me],
-            send_sem=send_sems.at[step],
-            recv_sem=recv_sems.at[me],
-            device_id=(peer, col),
-            device_id_type=mesh_kind,
-        )
-        copy.start()
-        copies.append(copy)
-    slots[me] = part_ref[...]
-    for copy in copies:
-        copy.wait_send()
-    for step in range(1, n_site):
-        src = lax.rem(me + step, n_site)
-        pltpu.make_async_remote_copy(
-            src_ref=part_ref,
-            dst_ref=slots.at[src],
-            send_sem=send_sems.at[0],
-            recv_sem=recv_sems.at[src],
-            device_id=(src, col),
-            device_id_type=mesh_kind,
-        ).wait_recv()
-    total = slots[0]
-    for index in range(1, n_site):
-        total = total + slots[index]
-    out_ref[...] = total
 
 
 def ring_pass(n, lanes):
@@ -109,7 +68,7 @@
             copy.wait_send()
 
 
-def fsdp_sum_kernel(n_z, n_y, part_ref, out_ref, xbuf, zrecv, zsend, ztot, yrecv, ysend, sems0, dsems, free_sems):
+def z_sum_kernel(n_z, n_y, part_ref, ztot, xbuf, zrecv, zsend, sems0, dsems, free_sems):
     me = lax.axis_index("fsdp")
     site = lax.axis_index("site")
     core = lax.rem(me, 2)
@@ -117,12 +76,12 @@
     zc, yc = chip // n_y, lax.rem(chip, n_y)
     sibling = me + 1 - 2 * core
 
-    def device(z, y):
-        return (site, 2 * (lax.rem(z + n_z, n_z) * n_y + lax.rem(y + n_y, n_y)) + core)
+    def device(z):
+        return (site, 2 * (lax.rem(z + n_z, n_z) * n_y + yc) + core)
 
     mesh_kind = pl.DeviceIdType.MESH
     barrier = pltpu.get_barrier_semaphore()
-    peers = ((site, sibling), device(zc - 1, yc), device(zc + 1, yc), device(zc, yc - 1), device(zc, yc + 1))
+    peers = ((site, sibling), device(zc - 1), device(zc + 1))
     for peer in peers:
         pl.semaphore_signal(barrier, inc=1, device_id=peer, device_id_type=mesh_kind)
     pl.semaphore_wait(barrier, len(peers))
@@ -142,68 +101,125 @@
         return carry
 
     lax.fori_loop(0, n_z * n_y, add_own, 0)
-
-    z_lanes, y_lanes = [], []
+    lanes = []
     for lane, way in enumerate((1, -1)):
 
         def z_chunk(step, lane=lane, way=way):
             column = lax.rem(zc - way * (1 + step) + 2 * n_z, n_z)
             return xbuf.at[pl.ds(column * n_y, n_y), lane]
 
+        lanes.append((
+            device(zc - way), device(zc + way), z_chunk, ztot.at[:, lane],
+            zrecv.at[lane], zsend.at[lane], dsems.at[lane, 0], dsems.at[lane, 1], free_sems.at[lane],
+        ))
+    ring_pass(n_z, lanes)
+
+
+def y_site_kernel(n_y, n_site, ztot, out_ref, yrecv, ysend, ytot, slots, dsems, free_sems, site_send, site_recv):
+    me = lax.axis_index("fsdp")
+    site = lax.axis_index("site")
+    core = lax.rem(me, 2)
+    chip = me // 2
+    zc, yc = chip // n_y, lax.rem(chip, n_y)
+
+    def device(y):
+        return (site, 2 * (zc * n_y + lax.rem(y + n_y, n_y)) + core)
+
+    mesh_kind = pl.DeviceIdType.MESH
+    barrier = pltpu.get_barrier_semaphore()
+    peers = [device(yc - 1), device(yc + 1)]
+    for step in range(1, n_site):
+        peers.append((lax.rem(site + step, n_site), me))
+    for peer in peers:
+        pl.semaphore_signal(barrier, inc=1, device_id=peer, device_id_type=mesh_kind)
+    pl.semaphore_wait(barrier, len(peers))
+    lanes = []
+    for lane, way in enumerate((1, -1)):
+
         def y_chunk(step, lane=lane, way=way):
             return ztot.at[lax.rem(yc - way * (1 + step) + 2 * n_y, n_y), lane]
 
-        z_lanes.append((
-            device(zc - way, yc), device(zc + way, yc), z_chunk, ztot.at[:, lane],
-            zrecv.at[lane], zsend.at[lane], dsems.at[0, lane, 0], dsems.at[0, lane, 1], free_sems.at[0, lane],
+        lanes.append((
+            device(yc - way), device(yc + way), y_chunk, ytot.at[lane],
+            yrecv.at[lane], ysend.at[lane], dsems.at[lane, 0], dsems.at[lane, 1], free_sems.at[lane],
         ))
-        y_lanes.append((
-            device(zc, yc - way), device(zc, yc + way), y_chunk, out_ref.at[lane],
-            yrecv.at[lane], ysend.at[lane], dsems.at[1, lane, 0], dsems.at[1, lane, 1], free_sems.at[1, lane],
-        ))
-    ring_pass(n_z, z_lanes)
-    ring_pass(n_y, y_lanes)
-
-
-def fsdp_sum(part, n_z):
+    ring_pass(n_y, lanes)
+    copies = []
+    for step in range(1, n_site):
+        peer = lax.rem(site + step, n_site)
+        copy = pltpu.make_async_remote_copy(
+            src_ref=ytot,
+            dst_ref=slots.at[site],
+            send_sem=site_send.at[step],
+            recv_sem=site_recv.at[site],
+            device_id=(peer, me),
+            device_id_type=mesh_kind,
+        )
+        copy.start()
+        copies.append(copy)
+    slots[site] = ytot[...]
+    for copy in copies:
+        copy.wait_send()
+    for step in range(1, n_site):
+        src = lax.rem(site + step, n_site)
+        pltpu.make_async_remote_copy(
+            src_ref=ytot,
+            dst_ref=slots.at[src],
+            send_sem=site_send.at[0],
+            recv_sem=site_recv.at[src],
+            device_id=(src, me),
+            device_id_type=mesh_kind,
+        ).wait_recv()
+    total = slots[0]
+    for index in range(1, n_site):
+        total = total + slots[index]
+    out_ref[...] = total
+
+
+def z_sum(part, n_z):
     n_chip = part.shape[1]
     n_y = n_chip // n_z
     block = part.shape[2:]
     lane_block = part.shape[3:]
     return pl.pallas_call(
-        functools.partial(fsdp_sum_kernel, n_z, n_y),
-        out_shape=jax.ShapeDtypeStruct(block, part.dtype),
+        functools.partial(z_sum_kernel, n_z, n_y),
+        out_shape=jax.ShapeDtypeStruct((n_y,) + block, part.dtype),
         in_specs=[pl.BlockSpec(memory_space=pltpu.VMEM)],
         out_specs=pl.BlockSpec(memory_space=pltpu.VMEM),
         scratch_shapes=[
             pltpu.VMEM((n_chip,) + block, part.dtype),
             pltpu.VMEM((2, 2, n_y) + lane_block, part.dtype),
             pltpu.VMEM((2, 2, n_y) + lane_block, part.dtype),
-            pltpu.VMEM((n_y,) + block, part.dtype),
-            pltpu.VMEM((2, 2) + lane_block, part.dtype),
-            pltpu.VMEM((2, 2) + lane_block, part.dtype),
             pltpu.SemaphoreType.DMA((2,)),
-            pltpu.SemaphoreType.DMA((2, 2, 2, 2)),
-            pltpu.SemaphoreType.REGULAR((2, 2)),
+            pltpu.SemaphoreType.DMA((2, 2, 2)),
+            pltpu.SemaphoreType.REGULAR((2,)),
         ],
         compiler_params=pltpu.CompilerParams(collective_id=1, has_side_effects=True),
     )(part)
 
 
-def site_sum(part):
+def y_site_sum(ztot):
+    n_y = ztot.shape[0]
     n_site = lax.axis_size("site")
+    block = ztot.shape[1:]
+    lane_block = ztot.shape[2:]
     return pl.pallas_call(
-        functools.partial(site_sum_kernel, n_site),
-        out_shape=jax.ShapeDtypeStruct(part.shape, part.dtype),
+        functools.partial(y_site_kernel, n_y, n_site),
+        out_shape=jax.ShapeDtypeStruct(block, ztot.dtype),
         in_specs=[pl.BlockSpec(memory_space=pltpu.VMEM)],
         out_specs=pl.BlockSpec(memory_space=pltpu.VMEM),
         scratch_shapes=[
-            pltpu.VMEM((n_site,) + part.shape, part.dtype),
+            pltpu.VMEM((2, 2) + lane_block, ztot.dtype),
+            pltpu.VMEM((2, 2) + lane_block, ztot.dtype),
+            pltpu.VMEM(block, ztot.dtype),
+            pltpu.VMEM((n_site,) + block, ztot.dtype),
+            pltpu.SemaphoreType.DMA((2, 2, 2)),
+            pltpu.SemaphoreType.REGULAR((2,)),
             pltpu.SemaphoreType.DMA((n_site,)),
             pltpu.SemaphoreType.DMA((n_site,)),
         ],
-        compiler_params=pltpu.CompilerParams(collective_id=0, has_side_effects=True),
-    )(part)
+        compiler_params=pltpu.CompilerParams(collective_id=2, has_side_effects=True),
+    )(ztot)
 
 
 def body(held_input, held_cotangent, proj_weight, stem_weight, seg_counts):
@@ -229,8 +245,8 @@
         cotangent.reshape(cotangent.shape[0], 2, D // 2),
         preferred_element_type=jnp.float32,
     )
-    shard_sum = fsdp_sum(partial, N_Z).transpose(1, 0, 2).reshape(rows_out, D)
-    shard_sum, gathered = lax.optimization_barrier((shard_sum, gathered))
+    z_total = z_sum(partial, N_Z)
+    z_total, gathered = lax.optimization_barrier((z_total, gathered))
     full_weight = gathered[:, :rows_w].reshape(group_size * rows_w, D)
     stem_gathered = gathered[:, rows_w:].reshape(group_size, taps_n, chans, D)
     proj_back = lax.dot_general(
@@ -293,7 +309,7 @@
         .reshape(2 * OWN_SEG * SEG, tap_terms.shape[2])
         .astype(jnp.bfloat16)
     )
-    shard_sum = site_sum(shard_sum)
+    shard_sum = y_site_sum(z_total).transpose(1, 0, 2).reshape(rows_out, D)
     weight_grad = shard_sum / math.sqrt(lax.axis_size("site") * group_size * HOLD * SEG)
     return (stem_rows[None], weight_grad)
 

time: 265 us -> 250 us (0.943)
  waiting for transfers between devices: 53.9 us -> 37.4 us
  Pallas kernels: 120 us -> 124 us
    all_to_all x1, waiting for transfers between devices: 53.8 us -> 37.4 us  [body(): lax.all_to_all(send_rows.reshape(group_size, capacity, SEG, D), 'fsdp', s...]
    pallas_call x2, Pallas kernels: 120 us -> 124 us  [the longest x1 93.5 us: z_sum(): pl.pallas_call(functools.partial(z_sum_kernel, n_z, n_y), out_shape=jax.S...]
  transfers between devices with their start and end apart: 2 -> 2, of which waited for: 1 -> 1; matrix products, arithmetic and copies ran while one was open for 10% -> 10% of each run, Pallas kernels for 46% -> 50%
where the time goes in v7:
time: 250 us
  Pallas kernels  124 us (50%)
  waiting for transfers between devices  37.4 us (15%)
  local copies, waits for them, and re-layouts  23.9 us (10%)
  other arithmetic  21.8 us (9%)
  matrix products  19.6 us (8%)
  between operations  14.2 us (6%)
  starting transfers between devices  8.31 us (3%)
    pallas_call x1, Pallas kernels, z_sum(): pl.pallas_call(functools.partial(z_sum_kernel, n_z, n_y), out_shape=jax.S...  93.5 us
    all_to_all x1, waiting for transfers between devices, body(): lax.all_to_all(send_rows.reshape(group_size, capacity, SEG, D), 'fsdp', s...  37.4 us
    pallas_call x1, Pallas kernels, y_site_sum(): pl.pallas_call(functools.partial(y_site_kernel, n_y, n_site), out_shape=j...  30.7 us
    dot_general x1, matrix products, stem_taps(): jnp.einsum('rd,fkcd->krfc', frames, stem_gathered, preferred_element_type...  8.7 us
    all_to_all x1, starting transfers between devices, body(): lax.all_to_all(send_rows.reshape(group_size, capacity, SEG, D), 'fsdp', s...  8.27 us
    dot_general x1, matrix products, body(): jnp.einsum('rckj,rhd->kchjd', normed_bf.reshape(normed_bf.shape[0], group...  6.51 us
  transfers between devices with their start and end apart: 2, of which 1 were waited for; matrix products, arithmetic and copies ran while one was open for 10% of the time, Pallas kernels for 50%

profile of v7, /device:TPU:24, one launch (start us, length us, event | category | flops | bytes accessed | tf_op | source)
XLA Modules:
  0.0 249.5 jit_solution(591534917342243753)
XLA Ops:
  7.2 0.0 copy-start
  7.2 0.0 all-gather.3.cloned.1.call-start
  7.2 1.7 pad_maximum_fusion.1
  8.9 0.0 all-gather.3.cloned.1.call-update
  9.0 1.7 convert_reduce_fusion
  10.7 2.0 fusion.15
  12.6 0.0 copy-done
  12.6 0.4 fusion.4
  13.1 1.6 copy.18
  14.6 0.0 copy-start.2
  14.6 4.7 %reshape_squeeze.3 = bf16[512,2,768]{2,1,0:T(2,128)(2,1)} reshape(bf16[1,512,1536]{2,1,0:T(8,128)(2,1)} %param.6) | data formatting | bytes 3145728 | tf_op jit(solution)/shard_map/reshape;squeeze | solution.py:245
  19.4 0.0 copy-done.2
  19.4 6.5 %convolution_bitcast_fusion.part_ref = f32[2,32,2,24,768]{4,3,2,1,0:T(8,128)} fusion(bf16[512,32,2,24,1]{0,3,2,1,4:T(8,128)(2,1)S(1)} %bitcast.110, bf16[512,2,768]{2,1,0:T(2,128)(2,1)} %reshape_squeeze.3), kind=kOutput, calls=%fused_computation.8 | convolution fusion | flops 2415919104 | bytes 12582912 | tf_op jit(solution)/shard_map/rckj,rhd->kchjd/dot_general | solution.py:242
  25.9 0.0 copy-start.3
  25.9 93.5 %shard_map.68.ztot = f32[4,2,24,768]{3,2,1,0:T(8,128)} custom-call(f32[2,32,2,24,768]{4,3,2,1,0:T(8,128)} %convolution_bitcast_fusion.part_ref), custom_call_target="tpu_custom_call" | custom-call | tf_op jit(solution)/shard_map/pallas_call | solution.py:184
  119.4 0.0 copy-done.3
  119.4 0.1 copy.21
  119.5 0.1 reduce-window.8
  119.6 0.1 reduce.2
  119.7 0.7 fusion.46
  120.4 0.2 convert_reduce_fusion.3
  120.6 0.2 convert_reduce_fusion.2
  120.8 0.1 select_reduce_fusion
  120.9 0.1 reduce_sum.104
  121.0 0.1 fusion.40
  121.1 0.2 broadcast_in_dim.86
  121.3 0.0 all-gather.3.cloned.1.call-done
  121.3 0.0 copy-start.1
  121.3 2.8 %slice.25 = bf16[64,24,1536]{2,1,0:T(8,128)(2,1)S(1)} slice(bf16[64,48,1536]{2,1,0:T(8,128)(2,1)} %bitcast.108), slice={[0:64], [0:24], [0:1536]} | slice | bytes 9437184 | tf_op jit(solution)/shard_map/slice | solution.py:250
  124.1 0.0 copy-done.1
  124.2 4.4 %fusion.10 = (f32[512]{0:T(512)S(1)}, f32[1536,512]{0,1:T(8,128)}) fusion(bf16[1,512,1536]{2,1,0:T(8,128)(2,1)S(1)} %copy-done, f32[512]{0:T(512)S(1)} %add_rsqrt_fusion, f32[512]{0:T(512)S(1)} %broadcast_multiply_fusion.2, bf16[1536,1536]{1,0:T(8,128)(2,1)S(1)} %bitcast.107, bf16[1,512,1536]{2,1,0:T(8,128)(2,1)S(1)} %copy-done.1), kind=kOutput, calls=%fused_computation.16 | convolution fusion | flops 2419850752 | bytes 11016192 | tf_op jit(solution)/shard_map/dot_general | solution.py:252
  128.5 2.1 reduce_sum.105
  130.6 3.4 %fusion.28 = bf16[64,8,1536]{2,1,0:T(8,128)(2,1)S(1)} fusion(bf16[1,512,1536]{2,1,0:T(8,128)(2,1)S(1)} %copy-done, f32[1536,512]{0,1:T(8,128)} %get-tuple-element.9, bf16[1,512,1536]{2,1,0:T(8,128)(2,1)} %param.6, f32[512]{0:T(512)S(1)} %get-tuple-element.10, f32[512]{0:T(512)S(1)} %get-tuple-element.11, f32[512]{0:T(512)S(1)} %add_rsqrt_fusion, ...), kind=kLoop, calls=%fused_computation.36 | loop fusion | flops 7864320 | bytes 7872512 | tf_op jit(solution)/shard_map/reshape | solution.py:290
  134.1 2.4 gather_fusion
  136.5 3.3 %select_select_fusion = bf16[64,2,8,1536]{3,2,1,0:T(8,128)(2,1)} fusion(bf16[64,2,8,1536]{3,2,1,0:T(8,128)(2,1)} %bitcast.106, pred[64,2]{1,0:T(8,128)(4,1)S(1)} %compare_and_fusion, pred[64,2]{1,0:T(8,128)(4,1)S(1)} %broadcast_in_dim.86), kind=kLoop, calls=%fused_computation.26 | loop fusion | flops 3145728 | bytes 6291712 | tf_op jit(solution)/shard_map/jit(_where)/select_n | solution.py:292
  139.8 8.3 %all-to-all-start = ((bf16[64,2,8,1536]{3,2,1,0:T(8,128)(2,1)}), bf16[64,2,8,1536]{3,2,1,0:T(8,128)(2,1)S(1)}, u32[]{:S(2)}, u32[]{:S(2)}) async-start(bf16[64,2,8,1536]{3,2,1,0:T(8,128)(2,1)} %select_select_fusion), calls=%async_computation | async-start | bytes 6291456 | tf_op jit(solution)/shard_map/all_to_all | solution.py:293
  148.1 0.7 iota_compare_fusion.3
  148.8 0.7 and_select_fusion.4
  149.4 0.2 convert_reduce_fusion.1
  149.6 1.3 fusion.53
  150.9 1.3 compare_and_fusion.1
  152.2 30.7 %shard_map.69 = f32[2,24,768]{2,1,0:T(8,128)} custom-call(f32[4,2,24,768]{3,2,1,0:T(8,128)} %shard_map.68.ztot), custom_call_target="tpu_custom_call" | custom-call | tf_op jit(solution)/shard_map/pallas_call | solution.py:206
  182.9 0.9 multiply_bitcast_fusion
  183.8 0.7 copy.28
  184.5 37.4 %all-to-all-done = bf16[64,2,8,1536]{3,2,1,0:T(8,128)(2,1)S(1)} async-done(((bf16[64,2,8,1536]{3,2,1,0:T(8,128)(2,1)}), bf16[64,2,8,1536]{3,2,1,0:T(8,128)(2,1)S(1)}, u32[]{:S(2)}, u32[]{:S(2)}) %all-to-all-start) | async-done | bytes 3145760 | tf_op jit(solution)/shard_map/all_to_all | solution.py:293
  221.9 2.4 gather_fusion.1
  224.3 8.7 %fusion.21 = f32[3,1024,64,8]{1,3,0,2:T(8,128)S(1)} fusion(bf16[128,8,1536]{2,1,0:T(8,128)(2,1)} %gather_fusion.1, pred[128]{0:T(512)(128)(4,1)S(1)} %compare_and_fusion.1, pred[128]{0:T(512)(128)(4,1)S(1)} %iota_compare_fusion.3, bf16[64,48,1536]{2,1,0:T(8,128)(2,1)} %bitcast.109), kind=kOutput, calls=%fused_computation.29 | convolution fusion | flops 4834983936 | bytes 14156032 | tf_op jit(solution)/shard_map/rd,fkcd->krfc/dot_general | solution.py:22
  233.0 0.6 slice_bitcast_fusion
  233.6 0.2 fusion.36
  233.8 0.5 fusion.37
  234.3 0.2 pad_maximum_fusion
  234.5 4.1 %copy.22 = bf16[1024,2,512]{2,1,0:T(2,128)(2,1)} copy(bf16[1024,2,512]{0,2,1:T(8,128)(2,1)S(1)} %pad_maximum_fusion) | data formatting | bytes 4194304 | tf_op jit(solution)/shard_map/stack | solution.py:308
  238.6 4.1 %convert_element_type.50 = bf16[1,2048,512]{2,1,0:T(8,128)(2,1)} reshape(bf16[1024,2,512]{2,1,0:T(2,128)(2,1)} %copy.22) | data formatting | bytes 4194304 | tf_op jit(solution)/shard_map/convert_element_type | solution.py:310
  (8 shorter events, 0.1 us)
Async XLA Ops:
  7.2 5.5 %copy-start = (bf16[1,512,1536]{2,1,0:T(8,128)(2,1)S(1)}, bf16[1,512,1536]{2,1,0:T(8,128)(2,1)}, u32[]{:S(2)}) copy-start(bf16[1,512,1536]{2,1,0:T(8,128)(2,1)} %param.5) | copy-start | bytes 4718596
  7.2 114.2 %all-gather.3.cloned.1.call-start = ((), (), s32[]{:S(2)}) async-start(), calls=%async_computation.1 | async-start | bytes 9584640 | tf_op jit(solution)/shard_map/all_gather | solution.py:240
  14.6 4.7 %copy-start.2 = (bf16[1,512,1536]{1,2,0:T(8,128)(2,1)S(1)}, bf16[1,512,1536]{1,2,0:T(8,128)(2,1)}, u32[]{:S(2)}) copy-start(bf16[1,512,1536]{1,2,0:T(8,128)(2,1)} %copy.18) | copy-start | bytes 4718596
  25.9 93.5 %copy-start.3 = (s32[1,64]{1,0:T(1,128)S(1)}, s32[1,64]{1,0:T(1,128)}, u32[]{:S(2)}) copy-start(s32[1,64]{1,0:T(1,128)} %param.9) | copy-start | bytes 772
  121.3 2.8 %copy-start.1 = (bf16[1,512,1536]{2,1,0:T(8,128)(2,1)S(1)}, bf16[1,512,1536]{2,1,0:T(8,128)(2,1)}, u32[]{:S(2)}) copy-start(bf16[1,512,1536]{2,1,0:T(8,128)(2,1)} %param.6) | copy-start | bytes 4718596
  139.8 82.1 %all-to-all-start = ((bf16[64,2,8,1536]{3,2,1,0:T(8,128)(2,1)}), bf16[64,2,8,1536]{3,2,1,0:T(8,128)(2,1)S(1)}, u32[]{:S(2)}, u32[]{:S(2)}) async-start(bf16[64,2,8,1536]{3,2,1,0:T(8,128)(2,1)} %select_select_fusion), calls=%async_computation | async-start | bytes 6291456 | tf_op jit(solution)/shard_map/all_to_all | solution.py:293
Sparse Core Ops, SparseCore 0:
  11.3 98.9 all-gather.2

commit v8 on v7

--- a/solution.py
+++ b/solution.py
@@ -25,12 +25,15 @@
     return taps.reshape(taps.shape[0], taps.shape[1], -1)
 
 
-def ring_pass(n, lanes):
+def ring_pass(n, lanes, prepare=None):
     mesh_kind = pl.DeviceIdType.MESH
     for step in range(n):
         slot, prev = step % 2, (step + 1) % 2
         sources = []
-        for left, right, chunk_of, land, recv_buf, send_buf, recv_sems, send_sems, free_sem in lanes:
+        for lane_index, lane in enumerate(lanes):
+            left, right, chunk_of, land, recv_buf, send_buf, recv_sems, send_sems, free_sem = lane
+            if prepare is not None:
+                prepare(lane_index, step)
             if step == 0:
                 sources.append(chunk_of(step))
                 continue
@@ -68,7 +71,7 @@
             copy.wait_send()
 
 
-def z_sum_kernel(n_z, n_y, part_ref, ztot, xbuf, zrecv, zsend, sems0, dsems, free_sems):
+def z_sum_kernel(n_z, n_y, lo_ref, hi_ref, ztot, xbuf, zrecv, zsend, swap_sems, dsems, free_sems):
     me = lax.axis_index("fsdp")
     site = lax.axis_index("site")
     core = lax.rem(me, 2)
@@ -85,34 +88,46 @@
     for peer in peers:
         pl.semaphore_signal(barrier, inc=1, device_id=peer, device_id_type=mesh_kind)
     pl.semaphore_wait(barrier, len(peers))
-    swap = pltpu.make_async_remote_copy(
-        src_ref=part_ref.at[1 - core],
-        dst_ref=xbuf,
-        send_sem=sems0.at[0],
-        recv_sem=sems0.at[1],
-        device_id=(site, sibling),
-        device_id_type=mesh_kind,
-    )
-    swap.start()
-    swap.wait()
-
-    def add_own(index, carry):
-        xbuf[index] = xbuf[index] + part_ref[core, index]
-        return carry
-
-    lax.fori_loop(0, n_z * n_y, add_own, 0)
+    ways = (1, -1)
+    parts = (lo_ref, hi_ref)
+
+    def rows(lane, step):
+        column = lax.rem(zc - ways[lane] * (1 + step) + 2 * n_z, n_z)
+        return pl.ds(column * n_y, n_y)
+
+    def swap(lane, step):
+        return pltpu.make_async_remote_copy(
+            src_ref=parts[lane].at[1 - core, rows(lane, step)],
+            dst_ref=xbuf.at[rows(lane, step), lane],
+            send_sem=swap_sems.at[lane, step, 0],
+            recv_sem=swap_sems.at[lane, step, 1],
+            device_id=(site, sibling),
+            device_id_type=mesh_kind,
+        )
+
+    for step in range(n_z):
+        for lane in range(2):
+            swap(lane, step).start()
+
+    def prepare(lane, step):
+        swap(lane, step).wait_recv()
+        here = rows(lane, step)
+        xbuf[here, lane] = xbuf[here, lane] + parts[lane][core, here]
+
     lanes = []
-    for lane, way in enumerate((1, -1)):
-
-        def z_chunk(step, lane=lane, way=way):
-            column = lax.rem(zc - way * (1 + step) + 2 * n_z, n_z)
-            return xbuf.at[pl.ds(column * n_y, n_y), lane]
+    for lane, way in enumerate(ways):
+
+        def z_chunk(step, lane=lane):
+            return xbuf.at[rows(lane, step), lane]
 
         lanes.append((
             device(zc - way), device(zc + way), z_chunk, ztot.at[:, lane],
             zrecv.at[lane], zsend.at[lane], dsems.at[lane, 0], dsems.at[lane, 1], free_sems.at[lane],
         ))
-    ring_pass(n_z, lanes)
+    ring_pass(n_z, lanes, prepare)
+    for step in range(n_z):
+        for lane in range(2):
+            swap(lane, step).wait_send()
 
 
 def y_site_kernel(n_y, n_site, ztot, out_ref, yrecv, ysend, ytot, slots, dsems, free_sems, site_send, site_recv):
@@ -176,26 +191,26 @@
     out_ref[...] = total
 
 
-def z_sum(part, n_z):
-    n_chip = part.shape[1]
+def z_sum(lo, hi, n_z):
+    n_chip = lo.shape[1]
     n_y = n_chip // n_z
-    block = part.shape[2:]
-    lane_block = part.shape[3:]
+    lane_block = lo.shape[2:]
+    block = (2,) + lane_block
     return pl.pallas_call(
         functools.partial(z_sum_kernel, n_z, n_y),
-        out_shape=jax.ShapeDtypeStruct((n_y,) + block, part.dtype),
-        in_specs=[pl.BlockSpec(memory_space=pltpu.VMEM)],
+        out_shape=jax.ShapeDtypeStruct((n_y,) + block, lo.dtype),
+        in_specs=[pl.BlockSpec(memory_space=pltpu.VMEM)] * 2,
         out_specs=pl.BlockSpec(memory_space=pltpu.VMEM),
         scratch_shapes=[
-            pltpu.VMEM((n_chip,) + block, part.dtype),
-            pltpu.VMEM((2, 2, n_y) + lane_block, part.dtype),
-            pltpu.VMEM((2, 2, n_y) + lane_block, part.dtype),
-            pltpu.SemaphoreType.DMA((2,)),
+            pltpu.VMEM((n_chip,) + block, lo.dtype),
+            pltpu.VMEM((2, 2, n_y) + lane_block, lo.dtype),
+            pltpu.VMEM((2, 2, n_y) + lane_block, lo.dtype),
+            pltpu.SemaphoreType.DMA((2, n_z, 2)),
             pltpu.SemaphoreType.DMA((2, 2, 2)),
             pltpu.SemaphoreType.REGULAR((2,)),
         ],
         compiler_params=pltpu.CompilerParams(collective_id=1, has_side_effects=True),
-    )(part)
+    )(lo, hi)
 
 
 def y_site_sum(ztot):
@@ -239,13 +254,13 @@
     joined = jnp.concatenate([proj_weight, stem_weight.reshape(taps_n * chans, D)], 0)
     gathered = lax.all_gather(joined, "fsdp", axis=0, tiled=False)
     rows_out = D // group_size
-    partial = jnp.einsum(
-        "rckj,rhd->kchjd",
-        normed_bf.reshape(normed_bf.shape[0], group_size // 2, 2, rows_out),
-        cotangent.reshape(cotangent.shape[0], 2, D // 2),
-        preferred_element_type=jnp.float32,
-    )
-    z_total = z_sum(partial, N_Z)
+    by_core = normed_bf.reshape(normed_bf.shape[0], group_size // 2, 2, rows_out)
+    halves = [
+        jnp.einsum("rckj,rd->kcjd", by_core, cotangent[:, part * (D // 2):(part + 1) * (D // 2)],
+                   preferred_element_type=jnp.float32)
+        for part in range(2)
+    ]
+    z_total = z_sum(halves[0], halves[1], N_Z)
     z_total, gathered = lax.optimization_barrier((z_total, gathered))
     full_weight = gathered[:, :rows_w].reshape(group_size * rows_w, D)
     stem_gathered = gathered[:, rows_w:].reshape(group_size, taps_n, chans, D)

time: 250 us -> 245 us (0.980)
  local copies, waits for them, and re-layouts: 23.9 us -> 19.8 us
    another operation x2 -> x1, local copies, waits for them, and re-layouts: 4.81 us -> 0.1 us  [the longest x1 4.71 us: body(): cotangent.reshape(cotangent.shape[0], 2, D // 2)]
    dot_general x1 -> x2, matrix products: 6.51 us -> 7.23 us  [body(): jnp.einsum('rckj,rd->kcjd', by_core, cotangent[:, part * (D // 2):(part +...]
  transfers between devices with their start and end apart: 2 -> 2, of which waited for: 1 -> 1; matrix products, arithmetic and copies ran while one was open for 10% -> 8% of each run, Pallas kernels for 50% -> 50%
where the time goes in v8:
time: 245 us; the launch traced here: 244 us
  Pallas kernels  123 us (50%)
  waiting for transfers between devices  37.1 us (15%)
  other arithmetic  21.6 us (9%)
  matrix products  20.3 us (8%)
  local copies, waits for them, and re-layouts  19.8 us (8%)
  between operations  14.3 us (6%)
  starting transfers between devices  7.62 us (3%)
    pallas_call x1, Pallas kernels, z_sum(): pl.pallas_call(functools.partial(z_sum_kernel, n_z, n_y), out_shape=jax.S...  92.1 us
    all_to_all x1, waiting for transfers between devices, body(): lax.all_to_all(send_rows.reshape(group_size, capacity, SEG, D), 'fsdp', s...  37 us
    pallas_call x1, Pallas kernels, y_site_sum(): pl.pallas_call(functools.partial(y_site_kernel, n_y, n_site), out_shape=j...  30.8 us
    dot_general x1, matrix products, stem_taps(): jnp.einsum('rd,fkcd->krfc', frames, stem_gathered, preferred_element_type...  8.7 us
    all_to_all x1, starting transfers between devices, body(): lax.all_to_all(send_rows.reshape(group_size, capacity, SEG, D), 'fsdp', s...  7.58 us
    dot_general x2, matrix products, body(): jnp.einsum('rckj,rd->kcjd', by_core, cotangent[:, part * (D // 2):(part +...  7.23 us
  transfers between devices with their start and end apart: 2, of which 1 were waited for; matrix products, arithmetic and copies ran while one was open for 8% of the time, Pallas kernels for 50%

profile of v8, /device:TPU:24, one launch (start us, length us, event | category | flops | bytes accessed | tf_op | source)
XLA Modules:
  0.0 243.5 jit_solution(13611919639679856961)
XLA Ops:
  7.2 0.0 copy-start.3
  7.2 0.0 all-gather.3.cloned.1.call-start
  7.2 1.6 pad_maximum_fusion.1
  8.8 0.0 all-gather.3.cloned.1.call-update
  8.8 1.7 copy.18
  10.6 0.0 copy-done.3
  10.6 0.1 copy.21
  10.7 0.1 reduce-window.8
  10.8 0.1 reduce.2
  10.9 0.7 fusion.36
  11.6 0.2 convert_reduce_fusion.3
  11.8 0.2 convert_reduce_fusion.2
  12.0 0.1 select_reduce_fusion
  12.1 0.1 reduce_sum.104
  12.2 0.1 fusion.30
  12.3 0.2 broadcast_in_dim.86
  12.5 0.0 copy-start.1
  12.5 1.8 convert_reduce_fusion
  14.3 2.0 multiply_reduce_fusion
  16.3 0.0 copy-done.1
  16.3 3.6 %convolution_bitcast_fusion.hi_ref = f32[2,32,24,768]{3,2,1,0:T(8,128)} fusion(bf16[512,1536]{1,0:T(8,128)(2,1)S(1)} %bitcast.106, f32[512,32,2,24]{0,3,2,1:T(8,128)S(1)} %bitcast.102, f32[512]{0:T(512)S(1)} %add_rsqrt_fusion, f32[512]{0:T(512)S(1)} %broadcast_multiply_fusion.2), kind=kOutput, calls=%fused_computation.24 | convolution fusion | flops 1210318848 | bytes 8654848 | tf_op jit(solution)/shard_map/rckj,rd->kcjd/dot_general | solution.py:259
  19.9 3.7 %convolution_bitcast_fusion.1.lo_ref = f32[2,32,24,768]{3,2,1,0:T(8,128)} fusion(bf16[512,1536]{1,0:T(8,128)(2,1)S(1)} %bitcast.107, f32[512,32,2,24]{0,3,2,1:T(8,128)S(1)} %bitcast.103, f32[512]{0:T(512)S(1)} %add_rsqrt_fusion, f32[512]{0:T(512)S(1)} %broadcast_multiply_fusion.2), kind=kOutput, calls=%fused_computation.25 | convolution fusion | flops 1210318848 | bytes 8654848 | tf_op jit(solution)/shard_map/rckj,rd->kcjd/dot_general | solution.py:259
  23.5 92.1 %shard_map.68.ztot = f32[4,2,24,768]{3,2,1,0:T(8,128)} custom-call(f32[2,32,24,768]{3,2,1,0:T(8,128)} %convolution_bitcast_fusion.1.lo_ref, f32[2,32,24,768]{3,2,1,0:T(8,128)} %convolution_bitcast_fusion.hi_ref), custom_call_target="tpu_custom_call" | custom-call | tf_op jit(solution)/shard_map/pallas_call | solution.py:199
  115.6 0.0 all-gather.3.cloned.1.call-done
  115.7 0.0 copy-start
  115.7 0.0 copy-start.2
  115.7 2.8 %slice.33 = bf16[64,24,1536]{2,1,0:T(8,128)(2,1)S(1)} slice(bf16[64,48,1536]{2,1,0:T(8,128)(2,1)} %bitcast.109), slice={[0:64], [0:24], [0:1536]} | slice | bytes 9437184 | tf_op jit(solution)/shard_map/slice | solution.py:265
  118.5 0.0 copy-done
  118.5 0.5 copy-done.2
  119.0 4.4 %fusion.8 = (f32[512]{0:T(512)S(1)}, f32[1536,512]{0,1:T(8,128)}) fusion(bf16[1,512,1536]{2,1,0:T(8,128)(2,1)S(1)} %copy-done, f32[512]{0:T(512)S(1)} %add_rsqrt_fusion, f32[512]{0:T(512)S(1)} %broadcast_multiply_fusion.2, bf16[1536,1536]{1,0:T(8,128)(2,1)S(1)} %bitcast.108, bf16[1,512,1536]{2,1,0:T(8,128)(2,1)S(1)} %copy-done.2), kind=kOutput, calls=%fused_computation.12 | convolution fusion | flops 2419850752 | bytes 11016192 | tf_op jit(solution)/shard_map/dot_general | solution.py:267
  123.3 2.1 reduce_sum.105
  125.5 3.4 %fusion.21 = bf16[64,8,1536]{2,1,0:T(8,128)(2,1)S(1)} fusion(bf16[1,512,1536]{2,1,0:T(8,128)(2,1)S(1)} %copy-done, f32[1536,512]{0,1:T(8,128)} %get-tuple-element.9, f32[512]{0:T(512)S(1)} %get-tuple-element.10, f32[512]{0:T(512)S(1)} %get-tuple-element.11, f32[512]{0:T(512)S(1)} %add_rsqrt_fusion, f32[512]{0:T(512)S(1)} %broadcast_multiply_fusion.2, ...), kind=kLoop, calls=%fused_computation.32 | loop fusion | flops 7864320 | bytes 7872512 | tf_op jit(solution)/shard_map/reshape | solution.py:305
  128.9 2.4 gather_fusion
  131.3 3.3 %select_select_fusion = bf16[64,2,8,1536]{3,2,1,0:T(8,128)(2,1)} fusion(bf16[64,2,8,1536]{3,2,1,0:T(8,128)(2,1)} %bitcast.105, pred[64,2]{1,0:T(8,128)(4,1)S(1)} %compare_and_fusion, pred[64,2]{1,0:T(8,128)(4,1)S(1)} %broadcast_in_dim.86), kind=kLoop, calls=%fused_computation.16 | loop fusion | flops 3145728 | bytes 6291712 | tf_op jit(solution)/shard_map/jit(_where)/select_n | solution.py:307
  134.6 7.6 %all-to-all-start = ((bf16[64,2,8,1536]{3,2,1,0:T(8,128)(2,1)}), bf16[64,2,8,1536]{3,2,1,0:T(8,128)(2,1)S(1)}, u32[]{:S(2)}, u32[]{:S(2)}) async-start(bf16[64,2,8,1536]{3,2,1,0:T(8,128)(2,1)} %select_select_fusion), calls=%async_computation | async-start | bytes 6291456 | tf_op jit(solution)/shard_map/all_to_all | solution.py:308
  142.2 0.7 iota_compare_fusion.3
  142.9 0.7 and_select_fusion.4
  143.6 0.2 convert_reduce_fusion.1
  143.8 1.4 fusion.43
  145.1 1.4 compare_and_fusion.1
  146.5 30.8 %shard_map.69 = f32[2,24,768]{2,1,0:T(8,128)} custom-call(f32[4,2,24,768]{3,2,1,0:T(8,128)} %shard_map.68.ztot), custom_call_target="tpu_custom_call" | custom-call | tf_op jit(solution)/shard_map/pallas_call | solution.py:221
  177.3 0.9 multiply_bitcast_fusion
  178.3 0.7 copy.25
  178.9 37.0 %all-to-all-done = bf16[64,2,8,1536]{3,2,1,0:T(8,128)(2,1)S(1)} async-done(((bf16[64,2,8,1536]{3,2,1,0:T(8,128)(2,1)}), bf16[64,2,8,1536]{3,2,1,0:T(8,128)(2,1)S(1)}, u32[]{:S(2)}, u32[]{:S(2)}) %all-to-all-start) | async-done | bytes 3145760 | tf_op jit(solution)/shard_map/all_to_all | solution.py:308
  216.0 2.4 gather_fusion.1
  218.3 8.7 %fusion.14 = f32[3,1024,64,8]{1,3,0,2:T(8,128)S(1)} fusion(bf16[128,8,1536]{2,1,0:T(8,128)(2,1)} %gather_fusion.1, pred[128]{0:T(512)(128)(4,1)S(1)} %compare_and_fusion.1, pred[128]{0:T(512)(128)(4,1)S(1)} %iota_compare_fusion.3, bf16[64,48,1536]{2,1,0:T(8,128)(2,1)} %bitcast.110), kind=kOutput, calls=%fused_computation.23 | convolution fusion | flops 4834983936 | bytes 14156032 | tf_op jit(solution)/shard_map/rd,fkcd->krfc/dot_general | solution.py:22
  227.0 0.6 slice_bitcast_fusion
  227.7 0.2 fusion.26
  227.8 0.5 fusion.27
  228.3 0.2 pad_maximum_fusion
  228.5 4.1 %copy.22 = bf16[1024,2,512]{2,1,0:T(2,128)(2,1)} copy(bf16[1024,2,512]{0,2,1:T(8,128)(2,1)S(1)} %pad_maximum_fusion) | data formatting | bytes 4194304 | tf_op jit(solution)/shard_map/stack | solution.py:323
  232.6 4.1 %convert_element_type.52 = bf16[1,2048,512]{2,1,0:T(8,128)(2,1)} reshape(bf16[1024,2,512]{2,1,0:T(2,128)(2,1)} %copy.22) | data formatting | bytes 4194304 | tf_op jit(solution)/shard_map/convert_element_type | solution.py:325
  (8 shorter events, 0.1 us)
Async XLA Ops:
  7.2 3.4 %copy-start.3 = (s32[1,64]{1,0:T(1,128)S(1)}, s32[1,64]{1,0:T(1,128)}, u32[]{:S(2)}) copy-start(s32[1,64]{1,0:T(1,128)} %param.9) | copy-start | bytes 772
  7.2 108.5 %all-gather.3.cloned.1.call-start = ((), (), s32[]{:S(2)}) async-start(), calls=%async_computation.1 | async-start | bytes 9584640 | tf_op jit(solution)/shard_map/all_gather | solution.py:255
  12.5 3.8 %copy-start.1 = (bf16[1,512,1536]{2,1,0:T(8,128)(2,1)S(1)}, bf16[1,512,1536]{2,1,0:T(8,128)(2,1)}, u32[]{:S(2)}) copy-start(bf16[1,512,1536]{2,1,0:T(8,128)(2,1)} %param.6) | copy-start | bytes 4718596
  115.7 2.8 %copy-start = (bf16[1,512,1536]{2,1,0:T(8,128)(2,1)S(1)}, bf16[1,512,1536]{2,1,0:T(8,128)(2,1)}, u32[]{:S(2)}) copy-start(bf16[1,512,1536]{2,1,0:T(8,128)(2,1)} %param.5) | copy-start | bytes 4718596
  115.7 3.3 %copy-start.2 = (bf16[1,512,1536]{2,1,0:T(8,128)(2,1)S(1)}, bf16[1,512,1536]{2,1,0:T(8,128)(2,1)}, u32[]{:S(2)}) copy-start(bf16[1,512,1536]{2,1,0:T(8,128)(2,1)} %param.6) | copy-start | bytes 4718596
  134.6 81.3 %all-to-all-start = ((bf16[64,2,8,1536]{3,2,1,0:T(8,128)(2,1)}), bf16[64,2,8,1536]{3,2,1,0:T(8,128)(2,1)S(1)}, u32[]{:S(2)}, u32[]{:S(2)}) async-start(bf16[64,2,8,1536]{3,2,1,0:T(8,128)(2,1)} %select_select_fusion), calls=%async_computation | async-start | bytes 6291456 | tf_op jit(solution)/shard_map/all_to_all | solution.py:308
Sparse Core Ops, SparseCore 0:
  11.3 98.4 all-gather.2

commit v9 on v8

--- a/solution.py
+++ b/solution.py
@@ -19,14 +19,14 @@
 
 
 def stem_taps(frames, stem_gathered):
-    taps = jnp.einsum(
-        "rd,fkcd->krfc", frames, stem_gathered, preferred_element_type=jnp.float32
-    )
-    return taps.reshape(taps.shape[0], taps.shape[1], -1)
+    devices, taps_n, chans = stem_gathered.shape[:3]
+    weights = stem_gathered.transpose(1, 0, 2, 3).reshape(taps_n, devices * chans, D)
+    return jnp.einsum("rd,kcd->krc", frames, weights, preferred_element_type=jnp.float32)
 
 
 def ring_pass(n, lanes, prepare=None):
     mesh_kind = pl.DeviceIdType.MESH
+    pending = [[None, None] for _ in lanes]
     for step in range(n):
         slot, prev = step % 2, (step + 1) % 2
         sources = []
@@ -45,6 +45,9 @@
                 device_id=left,
                 device_id_type=mesh_kind,
             ).wait_recv()
+            if step < n - 1 and pending[lane_index][slot] is not None:
+                pending[lane_index][slot].wait_send()
+                pending[lane_index][slot] = None
             target = land if step == n - 1 else send_buf.at[slot]
             target[...] = recv_buf[prev] + chunk_of(step)[...]
             if step <= n - 3:
@@ -52,8 +55,7 @@
             sources.append(send_buf.at[slot])
         if step == n - 1:
             break
-        copies = []
-        for lane, source in zip(lanes, sources):
+        for lane_index, (lane, source) in enumerate(zip(lanes, sources)):
             left, right, chunk_of, land, recv_buf, send_buf, recv_sems, send_sems, free_sem = lane
             if step >= 2:
                 pl.semaphore_wait(free_sem, 1)
@@ -66,9 +68,11 @@
                 device_id_type=mesh_kind,
             )
             copy.start()
-            copies.append(copy)
-        for copy in copies:
-            copy.wait_send()
+            pending[lane_index][slot] = copy
+    for slots in pending:
+        for copy in slots:
+            if copy is not None:
+                copy.wait_send()
 
 
 def z_sum_kernel(n_z, n_y, lo_ref, hi_ref, ztot, xbuf, zrecv, zsend, swap_sems, dsems, free_sems):

time: 245 us -> 248 us (1.012)
  local copies, waits for them, and re-layouts: 19.8 us -> 23.4 us
    transpose x0 -> x1, local copies, waits for them, and re-layouts: none -> 6.77 us  [stem_taps(): stem_gathered.transpose(1, 0, 2, 3).reshape(taps_n, devices * chans, D)]
    slice x1 -> x0, local copies, waits for them, and re-layouts: 2.81 us -> none  [body(): full_weight = gathered[:, :rows_w].reshape(group_size * rows_w, D)]
where the time goes in v9:
time: 248 us; the launch traced here: 247 us
  Pallas kernels  123 us (50%)
  waiting for transfers between devices  36.9 us (15%)
  local copies, waits for them, and re-layouts  23.4 us (9%)
  other arithmetic  21.6 us (9%)
  matrix products  20.3 us (8%)
  between operations  14.3 us (6%)
  starting transfers between devices  8.23 us (3%)
    pallas_call x1, Pallas kernels, z_sum(): pl.pallas_call(functools.partial(z_sum_kernel, n_z, n_y), out_shape=jax.S...  91.6 us
    all_to_all x1, waiting for transfers between devices, body(): lax.all_to_all(send_rows.reshape(group_size, capacity, SEG, D), 'fsdp', s...  36.8 us
    pallas_call x1, Pallas kernels, y_site_sum(): pl.pallas_call(functools.partial(y_site_kernel, n_y, n_site), out_shape=j...  31 us
    dot_general x1, matrix products, stem_taps(): jnp.einsum('rd,kcd->krc', frames, weights, preferred_element_type=jnp.flo...  8.66 us
    all_to_all x1, starting transfers between devices, body(): lax.all_to_all(send_rows.reshape(group_size, capacity, SEG, D), 'fsdp', s...  8.19 us
    dot_general x2, matrix products, body(): jnp.einsum('rckj,rd->kcjd', by_core, cotangent[:, part * (D // 2):(part +...  7.23 us
    transpose x1, local copies, waits for them, and re-layouts, stem_taps(): stem_gathered.transpose(1, 0, 2, 3).reshape(taps_n, devices * chans, D)  6.77 us
  transfers between devices with their start and end apart: 2, of which 1 were waited for; matrix products, arithmetic and copies ran while one was open for 8% of the time, Pallas kernels for 50%

profile of v9, /device:TPU:24, one launch (start us, length us, event | category | flops | bytes accessed | tf_op | source)
XLA Modules:
  0.0 247.3 jit_solution(2321710410337422617)
XLA Ops:
  7.2 0.0 copy-start.3
  7.2 0.0 all-gather.3.cloned.1.call-start
  7.2 1.6 pad_maximum_fusion.1
  8.8 0.0 all-gather.3.cloned.1.call-update
  8.8 1.7 copy.18
  10.6 0.0 copy-done.3
  10.6 0.1 copy.22
  10.7 0.1 reduce-window.8
  10.8 0.1 reduce.2
  10.9 0.7 fusion.36
  11.6 0.2 convert_reduce_fusion.3
  11.8 0.2 convert_reduce_fusion.2
  12.0 0.1 select_reduce_fusion
  12.1 0.1 reduce_sum.104
  12.2 0.1 fusion.30
  12.3 0.2 broadcast_in_dim.86
  12.5 0.0 copy-start.1
  12.5 1.8 convert_reduce_fusion
  14.3 2.0 multiply_reduce_fusion
  16.3 0.0 copy-done.1
  16.3 3.6 %convolution_bitcast_fusion.hi_ref = f32[2,32,24,768]{3,2,1,0:T(8,128)} fusion(bf16[512,1536]{1,0:T(8,128)(2,1)S(1)} %bitcast.109, f32[512,32,2,24]{0,3,2,1:T(8,128)S(1)} %bitcast.104, f32[512]{0:T(512)S(1)} %add_rsqrt_fusion, f32[512]{0:T(512)S(1)} %broadcast_multiply_fusion.2), kind=kOutput, calls=%fused_computation.25 | convolution fusion | flops 1210318848 | bytes 8654848 | tf_op jit(solution)/shard_map/rckj,rd->kcjd/dot_general | solution.py:263
  19.9 3.7 %convolution_bitcast_fusion.1.lo_ref = f32[2,32,24,768]{3,2,1,0:T(8,128)} fusion(bf16[512,1536]{1,0:T(8,128)(2,1)S(1)} %bitcast.110, f32[512,32,2,24]{0,3,2,1:T(8,128)S(1)} %bitcast.105, f32[512]{0:T(512)S(1)} %add_rsqrt_fusion, f32[512]{0:T(512)S(1)} %broadcast_multiply_fusion.2), kind=kOutput, calls=%fused_computation.26 | convolution fusion | flops 1210318848 | bytes 8654848 | tf_op jit(solution)/shard_map/rckj,rd->kcjd/dot_general | solution.py:263
  23.5 91.6 %shard_map.68.ztot = f32[4,2,24,768]{3,2,1,0:T(8,128)} custom-call(f32[2,32,24,768]{3,2,1,0:T(8,128)} %convolution_bitcast_fusion.1.lo_ref, f32[2,32,24,768]{3,2,1,0:T(8,128)} %convolution_bitcast_fusion.hi_ref), custom_call_target="tpu_custom_call" | custom-call | tf_op jit(solution)/shard_map/pallas_call | solution.py:203
  115.2 0.0 all-gather.3.cloned.1.call-done
  115.3 0.0 copy-start
  115.3 0.0 copy-start.2
  115.3 6.8 %slice_bitcast_fusion = (bf16[3,64,8,1536]{3,2,0,1:T(8,128)(2,1)}, bf16[64,24,1536]{2,1,0:T(8,128)(2,1)S(1)}) fusion(bf16[64,48,1536]{2,1,0:T(8,128)(2,1)} %bitcast.108), kind=kLoop, calls=%fused_computation.5 | loop fusion | bytes 18874368 | tf_op jit(solution)/shard_map/transpose | solution.py:23
  122.0 0.0 copy-done
  122.1 0.0 copy-done.2
  122.1 4.4 %fusion.8 = (f32[512]{0:T(512)S(1)}, f32[1536,512]{0,1:T(8,128)}) fusion(bf16[1,512,1536]{2,1,0:T(8,128)(2,1)S(1)} %copy-done, f32[512]{0:T(512)S(1)} %add_rsqrt_fusion, f32[512]{0:T(512)S(1)} %broadcast_multiply_fusion.2, bf16[1536,1536]{1,0:T(8,128)(2,1)S(1)} %bitcast.111, bf16[1,512,1536]{2,1,0:T(8,128)(2,1)S(1)} %copy-done.2), kind=kOutput, calls=%fused_computation.13 | convolution fusion | flops 2419850752 | bytes 11016192 | tf_op jit(solution)/shard_map/dot_general | solution.py:271
  126.4 2.1 reduce_sum.105
  128.6 3.4 %fusion.21 = bf16[64,8,1536]{2,1,0:T(8,128)(2,1)S(1)} fusion(bf16[1,512,1536]{2,1,0:T(8,128)(2,1)S(1)} %copy-done, f32[1536,512]{0,1:T(8,128)} %get-tuple-element.11, f32[512]{0:T(512)S(1)} %get-tuple-element.12, f32[512]{0:T(512)S(1)} %get-tuple-element.13, f32[512]{0:T(512)S(1)} %add_rsqrt_fusion, f32[512]{0:T(512)S(1)} %broadcast_multiply_fusion.2, ...), kind=kLoop, calls=%fused_computation.33 | loop fusion | flops 7864320 | bytes 7872512 | tf_op jit(solution)/shard_map/reshape | solution.py:309
  132.0 2.5 gather_fusion
  134.5 3.3 %select_select_fusion = bf16[64,2,8,1536]{3,2,1,0:T(8,128)(2,1)} fusion(bf16[64,2,8,1536]{3,2,1,0:T(8,128)(2,1)} %bitcast.107, pred[64,2]{1,0:T(8,128)(4,1)S(1)} %compare_and_fusion, pred[64,2]{1,0:T(8,128)(4,1)S(1)} %broadcast_in_dim.86), kind=kLoop, calls=%fused_computation.17 | loop fusion | flops 3145728 | bytes 6291712 | tf_op jit(solution)/shard_map/jit(_where)/select_n | solution.py:311
  137.8 8.2 %all-to-all-start = ((bf16[64,2,8,1536]{3,2,1,0:T(8,128)(2,1)}), bf16[64,2,8,1536]{3,2,1,0:T(8,128)(2,1)S(1)}, u32[]{:S(2)}, u32[]{:S(2)}) async-start(bf16[64,2,8,1536]{3,2,1,0:T(8,128)(2,1)} %select_select_fusion), calls=%async_computation | async-start | bytes 6291456 | tf_op jit(solution)/shard_map/all_to_all | solution.py:312
  146.0 0.7 iota_compare_fusion.3
  146.7 0.7 and_select_fusion.4
  147.4 0.2 convert_reduce_fusion.1
  147.5 1.4 fusion.43
  148.9 1.4 compare_and_fusion.1
  150.3 31.0 %shard_map.69 = f32[2,24,768]{2,1,0:T(8,128)} custom-call(f32[4,2,24,768]{3,2,1,0:T(8,128)} %shard_map.68.ztot), custom_call_target="tpu_custom_call" | custom-call | tf_op jit(solution)/shard_map/pallas_call | solution.py:225
  181.3 0.9 multiply_bitcast_fusion
  182.3 0.7 copy.25
  182.9 36.8 %all-to-all-done = bf16[64,2,8,1536]{3,2,1,0:T(8,128)(2,1)S(1)} async-done(((bf16[64,2,8,1536]{3,2,1,0:T(8,128)(2,1)}), bf16[64,2,8,1536]{3,2,1,0:T(8,128)(2,1)S(1)}, u32[]{:S(2)}, u32[]{:S(2)}) %all-to-all-start) | async-done | bytes 3145760 | tf_op jit(solution)/shard_map/all_to_all | solution.py:312
  219.8 2.4 gather_fusion.1
  222.2 8.7 %fusion.14 = f32[3,1024,512]{1,2,0:T(8,128)S(1)} fusion(bf16[128,8,1536]{2,1,0:T(8,128)(2,1)} %gather_fusion.1, pred[128]{0:T(512)(128)(4,1)S(1)} %compare_and_fusion.1, pred[128]{0:T(512)(128)(4,1)S(1)} %iota_compare_fusion.3, bf16[3,64,8,1536]{3,2,0,1:T(8,128)(2,1)} %get-tuple-element.8), kind=kOutput, calls=%fused_computation.24 | convolution fusion | flops 4834983936 | bytes 14156032 | tf_op jit(solution)/shard_map/rd,kcd->krc/dot_general | solution.py:24
  230.8 0.6 slice_bitcast_fusion.1
  231.4 0.2 fusion.26
  231.6 0.5 fusion.27
  232.1 0.2 pad_maximum_fusion
  232.3 4.1 %copy.23 = bf16[1024,2,512]{2,1,0:T(2,128)(2,1)} copy(bf16[1024,2,512]{0,2,1:T(8,128)(2,1)S(1)} %pad_maximum_fusion) | data formatting | bytes 4194304 | tf_op jit(solution)/shard_map/stack | solution.py:327
  236.4 4.1 %convert_element_type.52 = bf16[1,2048,512]{2,1,0:T(8,128)(2,1)} reshape(bf16[1024,2,512]{2,1,0:T(2,128)(2,1)} %copy.23) | data formatting | bytes 4194304 | tf_op jit(solution)/shard_map/convert_element_type | solution.py:329
  (8 shorter events, 0.1 us)
Async XLA Ops:
  7.2 3.4 %copy-start.3 = (s32[1,64]{1,0:T(1,128)S(1)}, s32[1,64]{1,0:T(1,128)}, u32[]{:S(2)}) copy-start(s32[1,64]{1,0:T(1,128)} %param.9) | copy-start | bytes 772
  7.2 108.1 %all-gather.3.cloned.1.call-start = ((), (), s32[]{:S(2)}) async-start(), calls=%async_computation.1 | async-start | bytes 9584640 | tf_op jit(solution)/shard_map/all_gather | solution.py:259
  12.5 3.8 %copy-start.1 = (bf16[1,512,1536]{2,1,0:T(8,128)(2,1)S(1)}, bf16[1,512,1536]{2,1,0:T(8,128)(2,1)}, u32[]{:S(2)}) copy-start(bf16[1,512,1536]{2,1,0:T(8,128)(2,1)} %param.6) | copy-start | bytes 4718596
  115.3 6.8 %copy-start = (bf16[1,512,1536]{2,1,0:T(8,128)(2,1)S(1)}, bf16[1,512,1536]{2,1,0:T(8,128)(2,1)}, u32[]{:S(2)}) copy-start(bf16[1,512,1536]{2,1,0:T(8,128)(2,1)} %param.5) | copy-start | bytes 4718596
  115.3 6.8 %copy-start.2 = (bf16[1,512,1536]{2,1,0:T(8,128)(2,1)S(1)}, bf16[1,512,1536]{2,1,0:T(8,128)(2,1)}, u32[]{:S(2)}) copy-start(bf16[1,512,1536]{2,1,0:T(8,128)(2,1)} %param.6) | copy-start | bytes 4718596
  137.8 82.0 %all-to-all-start = ((bf16[64,2,8,1536]{3,2,1,0:T(8,128)(2,1)}), bf16[64,2,8,1536]{3,2,1,0:T(8,128)(2,1)S(1)}, u32[]{:S(2)}, u32[]{:S(2)}) async-start(bf16[64,2,8,1536]{3,2,1,0:T(8,128)(2,1)} %select_select_fusion), calls=%async_computation | async-start | bytes 6291456 | tf_op jit(solution)/shard_map/all_to_all | solution.py:312
Sparse Core Ops, SparseCore 0:
  11.3 98.6 all-gather.2

commit v10 on v8

--- a/solution.py
+++ b/solution.py
@@ -13,6 +13,7 @@
 HOLD = 64
 OWN_SEG = 128
 N_Z = 8
+N_LANES = 4
 
 
 EPSILON = 1e-05
@@ -71,7 +72,9 @@
             copy.wait_send()
 
 
-def z_sum_kernel(n_z, n_y, lo_ref, hi_ref, ztot, xbuf, zrecv, zsend, swap_sems, dsems, free_sems):
+def z_sum_kernel(n_z, n_y, n_lanes, *refs):
+    parts = refs[:n_lanes]
+    ztot, xbuf, zrecv, zsend, swap_sems, dsems, free_sems = refs[n_lanes:]
     me = lax.axis_index("fsdp")
     site = lax.axis_index("site")
     core = lax.rem(me, 2)
@@ -88,8 +91,7 @@
     for peer in peers:
         pl.semaphore_signal(barrier, inc=1, device_id=peer, device_id_type=mesh_kind)
     pl.semaphore_wait(barrier, len(peers))
-    ways = (1, -1)
-    parts = (lo_ref, hi_ref)
+    ways = tuple(1 - 2 * (lane % 2) for lane in range(n_lanes))
 
     def rows(lane, step):
         column = lax.rem(zc - ways[lane] * (1 + step) + 2 * n_z, n_z)
@@ -106,7 +108,7 @@
         )
 
     for step in range(n_z):
-        for lane in range(2):
+        for lane in range(n_lanes):
             swap(lane, step).start()
 
     def prepare(lane, step):
@@ -126,7 +128,7 @@
         ))
     ring_pass(n_z, lanes, prepare)
     for step in range(n_z):
-        for lane in range(2):
+        for lane in range(n_lanes):
             swap(lane, step).wait_send()
 
 
@@ -149,7 +151,8 @@
         pl.semaphore_signal(barrier, inc=1, device_id=peer, device_id_type=mesh_kind)
     pl.semaphore_wait(barrier, len(peers))
     lanes = []
-    for lane, way in enumerate((1, -1)):
+    for lane in range(ztot.shape[1]):
+        way = 1 - 2 * (lane % 2)
 
         def y_chunk(step, lane=lane, way=way):
             return ztot.at[lax.rem(yc - way * (1 + step) + 2 * n_y, n_y), lane]
@@ -191,26 +194,28 @@
     out_ref[...] = total
 
 
-def z_sum(lo, hi, n_z):
-    n_chip = lo.shape[1]
+def z_sum(parts, n_z):
+    n_lanes = len(parts)
+    n_chip = parts[0].shape[1]
     n_y = n_chip // n_z
-    lane_block = lo.shape[2:]
-    block = (2,) + lane_block
+    lane_block = parts[0].shape[2:]
+    block = (n_lanes,) + lane_block
+    dtype = parts[0].dtype
     return pl.pallas_call(
-        functools.partial(z_sum_kernel, n_z, n_y),
-        out_shape=jax.ShapeDtypeStruct((n_y,) + block, lo.dtype),
-        in_specs=[pl.BlockSpec(memory_space=pltpu.VMEM)] * 2,
+        functools.partial(z_sum_kernel, n_z, n_y, n_lanes),
+        out_shape=jax.ShapeDtypeStruct((n_y,) + block, dtype),
+        in_specs=[pl.BlockSpec(memory_space=pltpu.VMEM)] * n_lanes,
         out_specs=pl.BlockSpec(memory_space=pltpu.VMEM),
         scratch_shapes=[
-            pltpu.VMEM((n_chip,) + block, lo.dtype),
-            pltpu.VMEM((2, 2, n_y) + lane_block, lo.dtype),
-            pltpu.VMEM((2, 2, n_y) + lane_block, lo.dtype),
-            pltpu.SemaphoreType.DMA((2, n_z, 2)),
-            pltpu.SemaphoreType.DMA((2, 2, 2)),
-            pltpu.SemaphoreType.REGULAR((2,)),
+            pltpu.VMEM((n_chip,) + block, dtype),
+            pltpu.VMEM((n_lanes, 2, n_y) + lane_block, dtype),
+            pltpu.VMEM((n_lanes, 2, n_y) + lane_block, dtype),
+            pltpu.SemaphoreType.DMA((n_lanes, n_z, 2)),
+            pltpu.SemaphoreType.DMA((n_lanes, 2, 2)),
+            pltpu.SemaphoreType.REGULAR((n_lanes,)),
         ],
         compiler_params=pltpu.CompilerParams(collective_id=1, has_side_effects=True),
-    )(lo, hi)
+    )(*parts)
 
 
 def y_site_sum(ztot):
@@ -218,18 +223,19 @@
     n_site = lax.axis_size("site")
     block = ztot.shape[1:]
     lane_block = ztot.shape[2:]
+    n_lanes = ztot.shape[1]
     return pl.pallas_call(
         functools.partial(y_site_kernel, n_y, n_site),
         out_shape=jax.ShapeDtypeStruct(block, ztot.dtype),
         in_specs=[pl.BlockSpec(memory_space=pltpu.VMEM)],
         out_specs=pl.BlockSpec(memory_space=pltpu.VMEM),
         scratch_shapes=[
-            pltpu.VMEM((2, 2) + lane_block, ztot.dtype),
-            pltpu.VMEM((2, 2) + lane_block, ztot.dtype),
+            pltpu.VMEM((n_lanes, 2) + lane_block, ztot.dtype),
+            pltpu.VMEM((n_lanes, 2) + lane_block, ztot.dtype),
             pltpu.VMEM(block, ztot.dtype),
             pltpu.VMEM((n_site,) + block, ztot.dtype),
-            pltpu.SemaphoreType.DMA((2, 2, 2)),
-            pltpu.SemaphoreType.REGULAR((2,)),
+            pltpu.SemaphoreType.DMA((n_lanes, 2, 2)),
+            pltpu.SemaphoreType.REGULAR((n_lanes,)),
             pltpu.SemaphoreType.DMA((n_site,)),
             pltpu.SemaphoreType.DMA((n_site,)),
         ],
@@ -255,12 +261,13 @@
     gathered = lax.all_gather(joined, "fsdp", axis=0, tiled=False)
     rows_out = D // group_size
     by_core = normed_bf.reshape(normed_bf.shape[0], group_size // 2, 2, rows_out)
-    halves = [
-        jnp.einsum("rckj,rd->kcjd", by_core, cotangent[:, part * (D // 2):(part + 1) * (D // 2)],
+    width = D // N_LANES
+    pieces = [
+        jnp.einsum("rckj,rd->kcjd", by_core, cotangent[:, part * width:(part + 1) * width],
                    preferred_element_type=jnp.float32)
-        for part in range(2)
+        for part in range(N_LANES)
     ]
-    z_total = z_sum(halves[0], halves[1], N_Z)
+    z_total = z_sum(pieces, N_Z)
     z_total, gathered = lax.optimization_barrier((z_total, gathered))
     full_weight = gathered[:, :rows_w].reshape(group_size * rows_w, D)
     stem_gathered = gathered[:, rows_w:].reshape(group_size, taps_n, chans, D)

time: 245 us -> 248 us (1.012)
  starting transfers between devices: 7.62 us -> 11 us
  matrix products: 20.3 us -> 22.8 us
    all_to_all x1, starting transfers between devices: 7.58 us -> 10.9 us  [body(): lax.all_to_all(send_rows.reshape(group_size, capacity, SEG, D), 'fsdp', s...]
    dot_general x2 -> x4, matrix products: 7.23 us -> 9.82 us  [body(): jnp.einsum('rckj,rd->kcjd', by_core, cotangent[:, part * width:(part + 1)...]
  transfers between devices with their start and end apart: 2 -> 2, of which waited for: 1 -> 1; matrix products, arithmetic and copies ran while one was open for 8% -> 9% of each run, Pallas kernels for 50% -> 49%
where the time goes in v10:
time: 248 us; the launch traced here: 247 us
  Pallas kernels  122 us (49%)
  waiting for transfers between devices  36.2 us (15%)
  matrix products  22.8 us (9%)
  local copies, waits for them, and re-layouts  21.6 us (9%)
  other arithmetic  19.3 us (8%)
  between operations  14.2 us (6%)
  starting transfers between devices  11 us (4%)
    pallas_call x1, Pallas kernels, z_sum(): pl.pallas_call(functools.partial(z_sum_kernel, n_z, n_y, n_lanes), out_sh...  90.2 us
    all_to_all x1, waiting for transfers between devices, body(): lax.all_to_all(send_rows.reshape(group_size, capacity, SEG, D), 'fsdp', s...  36.2 us
    pallas_call x1, Pallas kernels, y_site_sum(): pl.pallas_call(functools.partial(y_site_kernel, n_y, n_site), out_shape=j...  31.7 us
    all_to_all x1, starting transfers between devices, body(): lax.all_to_all(send_rows.reshape(group_size, capacity, SEG, D), 'fsdp', s...  10.9 us
    dot_general x4, matrix products, body(): jnp.einsum('rckj,rd->kcjd', by_core, cotangent[:, part * width:(part + 1)...  9.82 us
    dot_general x1, matrix products, stem_taps(): jnp.einsum('rd,fkcd->krfc', frames, stem_gathered, preferred_element_type...  8.7 us
  transfers between devices with their start and end apart: 2, of which 1 were waited for; matrix products, arithmetic and copies ran while one was open for 9% of the time, Pallas kernels for 49%

profile of v10, /device:TPU:24, one launch (start us, length us, event | category | flops | bytes accessed | tf_op | source)
XLA Modules:
  0.0 247.0 jit_solution(2627707201326831651)
XLA Ops:
  7.2 0.0 copy-start
  7.2 0.0 copy-start.3
  7.2 0.0 all-gather.3.cloned.1.call-start
  7.2 1.7 pad_maximum_fusion.1
  8.9 0.0 all-gather.3.cloned.1.call-update
  9.0 3.0 %copy.22 = f32[1,512,1536]{1,2,0:T(8,128)} copy(bf16[1,512,1536]{2,1,0:T(8,128)(2,1)} %param.5) | data formatting | bytes 4718592 | tf_op jit(solution)/shard_map/convert_element_type | solution.py:250
  12.0 0.0 copy-done.3
  12.0 0.1 copy.27
  12.1 0.1 reduce-window.8
  12.2 0.1 reduce.2
  12.3 0.7 fusion.38
  13.0 0.2 convert_reduce_fusion.3
  13.2 0.2 convert_reduce_fusion.2
  13.4 0.1 select_reduce_fusion
  13.5 0.1 reduce_sum.104
  13.7 0.1 fusion.32
  13.7 0.2 broadcast_in_dim.86
  13.9 0.0 copy-done
  13.9 0.0 copy-start.1
  13.9 0.3 convert_reduce_fusion
  14.2 0.0 copy-start.2
  14.2 0.5 multiply_reduce_fusion
  14.8 1.0 copy-done.1
  15.8 0.5 multiply_convert_fusion
  16.3 0.0 copy-done.2
  16.3 2.5 convolution_bitcast_fusion.refs_3_
  18.8 2.4 convolution_bitcast_fusion.1.refs_2_
  21.2 2.5 %convolution_bitcast_fusion.2.refs_1_ = f32[2,32,24,384]{3,2,1,0:T(8,128)} fusion(bf16[512,32,2,24]{0,3,2,1:T(8,128)(2,1)S(1)} %multiply_convert_fusion, bf16[512,1536]{1,0:T(8,128)(2,1)S(1)} %bitcast.117), kind=kOutput, calls=%fused_computation.32 | convolution fusion | flops 603979776 | bytes 4325376 | tf_op jit(solution)/shard_map/rckj,rd->kcjd/dot_general | solution.py:266
  23.7 2.4 convolution_bitcast_fusion.3.refs_0_
  26.2 90.2 %shard_map.68.ztot = f32[4,4,24,384]{3,2,1,0:T(8,128)} custom-call(f32[2,32,24,384]{3,2,1,0:T(8,128)} %convolution_bitcast_fusion.3.refs_0_, f32[2,32,24,384]{3,2,1,0:T(8,128)} %convolution_bitcast_fusion.2.refs_1_, f32[2,32,24,384]{3,2,1,0:T(8,128)} %convolution_bitcast_fusion.1.refs_2_, f32[2,32,24,384]{3,2,1,0:T(8,128)} %convolution_bitcast_fusion.refs_3_), custom_call_target="tpu_custom_call" | custom-call | tf_op jit(solution)/shard_map/pallas_call | solution.py:204
  116.5 0.0 all-gather.3.cloned.1.call-done
  116.5 2.7 %slice.41 = bf16[64,24,1536]{2,1,0:T(8,128)(2,1)S(1)} slice(bf16[64,48,1536]{2,1,0:T(8,128)(2,1)} %bitcast.120), slice={[0:64], [0:24], [0:1536]} | slice | bytes 9437184 | tf_op jit(solution)/shard_map/slice | solution.py:272
  119.1 4.3 %fusion.8 = (f32[512]{0:T(512)S(1)}, f32[1536,512]{0,1:T(8,128)}) fusion(bf16[1,512,1536]{2,1,0:T(8,128)(2,1)S(1)} %copy-done, f32[512]{0:T(512)S(1)} %add_rsqrt_fusion, f32[512]{0:T(512)S(1)} %broadcast_multiply_fusion.2, bf16[1536,1536]{1,0:T(8,128)(2,1)S(1)} %bitcast.119, bf16[1,512,1536]{2,1,0:T(8,128)(2,1)S(1)} %copy-done.2), kind=kOutput, calls=%fused_computation.12 | convolution fusion | flops 2419850752 | bytes 11016192 | tf_op jit(solution)/shard_map/dot_general | solution.py:274
  123.5 2.1 reduce_sum.105
  125.6 3.4 %fusion.21 = bf16[64,8,1536]{2,1,0:T(8,128)(2,1)S(1)} fusion(bf16[1,512,1536]{2,1,0:T(8,128)(2,1)S(1)} %copy-done, f32[1536,512]{0,1:T(8,128)} %get-tuple-element.9, f32[512]{0:T(512)S(1)} %get-tuple-element.10, f32[512]{0:T(512)S(1)} %get-tuple-element.11, f32[512]{0:T(512)S(1)} %add_rsqrt_fusion, f32[512]{0:T(512)S(1)} %broadcast_multiply_fusion.2, ...), kind=kLoop, calls=%fused_computation.34 | loop fusion | flops 7864320 | bytes 7872512 | tf_op jit(solution)/shard_map/reshape | solution.py:312
  129.0 2.4 gather_fusion
  131.5 3.3 %select_select_fusion = bf16[64,2,8,1536]{3,2,1,0:T(8,128)(2,1)} fusion(bf16[64,2,8,1536]{3,2,1,0:T(8,128)(2,1)} %bitcast.113, pred[64,2]{1,0:T(8,128)(4,1)S(1)} %compare_and_fusion, pred[64,2]{1,0:T(8,128)(4,1)S(1)} %broadcast_in_dim.86), kind=kLoop, calls=%fused_computation.16 | loop fusion | flops 3145728 | bytes 6291712 | tf_op jit(solution)/shard_map/jit(_where)/select_n | solution.py:314
  134.8 10.9 %all-to-all-start = ((bf16[64,2,8,1536]{3,2,1,0:T(8,128)(2,1)}), bf16[64,2,8,1536]{3,2,1,0:T(8,128)(2,1)S(1)}, u32[]{:S(2)}, u32[]{:S(2)}) async-start(bf16[64,2,8,1536]{3,2,1,0:T(8,128)(2,1)} %select_select_fusion), calls=%async_computation | async-start | bytes 6291456 | tf_op jit(solution)/shard_map/all_to_all | solution.py:315
  145.7 0.7 iota_compare_fusion.3
  146.4 0.7 and_select_fusion.4
  147.1 0.2 convert_reduce_fusion.1
  147.2 1.4 fusion.45
  148.6 1.4 compare_and_fusion.1
  150.0 31.7 %shard_map.69 = f32[4,24,384]{2,1,0:T(8,128)} custom-call(f32[4,4,24,384]{3,2,1,0:T(8,128)} %shard_map.68.ztot), custom_call_target="tpu_custom_call" | custom-call | tf_op jit(solution)/shard_map/pallas_call | solution.py:227
  181.7 0.9 multiply_bitcast_fusion
  182.6 0.7 copy.31
  183.3 36.2 %all-to-all-done = bf16[64,2,8,1536]{3,2,1,0:T(8,128)(2,1)S(1)} async-done(((bf16[64,2,8,1536]{3,2,1,0:T(8,128)(2,1)}), bf16[64,2,8,1536]{3,2,1,0:T(8,128)(2,1)S(1)}, u32[]{:S(2)}, u32[]{:S(2)}) %all-to-all-start) | async-done | bytes 3145760 | tf_op jit(solution)/shard_map/all_to_all | solution.py:315
  219.5 2.4 gather_fusion.1
  221.8 8.7 %fusion.14 = f32[3,1024,64,8]{1,3,0,2:T(8,128)S(1)} fusion(bf16[128,8,1536]{2,1,0:T(8,128)(2,1)} %gather_fusion.1, pred[128]{0:T(512)(128)(4,1)S(1)} %compare_and_fusion.1, pred[128]{0:T(512)(128)(4,1)S(1)} %iota_compare_fusion.3, bf16[64,48,1536]{2,1,0:T(8,128)(2,1)} %bitcast.121), kind=kOutput, calls=%fused_computation.23 | convolution fusion | flops 4834983936 | bytes 14156032 | tf_op jit(solution)/shard_map/rd,fkcd->krfc/dot_general | solution.py:23
  230.5 0.6 slice_bitcast_fusion
  231.1 0.2 fusion.24
  231.3 0.5 fusion.25
  231.8 0.2 pad_maximum_fusion
  232.0 4.1 %copy.28 = bf16[1024,2,512]{2,1,0:T(2,128)(2,1)} copy(bf16[1024,2,512]{0,2,1:T(8,128)(2,1)S(1)} %pad_maximum_fusion) | data formatting | bytes 4194304 | tf_op jit(solution)/shard_map/stack | solution.py:330
  236.1 4.1 %convert_element_type.52 = bf16[1,2048,512]{2,1,0:T(8,128)(2,1)} reshape(bf16[1024,2,512]{2,1,0:T(2,128)(2,1)} %copy.28) | data formatting | bytes 4194304 | tf_op jit(solution)/shard_map/convert_element_type | solution.py:332
  (8 shorter events, 0.1 us)
Async XLA Ops:
  7.2 6.7 %copy-start = (bf16[1,512,1536]{2,1,0:T(8,128)(2,1)S(1)}, bf16[1,512,1536]{2,1,0:T(8,128)(2,1)}, u32[]{:S(2)}) copy-start(bf16[1,512,1536]{2,1,0:T(8,128)(2,1)} %param.5) | copy-start | bytes 4718596
  7.2 4.8 %copy-start.3 = (s32[1,64]{1,0:T(1,128)S(1)}, s32[1,64]{1,0:T(1,128)}, u32[]{:S(2)}) copy-start(s32[1,64]{1,0:T(1,128)} %param.9) | copy-start | bytes 772
  7.2 109.3 %all-gather.3.cloned.1.call-start = ((), (), s32[]{:S(2)}) async-start(), calls=%async_computation.1 | async-start | bytes 9584640 | tf_op jit(solution)/shard_map/all_gather | solution.py:261
  13.9 1.9 copy-start.1
  14.2 2.1 copy-start.2
  134.8 84.7 %all-to-all-start = ((bf16[64,2,8,1536]{3,2,1,0:T(8,128)(2,1)}), bf16[64,2,8,1536]{3,2,1,0:T(8,128)(2,1)S(1)}, u32[]{:S(2)}, u32[]{:S(2)}) async-start(bf16[64,2,8,1536]{3,2,1,0:T(8,128)(2,1)} %select_select_fusion), calls=%async_computation | async-start | bytes 6291456 | tf_op jit(solution)/shard_map/all_to_all | solution.py:315
Sparse Core Ops, SparseCore 0:
  11.3 98.5 all-gather.2

commit v11 on v8

--- a/solution.py
+++ b/solution.py
@@ -19,10 +19,11 @@
 
 
 def stem_taps(frames, stem_gathered):
-    taps = jnp.einsum(
-        "rd,fkcd->krfc", frames, stem_gathered, preferred_element_type=jnp.float32
-    )
-    return taps.reshape(taps.shape[0], taps.shape[1], -1)
+    devices, taps_n, chans = stem_gathered.shape[:3]
+    width = devices * chans
+    weights = stem_gathered.transpose(1, 0, 2, 3).reshape(taps_n * width, D)
+    flat = lax.dot_general(frames, weights, (((1,), (1,)), ((), ())), preferred_element_type=jnp.float32)
+    return [flat[:, tap * width:(tap + 1) * width] for tap in range(taps_n)]
 
 
 def ring_pass(n, lanes, prepare=None):
@@ -316,13 +317,13 @@
     frames = jnp.where(is_live[:, None, None], picked, zero_bf).reshape(OWN_SEG * SEG, D)
     tap_terms = stem_taps(frames, stem_gathered)
     shifted = jnp.concatenate(
-        [tap_terms[0][1:], jnp.zeros((1, tap_terms.shape[2]), jnp.float32)], 0
+        [tap_terms[0][1:], jnp.zeros((1, tap_terms[0].shape[1]), jnp.float32)], 0
     )
     odd_rows = tap_terms[2] + shifted
     stem_rows = (
-        jnp.stack([tap_terms[1], odd_rows], 1)
-        .reshape(2 * OWN_SEG * SEG, tap_terms.shape[2])
+        jnp.concatenate([tap_terms[1], odd_rows], 1)
         .astype(jnp.bfloat16)
+        .reshape(2 * OWN_SEG * SEG, tap_terms[0].shape[1])
     )
     shard_sum = y_site_sum(z_total).transpose(1, 0, 2).reshape(rows_out, D)
     weight_grad = shard_sum / math.sqrt(lax.axis_size("site") * group_size * HOLD * SEG)

time: 245 us -> 242 us (0.988)
  waiting for transfers between devices: 37.1 us -> 33.9 us
    transpose x0 -> x1, local copies, waits for them, and re-layouts: none -> 4.95 us  [stem_taps(): weights = stem_gathered.transpose(1, 0, 2, 3).reshape(taps_n * width, D)]
    another operation x3 -> x1, local copies, waits for them, and re-layouts: 4.33 us -> 0.1 us  [the longest x2 4.23 us: body(): jnp.stack([tap_terms[1], odd_rows], 1)]
    slice x1, local copies, waits for them, and re-layouts: 2.81 us -> 6.77 us  [body(): full_weight = gathered[:, :rows_w].reshape(group_size * rows_w, D)]
    all_to_all x1, waiting for transfers between devices: 37 us -> 33.9 us  [body(): lax.all_to_all(send_rows.reshape(group_size, capacity, SEG, D), 'fsdp', s...]
  transfers between devices with their start and end apart: 2 -> 2, of which waited for: 1 -> 1; matrix products, arithmetic and copies ran while one was open for 8% -> 11% of each run, Pallas kernels for 50% -> 50%
where the time goes in v11:
time: 242 us; the launch traced here: 241 us
  Pallas kernels  121 us (50%)
  waiting for transfers between devices  33.9 us (14%)
  local copies, waits for them, and re-layouts  21.9 us (9%)
  other arithmetic  21.8 us (9%)
  matrix products  20.2 us (8%)
  between operations  14.3 us (6%)
  starting transfers between devices  7.62 us (3%)
    pallas_call x1, Pallas kernels, z_sum(): pl.pallas_call(functools.partial(z_sum_kernel, n_z, n_y), out_shape=jax.S...  92.1 us
    all_to_all x1, waiting for transfers between devices, body(): lax.all_to_all(send_rows.reshape(group_size, capacity, SEG, D), 'fsdp', s...  33.9 us
    pallas_call x1, Pallas kernels, y_site_sum(): pl.pallas_call(functools.partial(y_site_kernel, n_y, n_site), out_shape=j...  29 us
    dot_general x1, matrix products, stem_taps(): lax.dot_general(frames, weights, (((1,), (1,)), ((), ())), preferred_elem...  8.55 us
    all_to_all x1, starting transfers between devices, body(): lax.all_to_all(send_rows.reshape(group_size, capacity, SEG, D), 'fsdp', s...  7.58 us
    dot_general x2, matrix products, body(): jnp.einsum('rckj,rd->kcjd', by_core, cotangent[:, part * (D // 2):(part +...  7.23 us
    slice x1, local copies, waits for them, and re-layouts, body(): full_weight = gathered[:, :rows_w].reshape(group_size * rows_w, D)  6.77 us
    transpose x1, local copies, waits for them, and re-layouts, stem_taps(): weights = stem_gathered.transpose(1, 0, 2, 3).reshape(taps_n * width, D)  4.95 us
  transfers between devices with their start and end apart: 2, of which 1 were waited for; matrix products, arithmetic and copies ran while one was open for 11% of the time, Pallas kernels for 50%

profile of v11, /device:TPU:24, one launch (start us, length us, event | category | flops | bytes accessed | tf_op | source)
XLA Modules:
  0.0 240.7 jit_solution(2568328726553236171)
XLA Ops:
  7.2 0.0 copy-start.3
  7.2 0.0 all-gather.3.cloned.1.call-start
  7.2 1.6 pad_maximum_fusion.1
  8.8 0.0 all-gather.3.cloned.1.call-update
  8.8 1.7 copy.23
  10.6 0.0 copy-done.3
  10.6 0.1 copy.22
  10.7 0.1 reduce-window.8
  10.8 0.1 reduce.2
  10.9 0.7 fusion.26
  11.6 0.2 convert_reduce_fusion.3
  11.8 0.2 convert_reduce_fusion.2
  12.0 0.1 select_reduce_fusion
  12.1 0.1 reduce_sum.102
  12.2 0.1 fusion.20
  12.3 0.2 broadcast_in_dim.85
  12.5 0.0 copy-start.1
  12.5 1.8 convert_reduce_fusion
  14.3 2.0 multiply_reduce_fusion
  16.3 0.0 copy-done.1
  16.3 3.6 %convolution_bitcast_fusion.hi_ref = f32[2,32,24,768]{3,2,1,0:T(8,128)} fusion(bf16[512,1536]{1,0:T(8,128)(2,1)S(1)} %bitcast.86, f32[512,32,2,24]{0,3,2,1:T(8,128)S(1)} %bitcast.81, f32[512]{0:T(512)S(1)} %add_rsqrt_fusion, f32[512]{0:T(512)S(1)} %broadcast_multiply_fusion.2), kind=kOutput, calls=%fused_computation.22 | convolution fusion | flops 1210318848 | bytes 8654848 | tf_op jit(solution)/shard_map/rckj,rd->kcjd/dot_general | solution.py:260
  19.9 3.7 %convolution_bitcast_fusion.1.lo_ref = f32[2,32,24,768]{3,2,1,0:T(8,128)} fusion(bf16[512,1536]{1,0:T(8,128)(2,1)S(1)} %bitcast.87, f32[512,32,2,24]{0,3,2,1:T(8,128)S(1)} %bitcast.82, f32[512]{0:T(512)S(1)} %add_rsqrt_fusion, f32[512]{0:T(512)S(1)} %broadcast_multiply_fusion.2), kind=kOutput, calls=%fused_computation.23 | convolution fusion | flops 1210318848 | bytes 8654848 | tf_op jit(solution)/shard_map/rckj,rd->kcjd/dot_general | solution.py:260
  23.5 92.1 %shard_map.68.ztot = f32[4,2,24,768]{3,2,1,0:T(8,128)} custom-call(f32[2,32,24,768]{3,2,1,0:T(8,128)} %convolution_bitcast_fusion.1.lo_ref, f32[2,32,24,768]{3,2,1,0:T(8,128)} %convolution_bitcast_fusion.hi_ref), custom_call_target="tpu_custom_call" | custom-call | tf_op jit(solution)/shard_map/pallas_call | solution.py:200
  115.6 0.0 all-gather.3.cloned.1.call-done
  115.7 0.0 copy-start
  115.7 0.0 copy-start.2
  115.7 6.8 %fusion.38 = (bf16[64,24,1536]{2,1,0:T(8,128)(2,1)S(1)}, bf16[3,64,8,1536]{3,2,0,1:T(8,128)(2,1)}) fusion(bf16[64,48,1536]{2,1,0:T(8,128)(2,1)} %bitcast.85), kind=kLoop, calls=%fused_computation.101 | loop fusion | bytes 18874368 | tf_op jit(solution)/shard_map/slice | solution.py:266
  122.5 0.0 copy-done
  122.5 0.0 copy-done.2
  122.5 4.4 %fusion.6 = (f32[512]{0:T(512)S(1)}, f32[1536,512]{0,1:T(8,128)}) fusion(bf16[1,512,1536]{2,1,0:T(8,128)(2,1)S(1)} %copy-done, f32[512]{0:T(512)S(1)} %add_rsqrt_fusion, f32[512]{0:T(512)S(1)} %broadcast_multiply_fusion.2, bf16[1536,1536]{1,0:T(8,128)(2,1)S(1)} %bitcast.89, bf16[1,512,1536]{2,1,0:T(8,128)(2,1)S(1)} %copy-done.2), kind=kOutput, calls=%fused_computation.11 | convolution fusion | flops 2419850752 | bytes 11016192 | tf_op jit(solution)/shard_map/dot_general | solution.py:268
  126.9 2.1 reduce_sum.105
  129.0 3.4 %fusion.13 = bf16[64,8,1536]{2,1,0:T(8,128)(2,1)S(1)} fusion(bf16[1,512,1536]{2,1,0:T(8,128)(2,1)S(1)} %copy-done, f32[1536,512]{0,1:T(8,128)} %get-tuple-element.11, f32[512]{0:T(512)S(1)} %get-tuple-element.12, f32[512]{0:T(512)S(1)} %get-tuple-element.13, f32[512]{0:T(512)S(1)} %add_rsqrt_fusion, f32[512]{0:T(512)S(1)} %broadcast_multiply_fusion.2, ...), kind=kLoop, calls=%fused_computation.28 | loop fusion | flops 7864320 | bytes 7872512 | tf_op jit(solution)/shard_map/reshape | solution.py:306
  132.4 2.4 %gather_fusion = bf16[128,8,1536]{2,1,0:T(8,128)(2,1)} fusion(bf16[64,8,1536]{2,1,0:T(8,128)(2,1)S(1)} %fusion.13, s32[1024]{0:T(1024)S(1)} %pad_clamp_fusion.1), kind=kCustom, calls=%fused_computation | custom fusion | bytes 6291968 | tf_op jit(solution)/shard_map/jit(_take)/gather | solution.py:308
  134.9 3.3 %select_select_fusion = bf16[64,2,8,1536]{3,2,1,0:T(8,128)(2,1)} fusion(bf16[64,2,8,1536]{3,2,1,0:T(8,128)(2,1)} %bitcast.84, pred[64,2]{1,0:T(8,128)(4,1)S(1)} %compare_and_fusion, pred[64,2]{1,0:T(8,128)(4,1)S(1)} %broadcast_in_dim.85), kind=kLoop, calls=%fused_computation.15 | loop fusion | flops 3145728 | bytes 6291712 | tf_op jit(solution)/shard_map/jit(_where)/select_n | solution.py:308
  138.2 7.6 %all-to-all-start = ((bf16[64,2,8,1536]{3,2,1,0:T(8,128)(2,1)}), bf16[64,2,8,1536]{3,2,1,0:T(8,128)(2,1)S(1)}, u32[]{:S(2)}, u32[]{:S(2)}) async-start(bf16[64,2,8,1536]{3,2,1,0:T(8,128)(2,1)} %select_select_fusion), calls=%async_computation | async-start | bytes 6291456 | tf_op jit(solution)/shard_map/all_to_all | solution.py:309
  145.8 0.7 iota_compare_fusion.3
  146.4 0.7 and_select_fusion.4
  147.1 0.2 convert_reduce_fusion.1
  147.3 1.4 fusion.33
  148.7 1.4 compare_and_fusion.1
  150.1 5.0 %copy.26 = bf16[3,64,8,1536]{3,2,1,0:T(8,128)(2,1)} copy(bf16[3,64,8,1536]{3,2,0,1:T(8,128)(2,1)} %get-tuple-element.9) | data formatting | bytes 9437184 | tf_op jit(solution)/shard_map/transpose | solution.py:24
  155.0 29.0 %shard_map.69 = f32[2,24,768]{2,1,0:T(8,128)} custom-call(f32[4,2,24,768]{3,2,1,0:T(8,128)} %shard_map.68.ztot), custom_call_target="tpu_custom_call" | custom-call | tf_op jit(solution)/shard_map/pallas_call | solution.py:222
  184.1 0.9 multiply_bitcast_fusion
  185.0 0.7 copy.28
  185.7 33.9 %all-to-all-done = bf16[64,2,8,1536]{3,2,1,0:T(8,128)(2,1)S(1)} async-done(((bf16[64,2,8,1536]{3,2,1,0:T(8,128)(2,1)}), bf16[64,2,8,1536]{3,2,1,0:T(8,128)(2,1)S(1)}, u32[]{:S(2)}, u32[]{:S(2)}) %all-to-all-start) | async-done | bytes 3145760 | tf_op jit(solution)/shard_map/all_to_all | solution.py:309
  219.5 2.4 %gather_fusion.1 = bf16[128,8,1536]{2,1,0:T(8,128)(2,1)} fusion(bf16[128,8,1536]{2,1,0:T(8,128)(2,1)S(1)} %bitcast.83, s32[1024]{0:T(1024)S(1)} %pad_clamp_fusion), kind=kCustom, calls=%fused_computation.1 | custom fusion | bytes 6291968 | tf_op jit(solution)/shard_map/jit(_take)/gather | solution.py:316
  221.9 8.5 %fusion = f32[1024,1536]{1,0:T(8,128)S(1)} fusion(bf16[1536,1536]{1,0:T(8,128)(2,1)} %bitcast.88, bf16[128,8,1536]{2,1,0:T(8,128)(2,1)} %gather_fusion.1, pred[128]{0:T(512)(128)(4,1)S(1)} %compare_and_fusion.1, pred[128]{0:T(512)(128)(4,1)S(1)} %iota_compare_fusion.3), kind=kOutput, calls=%fused_computation.3 | convolution fusion | flops 4834983936 | bytes 14156032 | tf_op jit(solution)/shard_map/dot_general | solution.py:25
  230.5 0.2 slice.39
  230.8 0.1 slice.49
  230.9 0.6 fusion.12
  231.5 0.3 pad_maximum_fusion
  231.7 2.1 convert_element_type.52
  (8 shorter events, 0.1 us)
Async XLA Ops:
  7.2 3.4 %copy-start.3 = (s32[1,64]{1,0:T(1,128)S(1)}, s32[1,64]{1,0:T(1,128)}, u32[]{:S(2)}) copy-start(s32[1,64]{1,0:T(1,128)} %param.9) | copy-start | bytes 772
  7.2 108.5 %all-gather.3.cloned.1.call-start = ((), (), s32[]{:S(2)}) async-start(), calls=%async_computation.1 | async-start | bytes 9584640 | tf_op jit(solution)/shard_map/all_gather | solution.py:256
  12.5 3.8 %copy-start.1 = (bf16[1,512,1536]{2,1,0:T(8,128)(2,1)S(1)}, bf16[1,512,1536]{2,1,0:T(8,128)(2,1)}, u32[]{:S(2)}) copy-start(bf16[1,512,1536]{2,1,0:T(8,128)(2,1)} %param.6) | copy-start | bytes 4718596
  115.7 6.8 %copy-start = (bf16[1,512,1536]{2,1,0:T(8,128)(2,1)S(1)}, bf16[1,512,1536]{2,1,0:T(8,128)(2,1)}, u32[]{:S(2)}) copy-start(bf16[1,512,1536]{2,1,0:T(8,128)(2,1)} %param.5) | copy-start | bytes 4718596
  115.7 6.8 %copy-start.2 = (bf16[1,512,1536]{2,1,0:T(8,128)(2,1)S(1)}, bf16[1,512,1536]{2,1,0:T(8,128)(2,1)}, u32[]{:S(2)}) copy-start(bf16[1,512,1536]{2,1,0:T(8,128)(2,1)} %param.6) | copy-start | bytes 4718596
  138.2 81.3 %all-to-all-start = ((bf16[64,2,8,1536]{3,2,1,0:T(8,128)(2,1)}), bf16[64,2,8,1536]{3,2,1,0:T(8,128)(2,1)S(1)}, u32[]{:S(2)}, u32[]{:S(2)}) async-start(bf16[64,2,8,1536]{3,2,1,0:T(8,128)(2,1)} %select_select_fusion), calls=%async_computation | async-start | bytes 6291456 | tf_op jit(solution)/shard_map/all_to_all | solution.py:309
Sparse Core Ops, SparseCore 0:
  11.3 98.4 all-gather.2

commit v12 on v11

--- a/solution.py
+++ b/solution.py
@@ -252,8 +252,8 @@
     normed_bf = normed.astype(jnp.bfloat16)
     rows_w = proj_weight.shape[0]
     taps_n, chans = stem_weight.shape[0], stem_weight.shape[1]
-    joined = jnp.concatenate([proj_weight, stem_weight.reshape(taps_n * chans, D)], 0)
-    gathered = lax.all_gather(joined, "fsdp", axis=0, tiled=False)
+    joined = jnp.concatenate([proj_weight, stem_weight.reshape(taps_n * chans, D)], 1)
+    gathered = lax.all_gather(joined, "fsdp", axis=0, tiled=True)
     rows_out = D // group_size
     by_core = normed_bf.reshape(normed_bf.shape[0], group_size // 2, 2, rows_out)
     halves = [
@@ -263,8 +263,8 @@
     ]
     z_total = z_sum(halves[0], halves[1], N_Z)
     z_total, gathered = lax.optimization_barrier((z_total, gathered))
-    full_weight = gathered[:, :rows_w].reshape(group_size * rows_w, D)
-    stem_gathered = gathered[:, rows_w:].reshape(group_size, taps_n, chans, D)
+    full_weight = gathered[:, :D]
+    stem_gathered = gathered[:, D:].reshape(group_size, taps_n, chans, D)
     proj_back = lax.dot_general(
         cotangent,
         full_weight,

time: 242 us -> 237 us (0.979)
  local copies, waits for them, and re-layouts: 21.9 us -> 15 us
    slice x1 -> x2, local copies, waits for them, and re-layouts: 6.77 us -> 2.33 us  [body(): stem_gathered = gathered[:, D:].reshape(group_size, taps_n, chans, D)]
    transpose x1, local copies, waits for them, and re-layouts: 4.95 us -> 2.49 us  [stem_taps(): weights = stem_gathered.transpose(1, 0, 2, 3).reshape(taps_n * width, D)]
  transfers between devices with their start and end apart: 2 -> 2, of which waited for: 1 -> 1; matrix products, arithmetic and copies ran while one was open for 11% -> 10% of each run, Pallas kernels for 50% -> 51%
where the time goes in v12:
time: 237 us; the launch traced here: 236 us
  Pallas kernels  120 us (51%)
  waiting for transfers between devices  34.8 us (15%)
  matrix products  22.4 us (9%)
  other arithmetic  21.7 us (9%)
  local copies, waits for them, and re-layouts  15 us (6%)
  between operations  14.3 us (6%)
  starting transfers between devices  7.46 us (3%)
    pallas_call x1, Pallas kernels, z_sum(): pl.pallas_call(functools.partial(z_sum_kernel, n_z, n_y), out_shape=jax.S...  92 us
    all_to_all x1, waiting for transfers between devices, body(): lax.all_to_all(send_rows.reshape(group_size, capacity, SEG, D), 'fsdp', s...  34.8 us
    pallas_call x1, Pallas kernels, y_site_sum(): pl.pallas_call(functools.partial(y_site_kernel, n_y, n_site), out_shape=j...  28.2 us
    dot_general x1, matrix products, stem_taps(): lax.dot_general(frames, weights, (((1,), (1,)), ((), ())), preferred_elem...  8.55 us
    all_to_all x1, starting transfers between devices, body(): lax.all_to_all(send_rows.reshape(group_size, capacity, SEG, D), 'fsdp', s...  7.42 us
    dot_general x2, matrix products, body(): jnp.einsum('rckj,rd->kcjd', by_core, cotangent[:, part * (D // 2):(part +...  7.23 us
    dot_general x1, matrix products, body(): lax.dot_general(cotangent, full_weight, (((1,), (1,)), ((), ())), preferr...  6.62 us
  transfers between devices with their start and end apart: 2, of which 1 were waited for; matrix products, arithmetic and copies ran while one was open for 10% of the time, Pallas kernels for 51%

profile of v12, /device:TPU:24, one launch (start us, length us, event | category | flops | bytes accessed | tf_op | source)
XLA Modules:
  0.0 235.8 jit_solution(16643965387462523273)
XLA Ops:
  7.2 0.0 copy-start.3
  7.2 0.0 all-gather.2.cloned.1.call-start
  7.2 1.6 pad_maximum_fusion.1
  8.8 0.0 all-gather.2.cloned.1.call-update
  8.8 1.7 copy.23
  10.6 0.0 copy-done.3
  10.6 0.1 copy.22
  10.7 0.1 reduce-window.8
  10.8 0.1 reduce.2
  10.9 0.7 fusion.28
  11.6 0.2 convert_reduce_fusion.3
  11.8 0.2 convert_reduce_fusion.2
  12.0 0.1 select_reduce_fusion
  12.1 0.1 reduce_sum.102
  12.2 0.1 fusion.22
  12.3 0.2 broadcast_in_dim.85
  12.5 0.0 copy-start.1
  12.5 1.8 convert_reduce_fusion
  14.3 2.0 multiply_reduce_fusion
  16.3 0.0 copy-done.1
  16.3 3.6 %convolution_bitcast_fusion.hi_ref = f32[2,32,24,768]{3,2,1,0:T(8,128)} fusion(bf16[512,1536]{1,0:T(8,128)(2,1)S(1)} %bitcast.82, f32[512,32,2,24]{0,3,2,1:T(8,128)S(1)} %bitcast.77, f32[512]{0:T(512)S(1)} %add_rsqrt_fusion, f32[512]{0:T(512)S(1)} %broadcast_multiply_fusion.2), kind=kOutput, calls=%fused_computation.23 | convolution fusion | flops 1210318848 | bytes 8654848 | tf_op jit(solution)/shard_map/rckj,rd->kcjd/dot_general | solution.py:260
  19.9 3.7 %convolution_bitcast_fusion.1.lo_ref = f32[2,32,24,768]{3,2,1,0:T(8,128)} fusion(bf16[512,1536]{1,0:T(8,128)(2,1)S(1)} %bitcast.83, f32[512,32,2,24]{0,3,2,1:T(8,128)S(1)} %bitcast.78, f32[512]{0:T(512)S(1)} %add_rsqrt_fusion, f32[512]{0:T(512)S(1)} %broadcast_multiply_fusion.2), kind=kOutput, calls=%fused_computation.24 | convolution fusion | flops 1210318848 | bytes 8654848 | tf_op jit(solution)/shard_map/rckj,rd->kcjd/dot_general | solution.py:260
  23.5 0.0 copy-start
  23.5 0.0 copy-start.2
  23.5 92.0 %shard_map.68.ztot = f32[4,2,24,768]{3,2,1,0:T(8,128)} custom-call(f32[2,32,24,768]{3,2,1,0:T(8,128)} %convolution_bitcast_fusion.1.lo_ref, f32[2,32,24,768]{3,2,1,0:T(8,128)} %convolution_bitcast_fusion.hi_ref), custom_call_target="tpu_custom_call" | custom-call | tf_op jit(solution)/shard_map/pallas_call | solution.py:200
  115.5 0.0 all-gather.2.cloned.1.call-done
  115.6 0.0 copy-done
  115.6 0.0 copy-done.2
  115.6 6.6 %fusion.8 = (f32[512]{0:T(512)S(1)}, f32[1536,512]{0,1:T(8,128)}) fusion(bf16[1,512,1536]{2,1,0:T(8,128)(2,1)S(1)} %copy-done, f32[512]{0:T(512)S(1)} %add_rsqrt_fusion, f32[512]{0:T(512)S(1)} %broadcast_multiply_fusion.2, bf16[1,512,1536]{2,1,0:T(8,128)(2,1)S(1)} %copy-done.2, bf16[1536,3072]{1,0:T(8,128)(2,1)} %all-gather.2.cloned.1.call-done), kind=kOutput, calls=%fused_computation.12 | convolution fusion | flops 2419850752 | bytes 11016192 | tf_op jit(solution)/shard_map/dot_general | solution.py:268
  122.2 2.1 reduce_sum.105
  124.3 3.4 %fusion.15 = bf16[64,8,1536]{2,1,0:T(8,128)(2,1)S(1)} fusion(bf16[1,512,1536]{2,1,0:T(8,128)(2,1)S(1)} %copy-done, f32[1536,512]{0,1:T(8,128)} %get-tuple-element.9, f32[512]{0:T(512)S(1)} %get-tuple-element.10, f32[512]{0:T(512)S(1)} %get-tuple-element.11, f32[512]{0:T(512)S(1)} %add_rsqrt_fusion, f32[512]{0:T(512)S(1)} %broadcast_multiply_fusion.2, ...), kind=kLoop, calls=%fused_computation.29 | loop fusion | flops 7864320 | bytes 7872512 | tf_op jit(solution)/shard_map/reshape | solution.py:306
  127.8 2.4 %gather_fusion = bf16[128,8,1536]{2,1,0:T(8,128)(2,1)} fusion(bf16[64,8,1536]{2,1,0:T(8,128)(2,1)S(1)} %fusion.15, s32[1024]{0:T(1024)S(1)} %pad_clamp_fusion.1), kind=kCustom, calls=%fused_computation | custom fusion | bytes 6291968 | tf_op jit(solution)/shard_map/jit(_take)/gather | solution.py:308
  130.2 3.3 %select_select_fusion = bf16[64,2,8,1536]{3,2,1,0:T(8,128)(2,1)} fusion(bf16[64,2,8,1536]{3,2,1,0:T(8,128)(2,1)} %bitcast.81, pred[64,2]{1,0:T(8,128)(4,1)S(1)} %compare_and_fusion, pred[64,2]{1,0:T(8,128)(4,1)S(1)} %broadcast_in_dim.85), kind=kLoop, calls=%fused_computation.16 | loop fusion | flops 3145728 | bytes 6291712 | tf_op jit(solution)/shard_map/jit(_where)/select_n | solution.py:308
  133.5 7.4 %all-to-all-start = ((bf16[64,2,8,1536]{3,2,1,0:T(8,128)(2,1)}), bf16[64,2,8,1536]{3,2,1,0:T(8,128)(2,1)S(1)}, u32[]{:S(2)}, u32[]{:S(2)}) async-start(bf16[64,2,8,1536]{3,2,1,0:T(8,128)(2,1)} %select_select_fusion), calls=%async_computation | async-start | bytes 6291456 | tf_op jit(solution)/shard_map/all_to_all | solution.py:309
  140.9 0.7 iota_compare_fusion.3
  141.6 0.7 and_select_fusion.4
  142.3 0.2 convert_reduce_fusion.1
  142.5 1.4 fusion.35
  143.9 1.4 compare_and_fusion.1
  145.2 0.0 slice-start
  145.2 2.3 slice-done
  147.6 2.5 %copy.26 = bf16[3,64,8,1536]{3,2,1,0:T(8,128)(2,1)} copy(bf16[3,64,8,1536]{3,2,0,1:T(8,128)(2,1)S(1)} %bitcast.79) | data formatting | bytes 9437184 | tf_op jit(solution)/shard_map/transpose | solution.py:24
  150.0 28.2 %shard_map.69 = f32[2,24,768]{2,1,0:T(8,128)} custom-call(f32[4,2,24,768]{3,2,1,0:T(8,128)} %shard_map.68.ztot), custom_call_target="tpu_custom_call" | custom-call | tf_op jit(solution)/shard_map/pallas_call | solution.py:222
  178.3 0.9 multiply_bitcast_fusion
  179.2 0.7 copy.28
  179.9 34.8 %all-to-all-done = bf16[64,2,8,1536]{3,2,1,0:T(8,128)(2,1)S(1)} async-done(((bf16[64,2,8,1536]{3,2,1,0:T(8,128)(2,1)}), bf16[64,2,8,1536]{3,2,1,0:T(8,128)(2,1)S(1)}, u32[]{:S(2)}, u32[]{:S(2)}) %all-to-all-start) | async-done | bytes 3145760 | tf_op jit(solution)/shard_map/all_to_all | solution.py:309
  214.7 2.4 %gather_fusion.1 = bf16[128,8,1536]{2,1,0:T(8,128)(2,1)} fusion(bf16[128,8,1536]{2,1,0:T(8,128)(2,1)S(1)} %bitcast.80, s32[1024]{0:T(1024)S(1)} %pad_clamp_fusion), kind=kCustom, calls=%fused_computation.1 | custom fusion | bytes 6291968 | tf_op jit(solution)/shard_map/jit(_take)/gather | solution.py:316
  217.1 8.5 %fusion.2 = f32[1024,1536]{1,0:T(8,128)S(1)} fusion(bf16[1536,1536]{1,0:T(8,128)(2,1)} %bitcast.84, bf16[128,8,1536]{2,1,0:T(8,128)(2,1)} %gather_fusion.1, pred[128]{0:T(512)(128)(4,1)S(1)} %compare_and_fusion.1, pred[128]{0:T(512)(128)(4,1)S(1)} %iota_compare_fusion.3), kind=kOutput, calls=%fused_computation.4 | convolution fusion | flops 4834983936 | bytes 14156032 | tf_op jit(solution)/shard_map/dot_general | solution.py:25
  225.6 0.2 slice.39
  225.9 0.1 slice.50
  226.0 0.6 fusion.14
  226.6 0.3 pad_maximum_fusion
  226.9 2.1 convert_element_type.52
  (8 shorter events, 0.1 us)
Async XLA Ops:
  7.2 3.4 %copy-start.3 = (s32[1,64]{1,0:T(1,128)S(1)}, s32[1,64]{1,0:T(1,128)}, u32[]{:S(2)}) copy-start(s32[1,64]{1,0:T(1,128)} %param.9) | copy-start | bytes 772
  7.2 108.4 %all-gather.2.cloned.1.call-start = ((), (), s32[]{:S(2)}) async-start(), calls=%async_computation.1 | async-start | bytes 9584640 | tf_op jit(solution)/shard_map/all_gather | solution.py:256
  12.5 3.8 %copy-start.1 = (bf16[1,512,1536]{2,1,0:T(8,128)(2,1)S(1)}, bf16[1,512,1536]{2,1,0:T(8,128)(2,1)}, u32[]{:S(2)}) copy-start(bf16[1,512,1536]{2,1,0:T(8,128)(2,1)} %param.6) | copy-start | bytes 4718596
  23.5 92.1 %copy-start = (bf16[1,512,1536]{2,1,0:T(8,128)(2,1)S(1)}, bf16[1,512,1536]{2,1,0:T(8,128)(2,1)}, u32[]{:S(2)}) copy-start(bf16[1,512,1536]{2,1,0:T(8,128)(2,1)} %param.5) | copy-start | bytes 4718596
  23.5 92.1 %copy-start.2 = (bf16[1,512,1536]{2,1,0:T(8,128)(2,1)S(1)}, bf16[1,512,1536]{2,1,0:T(8,128)(2,1)}, u32[]{:S(2)}) copy-start(bf16[1,512,1536]{2,1,0:T(8,128)(2,1)} %param.6) | copy-start | bytes 4718596
  133.5 81.2 %all-to-all-start = ((bf16[64,2,8,1536]{3,2,1,0:T(8,128)(2,1)}), bf16[64,2,8,1536]{3,2,1,0:T(8,128)(2,1)S(1)}, u32[]{:S(2)}, u32[]{:S(2)}) async-start(bf16[64,2,8,1536]{3,2,1,0:T(8,128)(2,1)} %select_select_fusion), calls=%async_computation | async-start | bytes 6291456 | tf_op jit(solution)/shard_map/all_to_all | solution.py:309
  145.2 2.3 slice-start
Sparse Core Ops, SparseCore 0:
  11.3 99.3 all-gather.1

commit v13 on v12

--- a/solution.py
+++ b/solution.py
@@ -305,7 +305,7 @@
     row_index = jnp.where(is_live, holder * capacity + holder_rank, 0)
     held_segments = input_grad.reshape(HOLD, SEG, D)
     zero_bf = jnp.zeros((), jnp.bfloat16)
-    send_rows = jnp.where(filled[:, None, None], jnp.take(held_segments, source, axis=0), zero_bf)
+    send_rows = jnp.take(held_segments, source, axis=0, mode="clip")
     received = lax.all_to_all(
         send_rows.reshape(group_size, capacity, SEG, D),
         "fsdp",
@@ -313,7 +313,7 @@
         concat_axis=0,
         tiled=True,
     )
-    picked = jnp.take(received.reshape(group_size * capacity, SEG, D), row_index, axis=0)
+    picked = jnp.take(received.reshape(group_size * capacity, SEG, D), row_index, axis=0, mode="clip")
     frames = jnp.where(is_live[:, None, None], picked, zero_bf).reshape(OWN_SEG * SEG, D)
     tap_terms = stem_taps(frames, stem_gathered)
     shifted = jnp.concatenate(

time: 237 us -> 232 us (0.979)
  other arithmetic: 21.7 us -> 16.7 us
    select_n x3 -> x1, other arithmetic: 4.66 us -> 1.28 us  [body(): row_index = jnp.where(is_live, holder * capacity + holder_rank, 0)]
  transfers between devices with their start and end apart: 2 -> 2, of which waited for: 1 -> 1; matrix products, arithmetic and copies ran while one was open for 10% -> 9% of each run, Pallas kernels for 51% -> 52%
where the time goes in v13:
time: 232 us; the launch traced here: 231 us
  Pallas kernels  121 us (52%)
  waiting for transfers between devices  36.3 us (16%)
  matrix products  21.8 us (9%)
  other arithmetic  16.7 us (7%)
  local copies, waits for them, and re-layouts  14.6 us (6%)
  between operations  14.2 us (6%)
  starting transfers between devices  6.49 us (3%)
    pallas_call x1, Pallas kernels, z_sum(): pl.pallas_call(functools.partial(z_sum_kernel, n_z, n_y), out_shape=jax.S...  93 us
    all_to_all x1, waiting for transfers between devices, body(): lax.all_to_all(send_rows.reshape(group_size, capacity, SEG, D), 'fsdp', s...  36.2 us
    pallas_call x1, Pallas kernels, y_site_sum(): pl.pallas_call(functools.partial(y_site_kernel, n_y, n_site), out_shape=j...  28.3 us
    dot_general x1, matrix products, stem_taps(): lax.dot_general(frames, weights, (((1,), (1,)), ((), ())), preferred_elem...  7.94 us
    dot_general x2, matrix products, body(): jnp.einsum('rckj,rd->kcjd', by_core, cotangent[:, part * (D // 2):(part +...  7.23 us
    dot_general x1, matrix products, body(): lax.dot_general(cotangent, full_weight, (((1,), (1,)), ((), ())), preferr...  6.62 us
    all_to_all x1, starting transfers between devices, body(): lax.all_to_all(send_rows.reshape(group_size, capacity, SEG, D), 'fsdp', s...  6.45 us
  transfers between devices with their start and end apart: 2, of which 1 were waited for; matrix products, arithmetic and copies ran while one was open for 9% of the time, Pallas kernels for 52%

profile of v13, /device:TPU:24, one launch (start us, length us, event | category | flops | bytes accessed | tf_op | source)
XLA Modules:
  0.0 231.4 jit_solution(16441677391050348689)
XLA Ops:
  7.2 0.0 copy-start.3
  7.2 0.0 all-gather.2.cloned.1.call-start
  7.2 1.6 pad_maximum_fusion.1
  8.8 0.0 all-gather.2.cloned.1.call-update
  8.8 1.7 copy.22
  10.6 0.0 copy-done.3
  10.6 0.1 copy.25
  10.7 0.1 reduce-window.8
  10.8 0.1 reduce.2
  10.9 0.0 copy-start.1
  10.9 1.8 convert_reduce_fusion
  12.7 2.0 multiply_reduce_fusion
  14.7 0.0 copy-done.1
  14.7 3.6 %convolution_bitcast_fusion.hi_ref = f32[2,32,24,768]{3,2,1,0:T(8,128)} fusion(bf16[512,1536]{1,0:T(8,128)(2,1)S(1)} %bitcast.76, f32[512,32,2,24]{0,3,2,1:T(8,128)S(1)} %bitcast.71, f32[512]{0:T(512)S(1)} %add_rsqrt_fusion, f32[512]{0:T(512)S(1)} %broadcast_multiply_fusion.2), kind=kOutput, calls=%fused_computation.20 | convolution fusion | flops 1210318848 | bytes 8654848 | tf_op jit(solution)/shard_map/rckj,rd->kcjd/dot_general | solution.py:260
  18.3 3.7 %convolution_bitcast_fusion.1.lo_ref = f32[2,32,24,768]{3,2,1,0:T(8,128)} fusion(bf16[512,1536]{1,0:T(8,128)(2,1)S(1)} %bitcast.77, f32[512,32,2,24]{0,3,2,1:T(8,128)S(1)} %bitcast.72, f32[512]{0:T(512)S(1)} %add_rsqrt_fusion, f32[512]{0:T(512)S(1)} %broadcast_multiply_fusion.2), kind=kOutput, calls=%fused_computation.21 | convolution fusion | flops 1210318848 | bytes 8654848 | tf_op jit(solution)/shard_map/rckj,rd->kcjd/dot_general | solution.py:260
  21.9 0.0 copy-start
  21.9 0.0 copy-start.2
  21.9 93.0 %shard_map.68.ztot = f32[4,2,24,768]{3,2,1,0:T(8,128)} custom-call(f32[2,32,24,768]{3,2,1,0:T(8,128)} %convolution_bitcast_fusion.1.lo_ref, f32[2,32,24,768]{3,2,1,0:T(8,128)} %convolution_bitcast_fusion.hi_ref), custom_call_target="tpu_custom_call" | custom-call | tf_op jit(solution)/shard_map/pallas_call | solution.py:200
  114.9 0.7 fusion.24
  115.6 0.2 convert_reduce_fusion.3
  115.7 0.2 convert_reduce_fusion.2
  115.9 0.1 select_reduce_fusion
  116.1 0.0 all-gather.2.cloned.1.call-done
  116.1 0.0 copy-done
  116.1 0.0 copy-done.2
  116.1 6.6 %fusion.8 = (f32[512]{0:T(512)S(1)}, f32[1536,512]{0,1:T(8,128)}) fusion(bf16[1,512,1536]{2,1,0:T(8,128)(2,1)S(1)} %copy-done, f32[512]{0:T(512)S(1)} %add_rsqrt_fusion, f32[512]{0:T(512)S(1)} %broadcast_multiply_fusion.2, bf16[1,512,1536]{2,1,0:T(8,128)(2,1)S(1)} %copy-done.2, bf16[1536,3072]{1,0:T(8,128)(2,1)} %all-gather.2.cloned.1.call-done), kind=kOutput, calls=%fused_computation.12 | convolution fusion | flops 2419850752 | bytes 11016192 | tf_op jit(solution)/shard_map/dot_general | solution.py:268
  122.7 2.1 reduce_sum.95
  124.8 3.4 %fusion.13 = bf16[64,8,1536]{2,1,0:T(8,128)(2,1)S(1)} fusion(bf16[1,512,1536]{2,1,0:T(8,128)(2,1)S(1)} %copy-done, f32[1536,512]{0,1:T(8,128)} %get-tuple-element.9, f32[512]{0:T(512)S(1)} %get-tuple-element.10, f32[512]{0:T(512)S(1)} %get-tuple-element.11, f32[512]{0:T(512)S(1)} %add_rsqrt_fusion, f32[512]{0:T(512)S(1)} %broadcast_multiply_fusion.2, ...), kind=kLoop, calls=%fused_computation.26 | loop fusion | flops 7864320 | bytes 7872512 | tf_op jit(solution)/shard_map/reshape | solution.py:306
  128.3 2.4 %gather_fusion = bf16[128,8,1536]{2,1,0:T(8,128)(2,1)} fusion(bf16[64,8,1536]{2,1,0:T(8,128)(2,1)S(1)} %fusion.13, s32[1024]{0:T(1024)S(1)} %pad_clamp_fusion.1), kind=kCustom, calls=%fused_computation | custom fusion | bytes 6291968 | tf_op jit(solution)/shard_map/jit(_take)/gather | solution.py:308
  130.7 6.4 %all-to-all-start = ((bf16[64,2,8,1536]{3,2,1,0:T(8,128)(2,1)}), bf16[64,2,8,1536]{3,2,1,0:T(8,128)(2,1)S(1)}, u32[]{:S(2)}, u32[]{:S(2)}) async-start(bf16[64,2,8,1536]{3,2,1,0:T(8,128)(2,1)} %bitcast.75), calls=%async_computation | async-start | bytes 6291456 | tf_op jit(solution)/shard_map/all_to_all | solution.py:309
  137.1 0.7 iota_compare_fusion.3
  137.8 0.6 and_select_fusion
  138.4 0.2 convert_reduce_fusion.1
  138.6 1.3 fusion.26
  139.9 0.0 slice-start
  139.9 2.3 %slice-done = bf16[1536,1536]{1,0:T(8,128)(2,1)S(1)} async-done(((bf16[1536,3072]{1,0:T(8,128)(2,1)}), bf16[1536,1536]{1,0:T(8,128)(2,1)S(1)}, s32[]{:S(2)}) %slice-start) | async-done | bytes 4718616 | tf_op jit(solution)/shard_map/slice | solution.py:267
  142.2 2.5 %copy.26 = bf16[3,64,8,1536]{3,2,1,0:T(8,128)(2,1)} copy(bf16[3,64,8,1536]{3,2,0,1:T(8,128)(2,1)S(1)} %bitcast.73) | data formatting | bytes 9437184 | tf_op jit(solution)/shard_map/transpose | solution.py:24
  144.7 28.3 %shard_map.69 = f32[2,24,768]{2,1,0:T(8,128)} custom-call(f32[4,2,24,768]{3,2,1,0:T(8,128)} %shard_map.68.ztot), custom_call_target="tpu_custom_call" | custom-call | tf_op jit(solution)/shard_map/pallas_call | solution.py:222
  173.1 0.9 multiply_bitcast_fusion
  174.0 0.7 copy.28
  174.7 36.2 %all-to-all-done = bf16[64,2,8,1536]{3,2,1,0:T(8,128)(2,1)S(1)} async-done(((bf16[64,2,8,1536]{3,2,1,0:T(8,128)(2,1)}), bf16[64,2,8,1536]{3,2,1,0:T(8,128)(2,1)S(1)}, u32[]{:S(2)}, u32[]{:S(2)}) %all-to-all-start) | async-done | bytes 3145760 | tf_op jit(solution)/shard_map/all_to_all | solution.py:309
  210.9 2.4 %gather_fusion.1 = bf16[128,8,1536]{2,1,0:T(8,128)(2,1)} fusion(bf16[128,8,1536]{2,1,0:T(8,128)(2,1)S(1)} %bitcast.74, s32[1024]{0:T(1024)S(1)} %pad_clamp_fusion), kind=kCustom, calls=%fused_computation.1 | custom fusion | bytes 6291968 | tf_op jit(solution)/shard_map/jit(_take)/gather | solution.py:316
  213.3 7.9 %fusion.2 = f32[1024,1536]{1,0:T(8,128)S(1)} fusion(bf16[1536,1536]{1,0:T(8,128)(2,1)} %bitcast.78, bf16[128,8,1536]{2,1,0:T(8,128)(2,1)} %gather_fusion.1, pred[128]{0:T(512)(128)(4,1)S(1)} %iota_compare_fusion.3), kind=kOutput, calls=%fused_computation.4 | convolution fusion | flops 4833411072 | bytes 14155904 | tf_op jit(solution)/shard_map/dot_general | solution.py:25
  221.2 0.2 slice.39
  221.5 0.1 slice.50
  221.6 0.6 fusion.12
  222.2 0.3 pad_maximum_fusion
  222.5 2.1 convert_element_type.52
  (6 shorter events, 0.0 us)
Async XLA Ops:
  7.2 3.4 %copy-start.3 = (s32[1,64]{1,0:T(1,128)S(1)}, s32[1,64]{1,0:T(1,128)}, u32[]{:S(2)}) copy-start(s32[1,64]{1,0:T(1,128)} %param.9) | copy-start | bytes 772
  7.2 108.9 %all-gather.2.cloned.1.call-start = ((), (), s32[]{:S(2)}) async-start(), calls=%async_computation.1 | async-start | bytes 9584640 | tf_op jit(solution)/shard_map/all_gather | solution.py:256
  10.9 3.8 %copy-start.1 = (bf16[1,512,1536]{2,1,0:T(8,128)(2,1)S(1)}, bf16[1,512,1536]{2,1,0:T(8,128)(2,1)}, u32[]{:S(2)}) copy-start(bf16[1,512,1536]{2,1,0:T(8,128)(2,1)} %param.6) | copy-start | bytes 4718596
  21.9 94.2 %copy-start = (bf16[1,512,1536]{2,1,0:T(8,128)(2,1)S(1)}, bf16[1,512,1536]{2,1,0:T(8,128)(2,1)}, u32[]{:S(2)}) copy-start(bf16[1,512,1536]{2,1,0:T(8,128)(2,1)} %param.5) | copy-start | bytes 4718596
  21.9 94.2 %copy-start.2 = (bf16[1,512,1536]{2,1,0:T(8,128)(2,1)S(1)}, bf16[1,512,1536]{2,1,0:T(8,128)(2,1)}, u32[]{:S(2)}) copy-start(bf16[1,512,1536]{2,1,0:T(8,128)(2,1)} %param.6) | copy-start | bytes 4718596
  130.7 80.2 %all-to-all-start = ((bf16[64,2,8,1536]{3,2,1,0:T(8,128)(2,1)}), bf16[64,2,8,1536]{3,2,1,0:T(8,128)(2,1)S(1)}, u32[]{:S(2)}, u32[]{:S(2)}) async-start(bf16[64,2,8,1536]{3,2,1,0:T(8,128)(2,1)} %bitcast.75), calls=%async_computation | async-start | bytes 6291456 | tf_op jit(solution)/shard_map/all_to_all | solution.py:309
  139.9 2.3 %slice-start = ((bf16[1536,3072]{1,0:T(8,128)(2,1)}), bf16[1536,1536]{1,0:T(8,128)(2,1)S(1)}, s32[]{:S(2)}) async-start(bf16[1536,3072]{1,0:T(8,128)(2,1)} %all-gather.2.cloned.1.call-done), calls=%async_computation.2 | async-start | bytes 9437184 | tf_op jit(solution)/shard_map/slice | solution.py:267
Sparse Core Ops, SparseCore 0:
  11.3 98.0 all-gather.1

commit v14 on v13

--- a/solution.py
+++ b/solution.py
@@ -271,10 +271,14 @@
         (((1,), (1,)), ((), ())),
         preferred_element_type=jnp.float32,
     )
+    sum_back, sum_cross = lax.reduce(
+        (proj_back, proj_back * normed),
+        (jnp.float32(0), jnp.float32(0)),
+        lambda a, b: (a[0] + b[0], a[1] + b[1]),
+        (1,),
+    )
     input_grad = cotangent.astype(jnp.float32) + inverse * (
-        proj_back
-        - jnp.mean(proj_back, axis=-1, keepdims=True)
-        - normed * jnp.mean(proj_back * normed, axis=-1, keepdims=True)
+        proj_back - (sum_back / D)[:, None] - normed * (sum_cross / D)[:, None]
     )
     input_grad = input_grad.astype(jnp.bfloat16)
     counts = seg_counts[0]

time: 232 us -> 232 us (level)
  local copies, waits for them, and re-layouts: 14.6 us -> 21.5 us
  other arithmetic: 16.7 us -> 11.8 us
  transfers between devices with their start and end apart: 2 -> 2, of which waited for: 1 -> 1; matrix products, arithmetic and copies ran while one was open for 9% -> 8% of each run, Pallas kernels for 52% -> 52%
where the time goes in v14:
time: 232 us; the launch traced here: 231 us
  Pallas kernels  121 us (52%)
  waiting for transfers between devices  35.8 us (15%)
  local copies, waits for them, and re-layouts  21.5 us (9%)
  matrix products  19.8 us (9%)
  between operations  14.2 us (6%)
  other arithmetic  11.8 us (5%)
  starting transfers between devices  6.73 us (3%)
    pallas_call x1, Pallas kernels, z_sum(): pl.pallas_call(functools.partial(z_sum_kernel, n_z, n_y), out_shape=jax.S...  92.7 us
    all_to_all x1, waiting for transfers between devices, body(): lax.all_to_all(send_rows.reshape(group_size, capacity, SEG, D), 'fsdp', s...  35.8 us
    pallas_call x1, Pallas kernels, y_site_sum(): pl.pallas_call(functools.partial(y_site_kernel, n_y, n_site), out_shape=j...  28.6 us
    dot_general x1, matrix products, stem_taps(): lax.dot_general(frames, weights, (((1,), (1,)), ((), ())), preferred_elem...  7.95 us
    dot_general x2, matrix products, body(): jnp.einsum('rckj,rd->kcjd', by_core, cotangent[:, part * (D // 2):(part +...  7.31 us
    all_to_all x1, starting transfers between devices, body(): lax.all_to_all(send_rows.reshape(group_size, capacity, SEG, D), 'fsdp', s...  6.7 us
  transfers between devices with their start and end apart: 2, of which 1 were waited for; matrix products, arithmetic and copies ran while one was open for 8% of the time, Pallas kernels for 52%

profile of v14, /device:TPU:24, one launch (start us, length us, event | category | flops | bytes accessed | tf_op | source)
XLA Modules:
  0.0 231.2 jit_solution(15998940484099988236)
XLA Ops:
  7.2 0.0 copy-start
  7.2 0.0 copy-start.4
  7.2 0.0 all-gather.2.cloned.1.call-start
  7.2 1.7 pad_maximum_fusion.1
  8.9 0.0 all-gather.2.cloned.1.call-update
  9.0 0.0 copy-start.2
  9.0 3.2 %copy.22 = f32[1,512,1536]{1,2,0:T(8,128)} copy(bf16[1,512,1536]{2,1,0:T(8,128)(2,1)} %param.5) | data formatting | bytes 4718592 | tf_op jit(solution)/shard_map/convert_element_type | solution.py:245
  12.1 0.0 copy-done.4
  12.1 0.1 copy.25
  12.2 0.1 reduce-window.8
  12.3 0.1 reduce.17
  12.4 0.0 copy-done
  12.4 0.0 copy-start.1
  12.5 0.3 convert_reduce_fusion
  12.8 0.5 multiply_reduce_fusion.1
  13.3 0.0 copy-done.2
  13.3 1.0 copy-done.1
  14.3 3.6 %convolution_bitcast_fusion.hi_ref = f32[2,32,24,768]{3,2,1,0:T(8,128)} fusion(bf16[512,1536]{1,0:T(8,128)(2,1)S(1)} %bitcast.60, f32[512,32,2,24]{0,3,2,1:T(8,128)S(1)} %bitcast.56, f32[512]{0:T(512)S(1)} %add_rsqrt_fusion, f32[512]{0:T(512)S(1)} %broadcast_multiply_fusion.2), kind=kOutput, calls=%fused_computation.16 | convolution fusion | flops 1210318848 | bytes 8654848 | tf_op jit(solution)/shard_map/rckj,rd->kcjd/dot_general | solution.py:260
  17.9 3.7 %convolution_bitcast_fusion.1.lo_ref = f32[2,32,24,768]{3,2,1,0:T(8,128)} fusion(bf16[512,1536]{1,0:T(8,128)(2,1)S(1)} %bitcast.61, f32[512,32,2,24]{0,3,2,1:T(8,128)S(1)} %bitcast.57, f32[512]{0:T(512)S(1)} %add_rsqrt_fusion, f32[512]{0:T(512)S(1)} %broadcast_multiply_fusion.2), kind=kOutput, calls=%fused_computation.17 | convolution fusion | flops 1210318848 | bytes 8654848 | tf_op jit(solution)/shard_map/rckj,rd->kcjd/dot_general | solution.py:260
  21.7 92.7 %shard_map.68.ztot = f32[4,2,24,768]{3,2,1,0:T(8,128)} custom-call(f32[2,32,24,768]{3,2,1,0:T(8,128)} %convolution_bitcast_fusion.1.lo_ref, f32[2,32,24,768]{3,2,1,0:T(8,128)} %convolution_bitcast_fusion.hi_ref), custom_call_target="tpu_custom_call" | custom-call | tf_op jit(solution)/shard_map/pallas_call | solution.py:200
  114.4 0.7 fusion.22
  115.0 0.2 convert_reduce_fusion.3
  115.2 0.2 convert_reduce_fusion.2
  115.4 0.1 select_reduce_fusion
  115.5 0.0 all-gather.2.cloned.1.call-done
  115.5 4.5 %fusion.2 = f32[512,1536]{1,0:T(8,128)S(1)} fusion(bf16[1536,3072]{1,0:T(8,128)(2,1)} %all-gather.2.cloned.1.call-done, bf16[1,512,1536]{2,1,0:T(8,128)(2,1)S(1)} %copy-done.2), kind=kOutput, calls=%fused_computation.5 | convolution fusion | flops 2415919104 | bytes 9437184 | tf_op jit(solution)/shard_map/dot_general | solution.py:268
  120.1 0.0 copy-start.3
  120.1 0.8 multiply_reduce_fusion
  120.9 0.6 copy-done.3
  121.5 1.1 fusion.11
  122.6 2.4 %gather_fusion = bf16[128,8,1536]{2,1,0:T(8,128)(2,1)} fusion(bf16[64,8,1536]{2,1,0:T(8,128)(2,1)S(1)} %fusion.11, s32[1024]{0:T(1024)S(1)} %pad_clamp_fusion.1), kind=kCustom, calls=%fused_computation | custom fusion | bytes 6291968 | tf_op jit(solution)/shard_map/jit(_take)/gather | solution.py:312
  125.0 6.7 %all-to-all-start = ((bf16[64,2,8,1536]{3,2,1,0:T(8,128)(2,1)}), bf16[64,2,8,1536]{3,2,1,0:T(8,128)(2,1)}, u32[]{:S(2)}, u32[]{:S(2)}) async-start(bf16[64,2,8,1536]{3,2,1,0:T(8,128)(2,1)} %bitcast.59), calls=%async_computation | async-start | bytes 6291456 | tf_op jit(solution)/shard_map/all_to_all | solution.py:313
  131.7 0.7 iota_compare_fusion.3
  132.4 0.7 and_select_fusion
  133.0 0.2 convert_reduce_fusion.1
  133.2 1.3 fusion.24
  134.6 0.0 slice-start
  134.6 2.3 %slice-done = bf16[1536,1536]{1,0:T(8,128)(2,1)S(1)} async-done(((bf16[1536,3072]{1,0:T(8,128)(2,1)}), bf16[1536,1536]{1,0:T(8,128)(2,1)S(1)}, s32[]{:S(2)}) %slice-start) | async-done | bytes 4718616 | tf_op jit(solution)/shard_map/slice | solution.py:267
  136.9 2.5 %copy.26 = bf16[3,64,8,1536]{3,2,1,0:T(8,128)(2,1)} copy(bf16[3,64,8,1536]{3,2,0,1:T(8,128)(2,1)S(1)} %bitcast.58) | data formatting | bytes 9437184 | tf_op jit(solution)/shard_map/transpose | solution.py:24
  139.4 28.6 %shard_map.69 = f32[2,24,768]{2,1,0:T(8,128)} custom-call(f32[4,2,24,768]{3,2,1,0:T(8,128)} %shard_map.68.ztot), custom_call_target="tpu_custom_call" | custom-call | tf_op jit(solution)/shard_map/pallas_call | solution.py:222
  168.0 0.9 multiply_bitcast_fusion
  169.0 0.7 copy.28
  169.6 35.8 %all-to-all-done = bf16[64,2,8,1536]{3,2,1,0:T(8,128)(2,1)} async-done(((bf16[64,2,8,1536]{3,2,1,0:T(8,128)(2,1)}), bf16[64,2,8,1536]{3,2,1,0:T(8,128)(2,1)}, u32[]{:S(2)}, u32[]{:S(2)}) %all-to-all-start) | async-done | bytes 3145760 | tf_op jit(solution)/shard_map/all_to_all | solution.py:313
  205.4 4.3 %gather_fusion.1 = bf16[128,8,1536]{2,1,0:T(8,128)(2,1)} fusion(bf16[128,8,1536]{2,1,0:T(8,128)(2,1)} %bitcast.13, s32[1024]{0:T(1024)S(1)} %pad_clamp_fusion), kind=kCustom, calls=%fused_computation.1 | custom fusion | bytes 6291968 | tf_op jit(solution)/shard_map/jit(_take)/gather | solution.py:320
  209.7 8.0 %fusion.5 = f32[1024,1536]{1,0:T(8,128)S(1)} fusion(bf16[1536,1536]{1,0:T(8,128)(2,1)} %bitcast.62, bf16[128,8,1536]{2,1,0:T(8,128)(2,1)} %gather_fusion.1, pred[128]{0:T(512)(128)(4,1)S(1)} %iota_compare_fusion.3), kind=kOutput, calls=%fused_computation.6 | convolution fusion | flops 4833411072 | bytes 14155904 | tf_op jit(solution)/shard_map/dot_general | solution.py:25
  217.7 0.2 slice.39
  217.9 0.1 slice.52
  218.1 0.6 fusion.10
  218.6 1.6 pad_maximum_fusion
  220.3 4.1 %convert_element_type.52 = bf16[1,2048,512]{2,1,0:T(8,128)(2,1)} reshape(bf16[1024,1024]{1,0:T(8,128)(2,1)} %pad_maximum_fusion) | data formatting | bytes 4194304 | tf_op jit(solution)/shard_map/convert_element_type | solution.py:329
  (6 shorter events, 0.0 us)
Async XLA Ops:
  7.2 5.3 %copy-start = (bf16[1,512,1536]{2,1,0:T(8,128)(2,1)S(1)}, bf16[1,512,1536]{2,1,0:T(8,128)(2,1)}, u32[]{:S(2)}) copy-start(bf16[1,512,1536]{2,1,0:T(8,128)(2,1)} %param.5) | copy-start | bytes 4718596
  7.2 5.0 %copy-start.4 = (s32[1,64]{1,0:T(1,128)S(1)}, s32[1,64]{1,0:T(1,128)}, u32[]{:S(2)}) copy-start(s32[1,64]{1,0:T(1,128)} %param.9) | copy-start | bytes 772
  7.2 108.3 %all-gather.2.cloned.1.call-start = ((), (), s32[]{:S(2)}) async-start(), calls=%async_computation.1 | async-start | bytes 9584640 | tf_op jit(solution)/shard_map/all_gather | solution.py:256
  9.0 4.4 %copy-start.2 = (bf16[1,512,1536]{2,1,0:T(8,128)(2,1)S(1)}, bf16[1,512,1536]{2,1,0:T(8,128)(2,1)}, u32[]{:S(2)}) copy-start(bf16[1,512,1536]{2,1,0:T(8,128)(2,1)} %param.6) | copy-start | bytes 4718596
  12.4 1.9 copy-start.1
  120.1 1.4 copy-start.3
  125.0 80.4 %all-to-all-start = ((bf16[64,2,8,1536]{3,2,1,0:T(8,128)(2,1)}), bf16[64,2,8,1536]{3,2,1,0:T(8,128)(2,1)}, u32[]{:S(2)}, u32[]{:S(2)}) async-start(bf16[64,2,8,1536]{3,2,1,0:T(8,128)(2,1)} %bitcast.59), calls=%async_computation | async-start | bytes 6291456 | tf_op jit(solution)/shard_map/all_to_all | solution.py:313
  134.6 2.3 %slice-start = ((bf16[1536,3072]{1,0:T(8,128)(2,1)}), bf16[1536,1536]{1,0:T(8,128)(2,1)S(1)}, s32[]{:S(2)}) async-start(bf16[1536,3072]{1,0:T(8,128)(2,1)} %all-gather.2.cloned.1.call-done), calls=%async_computation.2 | async-start | bytes 9437184 | tf_op jit(solution)/shard_map/slice | solution.py:267
Sparse Core Ops, SparseCore 0:
  11.3 97.5 all-gather.1

commit v15 on v13

--- a/solution.py
+++ b/solution.py
@@ -255,9 +255,9 @@
     joined = jnp.concatenate([proj_weight, stem_weight.reshape(taps_n * chans, D)], 1)
     gathered = lax.all_gather(joined, "fsdp", axis=0, tiled=True)
     rows_out = D // group_size
-    by_core = normed_bf.reshape(normed_bf.shape[0], group_size // 2, 2, rows_out)
+    by_core = normed_bf.T.reshape(group_size // 2, 2, rows_out, normed_bf.shape[0])
     halves = [
-        jnp.einsum("rckj,rd->kcjd", by_core, cotangent[:, part * (D // 2):(part + 1) * (D // 2)],
+        jnp.einsum("ckjr,rd->kcjd", by_core, cotangent[:, part * (D // 2):(part + 1) * (D // 2)],
                    preferred_element_type=jnp.float32)
         for part in range(2)
     ]

time: 232 us -> 241 us (1.039)
  local copies, waits for them, and re-layouts: 14.6 us -> 18.5 us
  other arithmetic: 16.7 us -> 19.7 us
  transfers between devices with their start and end apart: 2 -> 2, of which waited for: 1 -> 1; matrix products, arithmetic and copies ran while one was open for 9% -> 10% of each run, Pallas kernels for 52% -> 50%
where the time goes in v15:
time: 241 us; the launch traced here: 240 us
  Pallas kernels  120 us (50%)
  waiting for transfers between devices  35.1 us (15%)
  matrix products  23 us (10%)
  other arithmetic  19.7 us (8%)
  local copies, waits for them, and re-layouts  18.5 us (8%)
  between operations  14.2 us (6%)
  starting transfers between devices  8.67 us (4%)
    pallas_call x1, Pallas kernels, z_sum(): pl.pallas_call(functools.partial(z_sum_kernel, n_z, n_y), out_shape=jax.S...  91 us
    all_to_all x1, waiting for transfers between devices, body(): lax.all_to_all(send_rows.reshape(group_size, capacity, SEG, D), 'fsdp', s...  35.1 us
    pallas_call x1, Pallas kernels, y_site_sum(): pl.pallas_call(functools.partial(y_site_kernel, n_y, n_site), out_shape=j...  29.3 us
    all_to_all x1, starting transfers between devices, body(): lax.all_to_all(send_rows.reshape(group_size, capacity, SEG, D), 'fsdp', s...  8.63 us
    dot_general x2, matrix products, body(): jnp.einsum('ckjr,rd->kcjd', by_core, cotangent[:, part * (D // 2):(part +...  8.45 us
    dot_general x1, matrix products, stem_taps(): lax.dot_general(frames, weights, (((1,), (1,)), ((), ())), preferred_elem...  7.93 us
    dot_general x1, matrix products, body(): lax.dot_general(cotangent, full_weight, (((1,), (1,)), ((), ())), preferr...  6.62 us
  transfers between devices with their start and end apart: 2, of which 1 were waited for; matrix products, arithmetic and copies ran while one was open for 10% of the time, Pallas kernels for 50%

profile of v15, /device:TPU:24, one launch (start us, length us, event | category | flops | bytes accessed | tf_op | source)
XLA Modules:
  0.0 239.5 jit_solution(7566008492962455790)
XLA Ops:
  7.2 0.0 copy-start
  7.2 0.0 all-gather.2.cloned.1.call-start
  7.2 1.7 pad_maximum_fusion.1
  8.9 0.0 all-gather.2.cloned.1.call-update
  9.0 1.7 convert_reduce_fusion
  10.7 2.0 fusion.13
  12.6 0.0 copy-done
  12.6 0.0 copy-start.3
  12.6 1.6 fusion.20
  14.2 1.7 copy.23
  15.9 0.0 copy-done.3
  15.9 0.1 copy.26
  16.0 0.1 reduce-window.8
  16.1 0.1 reduce.2
  16.2 0.0 copy-start.1
  16.3 4.8 %convolution_bitcast_fusion.hi_ref = f32[2,32,24,768]{3,2,1,0:T(8,128)} fusion(bf16[32,2,24,512]{3,2,1,0:T(8,128)(2,1)S(1)} %bitcast.84, bf16[512,1536]{1,0:T(8,128)(2,1)} %bitcast.87), kind=kOutput, calls=%fused_computation.23 | convolution fusion | flops 1207959552 | bytes 7077888 | tf_op jit(solution)/shard_map/ckjr,rd->kcjd/dot_general | solution.py:260
  21.1 0.0 copy-done.1
  21.1 3.6 %convolution_bitcast_fusion.1.lo_ref = f32[2,32,24,768]{3,2,1,0:T(8,128)} fusion(bf16[32,2,24,512]{3,2,1,0:T(8,128)(2,1)S(1)} %bitcast.85, bf16[512,1536]{1,0:T(8,128)(2,1)S(1)} %bitcast.88), kind=kOutput, calls=%fused_computation.24 | convolution fusion | flops 1207959552 | bytes 7077888 | tf_op jit(solution)/shard_map/ckjr,rd->kcjd/dot_general | solution.py:260
  24.7 0.0 copy-start.2
  24.7 91.0 %shard_map.68.ztot = f32[4,2,24,768]{3,2,1,0:T(8,128)} custom-call(f32[2,32,24,768]{3,2,1,0:T(8,128)} %convolution_bitcast_fusion.1.lo_ref, f32[2,32,24,768]{3,2,1,0:T(8,128)} %convolution_bitcast_fusion.hi_ref), custom_call_target="tpu_custom_call" | custom-call | tf_op jit(solution)/shard_map/pallas_call | solution.py:200
  115.7 0.7 fusion.31
  116.3 0.2 convert_reduce_fusion.3
  116.5 0.2 convert_reduce_fusion.2
  116.7 0.1 select_reduce_fusion
  116.8 0.0 all-gather.2.cloned.1.call-done
  116.8 0.0 copy-done.2
  116.9 6.6 %fusion.8 = (f32[512]{0:T(512)S(1)}, f32[1536,512]{0,1:T(8,128)}) fusion(bf16[1,512,1536]{2,1,0:T(8,128)(2,1)S(1)} %copy-done, f32[512]{0:T(512)S(1)} %add_rsqrt_fusion, f32[512]{0:T(512)S(1)} %broadcast_multiply_fusion.2, bf16[1,512,1536]{2,1,0:T(8,128)(2,1)S(1)} %copy-done.2, bf16[1536,3072]{1,0:T(8,128)(2,1)} %all-gather.2.cloned.1.call-done), kind=kOutput, calls=%fused_computation.12 | convolution fusion | flops 2419850752 | bytes 11016192 | tf_op jit(solution)/shard_map/dot_general | solution.py:268
  123.5 2.1 reduce_sum.95
  125.6 3.4 %fusion.19 = bf16[64,8,1536]{2,1,0:T(8,128)(2,1)S(1)} fusion(bf16[1,512,1536]{2,1,0:T(8,128)(2,1)S(1)} %copy-done, f32[1536,512]{0,1:T(8,128)} %get-tuple-element.9, f32[512]{0:T(512)S(1)} %get-tuple-element.10, f32[512]{0:T(512)S(1)} %get-tuple-element.11, f32[512]{0:T(512)S(1)} %add_rsqrt_fusion, f32[512]{0:T(512)S(1)} %broadcast_multiply_fusion.2, ...), kind=kLoop, calls=%fused_computation.29 | loop fusion | flops 7864320 | bytes 7872512 | tf_op jit(solution)/shard_map/reshape | solution.py:306
  129.1 2.4 %gather_fusion = bf16[128,8,1536]{2,1,0:T(8,128)(2,1)} fusion(bf16[64,8,1536]{2,1,0:T(8,128)(2,1)S(1)} %fusion.19, s32[1024]{0:T(1024)S(1)} %pad_clamp_fusion.1), kind=kCustom, calls=%fused_computation | custom fusion | bytes 6291968 | tf_op jit(solution)/shard_map/jit(_take)/gather | solution.py:308
  131.5 8.6 %all-to-all-start = ((bf16[64,2,8,1536]{3,2,1,0:T(8,128)(2,1)}), bf16[64,2,8,1536]{3,2,1,0:T(8,128)(2,1)}, u32[]{:S(2)}, u32[]{:S(2)}) async-start(bf16[64,2,8,1536]{3,2,1,0:T(8,128)(2,1)} %bitcast.86), calls=%async_computation | async-start | bytes 6291456 | tf_op jit(solution)/shard_map/all_to_all | solution.py:309
  140.1 0.7 iota_compare_fusion.3
  140.8 0.7 and_select_fusion
  141.4 0.2 convert_reduce_fusion.1
  141.6 1.3 fusion.33
  142.9 0.0 slice-start
  142.9 2.3 slice-done
  145.3 2.5 %copy.27 = bf16[3,64,8,1536]{3,2,1,0:T(8,128)(2,1)} copy(bf16[3,64,8,1536]{3,2,0,1:T(8,128)(2,1)S(1)} %bitcast.83) | data formatting | bytes 9437184 | tf_op jit(solution)/shard_map/transpose | solution.py:24
  147.8 29.3 %shard_map.69 = f32[2,24,768]{2,1,0:T(8,128)} custom-call(f32[4,2,24,768]{3,2,1,0:T(8,128)} %shard_map.68.ztot), custom_call_target="tpu_custom_call" | custom-call | tf_op jit(solution)/shard_map/pallas_call | solution.py:222
  177.1 0.9 multiply_bitcast_fusion
  178.0 0.7 copy.29
  178.7 35.1 %all-to-all-done = bf16[64,2,8,1536]{3,2,1,0:T(8,128)(2,1)} async-done(((bf16[64,2,8,1536]{3,2,1,0:T(8,128)(2,1)}), bf16[64,2,8,1536]{3,2,1,0:T(8,128)(2,1)}, u32[]{:S(2)}, u32[]{:S(2)}) %all-to-all-start) | async-done | bytes 3145760 | tf_op jit(solution)/shard_map/all_to_all | solution.py:309
  213.8 4.3 %gather_fusion.1 = bf16[128,8,1536]{2,1,0:T(8,128)(2,1)} fusion(bf16[128,8,1536]{2,1,0:T(8,128)(2,1)} %bitcast.14, s32[1024]{0:T(1024)S(1)} %pad_clamp_fusion), kind=kCustom, calls=%fused_computation.1 | custom fusion | bytes 6291968 | tf_op jit(solution)/shard_map/jit(_take)/gather | solution.py:316
  218.1 7.9 %fusion.14 = f32[1024,1536]{1,0:T(8,128)S(1)} fusion(bf16[1536,1536]{1,0:T(8,128)(2,1)} %bitcast.89, bf16[128,8,1536]{2,1,0:T(8,128)(2,1)} %gather_fusion.1, pred[128]{0:T(512)(128)(4,1)S(1)} %iota_compare_fusion.3), kind=kOutput, calls=%fused_computation.18 | convolution fusion | flops 4833411072 | bytes 14155904 | tf_op jit(solution)/shard_map/dot_general | solution.py:25
  226.0 0.2 slice.39
  226.3 0.1 slice.50
  226.4 0.6 fusion.18
  227.0 1.6 pad_maximum_fusion
  228.6 4.1 %convert_element_type.43 = bf16[1,2048,512]{2,1,0:T(8,128)(2,1)} reshape(bf16[1024,1024]{1,0:T(8,128)(2,1)} %pad_maximum_fusion) | data formatting | bytes 4194304 | tf_op jit(solution)/shard_map/convert_element_type | solution.py:325
  (6 shorter events, 0.0 us)
Async XLA Ops:
  7.2 5.5 %copy-start = (bf16[1,512,1536]{2,1,0:T(8,128)(2,1)S(1)}, bf16[1,512,1536]{2,1,0:T(8,128)(2,1)}, u32[]{:S(2)}) copy-start(bf16[1,512,1536]{2,1,0:T(8,128)(2,1)} %param.5) | copy-start | bytes 4718596
  7.2 109.7 %all-gather.2.cloned.1.call-start = ((), (), s32[]{:S(2)}) async-start(), calls=%async_computation.1 | async-start | bytes 9584640 | tf_op jit(solution)/shard_map/all_gather | solution.py:256
  12.6 3.3 %copy-start.3 = (s32[1,64]{1,0:T(1,128)S(1)}, s32[1,64]{1,0:T(1,128)}, u32[]{:S(2)}) copy-start(s32[1,64]{1,0:T(1,128)} %param.9) | copy-start | bytes 772
  16.2 4.8 %copy-start.1 = (bf16[1,512,1536]{2,1,0:T(8,128)(2,1)S(1)}, bf16[1,512,1536]{2,1,0:T(8,128)(2,1)}, u32[]{:S(2)}) copy-start(bf16[1,512,1536]{2,1,0:T(8,128)(2,1)} %param.6) | copy-start | bytes 4718596
  24.7 92.1 %copy-start.2 = (bf16[1,512,1536]{2,1,0:T(8,128)(2,1)S(1)}, bf16[1,512,1536]{2,1,0:T(8,128)(2,1)}, u32[]{:S(2)}) copy-start(bf16[1,512,1536]{2,1,0:T(8,128)(2,1)} %param.6) | copy-start | bytes 4718596
  131.5 82.3 %all-to-all-start = ((bf16[64,2,8,1536]{3,2,1,0:T(8,128)(2,1)}), bf16[64,2,8,1536]{3,2,1,0:T(8,128)(2,1)}, u32[]{:S(2)}, u32[]{:S(2)}) async-start(bf16[64,2,8,1536]{3,2,1,0:T(8,128)(2,1)} %bitcast.86), calls=%async_computation | async-start | bytes 6291456 | tf_op jit(solution)/shard_map/all_to_all | solution.py:309
  142.9 2.3 slice-start
Sparse Core Ops, SparseCore 0:
  11.3 98.2 all-gather.1
